TPU v7x, 32 devices: a whole 2x2x4 slice. The times are simulated.
32 devices in a mesh: fsdp: 8 (over y, x, core), seq: 4 (over z).
Axes of the slice: x: 2, y: 2, z: 4, core: 2. Of those that a mesh axis runs over, the one named last changes fastest.
Arguments:
- layer_input: bfloat16 [3, 8, 1024, 1472], P(None, 'fsdp', 'seq'), may hold values from -6 to 6
- segment_ids: int32 [3, 8, 1024], P(None, 'fsdp', 'seq'), may hold values from 0 to 15, never falling along the last dimension, each value on 1 to 768 neighbouring positions
- grad_out: bfloat16 [3, 8, 1024, 1472], P(None, 'fsdp', 'seq'), may hold values from -6 to 6
- grad_gate: float32 [3, 8, 1024], P(None, 'fsdp', 'seq'), may hold values from -0.625 to 0.625
- attn_gain: float32 [1472], P('fsdp'), may hold values from 0.5 to 2
- w_query: float32 [1472, 384], P('fsdp', 'seq'), may hold values from -0.01953125 to 0.01953125
- w_key: float32 [1472, 384], P('fsdp', 'seq'), may hold values from -0.15625 to 0.15625
- w_value: float32 [1472, 384], P('fsdp', 'seq'), may hold values from -0.15625 to 0.15625
- w_out: float32 [384, 1472], P('seq', 'fsdp'), may hold values from -1.25 to 1.25
- rel_table: float32 [32, 6], replicated, may hold values from -4 to 4
- ffn_gain: float32 [1472], P('fsdp'), may hold values from 0.5 to 2
- w_gate: float32 [1472, 3584], P('fsdp', 'seq'), may hold values from -0.15625 to 0.15625
- w_up: float32 [1472, 3584], P('fsdp', 'seq'), may hold values from -0.15625 to 0.15625
- w_down: float32 [3584, 1472], P('seq', 'fsdp'), may hold values from -0.1875 to 0.1875
- delete_gain: float32 [1472], P('fsdp'), may hold values from 0.5 to 2
- w_delete: float32 [1472], P('fsdp'), may hold values from -0.15625 to 0.15625
Outputs:
- activations: bfloat16 [3, 8, 1024, 1472], P(None, 'fsdp', 'seq')
- gate_mask: float32 [3, 8, 1024], P(None, 'fsdp', 'seq')
- grad_input: bfloat16 [3, 8, 1024, 1472], P(None, 'fsdp', 'seq')
- grad_attn_gain: float32 [1472], P('fsdp')
- grad_w_query: float32 [1472, 384], P('fsdp', 'seq')
- grad_w_key: float32 [1472, 384], P('fsdp', 'seq')
- grad_w_value: float32 [1472, 384], P('fsdp', 'seq')
- grad_w_out: float32 [384, 1472], P('seq', 'fsdp')
- grad_rel_table: float32 [32, 6], replicated
- grad_ffn_gain: float32 [1472], P('fsdp')
- grad_w_gate: float32 [1472, 3584], P('fsdp', 'seq')
- grad_w_up: float32 [1472, 3584], P('fsdp', 'seq')
- grad_w_down: float32 [3584, 1472], P('seq', 'fsdp')
- grad_delete_gain: float32 [1472], P('fsdp')
- grad_w_delete: float32 [1472], P('fsdp')
Inputs may be any that keep to these rules, and one draw needn't show every extreme that they name: `segment_ids`: in each sequence the segment ids never fall; each document holds 1 to 768 tokens and one holds exactly that many.
All inputs are finite; a program needn't handle non-finite values.
Results may differ from a plain program's by a relative error of at most 0.02.
The roundings to bfloat16 on the way count: a program that leaves them out, or rounds other values in their place, can miss the bound.
Values may be sent and summed in bfloat16 or wider, within the bound.
No kernel may reach another device: no remote copies, remote signals or barrier semaphores. Data moves between devices by JAX's collectives and lax.ppermute only.
A program may use at most 320 MiB of HBM per device.

v0:
```python
import functools

import jax
import jax.numpy as jnp
from jax import lax
from jax.experimental import pallas as pl
from jax.experimental.pallas import tpu as pltpu
from jax.sharding import PartitionSpec as P

EPSILON = 1e-06
THRESHOLDS = (12, 16, 23, 32, 46, 64, 91)
MASKED_SCORE = -1e30
DELETE_SCALE = -30.0
BF = jnp.bfloat16
F32 = jnp.float32
LANES = 128
NT = (((1,), (1,)), ((), ()))
TN = (((0,), (0,)), ((), ()))


def bucket_of(distance):
    magnitude = jnp.abs(distance)
    passed_count = jnp.zeros_like(distance)
    for threshold in THRESHOLDS:
        passed_count = passed_count + (magnitude >= threshold).astype(jnp.int32)
    near_bucket = jnp.where(magnitude < 8, magnitude, 8 + passed_count)
    return near_bucket + 16 * (distance > 0).astype(jnp.int32)


class Ring:
    def __init__(self, axis, order, groups):
        self.axis = axis
        self.size = len(order)
        onward, back = [], []
        for group in groups:
            for place in range(self.size):
                here = group(order[place])
                there = group(order[(place + 1) % self.size])
                onward.append((here, there))
                back.append((there, here))
        self.onward, self.back = onward, back
        self.order, self.groups = order, groups

    def right(self, value):
        return lax.ppermute(value, self.axis, self.onward)

    def left(self, value):
        return lax.ppermute(value, self.axis, self.back)

    def shift(self, value, offset):
        pairs = [
            (group(self.order[(place + offset) % self.size]), group(self.order[place]))
            for group in self.groups for place in range(self.size)
        ]
        return lax.ppermute(value, self.axis, pairs)


def cut_of(width):
    return width // 2 // LANES * LANES or width // 2


def halve_last(value):
    cut = cut_of(value.shape[-1])
    return value[..., :cut], value[..., cut:]


def halve_first(value):
    cut = value.shape[0] // 2
    return value[:cut], value[cut:]


class Chain:
    def __init__(self, steps):
        self.steps, self.requests = steps, ()
        self.advance(None)

    def run(self):
        while self.requests is not None:
            self.advance([request[0](*request[1:]) for request in self.requests])

    def advance(self, results):
        try:
            self.requests = self.steps.send(results)
        except StopIteration:
            self.requests = None


class Flow:
    def __init__(self):
        self.last = ()

    def slot(self, chains, function=None, *operands):
        chains = [chain for chain in chains if chain.requests is not None]
        held = [[request[1:] for request in chain.requests] for chain in chains]
        operands, held, _ = lax.optimization_barrier((operands, held, self.last))
        results = [
            [request[0](*own) for request, own in zip(chain.requests, owns)]
            for chain, owns in zip(chains, held)
        ]
        for chain, result in zip(chains, results):
            chain.advance(result)
        out = function(*operands) if function is not None else ()
        self.last = (out, results)
        return out

    def finish(self, *chains):
        while any(chain.requests is not None for chain in chains):
            self.slot(chains)


def plus(one, two):
    return one.astype(F32) + two.astype(F32)


def ring_gather(ring, block, halve, finish, found=None):
    found = {} if found is None else found
    found[0] = block
    onward = back = block
    for step in range(1, ring.size // 2):
        onward, back = yield [(ring.right, onward), (ring.left, back)]
        found[-step], found[step] = onward, back
    found[ring.size // 2] = tuple(
        (yield [(ring.right, halve(onward)[0]), (ring.left, halve(back)[1])])
    )
    more = finish(found)
    if more is not None:
        yield from more


def direct_gather(ring, block, finish):
    offsets = [s * k for k in range(1, ring.size // 2) for s in (-1, 1)] + [ring.size // 2]
    results = yield [(functools.partial(ring.shift, offset=k), block) for k in offsets]
    found = dict(zip(offsets, results))
    found[0] = block
    more = finish(found)
    if more is not None:
        yield from more


def exchange(ring, offsets, send_of, finish):
    results = yield [
        (functools.partial(ring.shift, offset=-offset), send_of(offset)) for offset in offsets[1:]
    ]
    found = {offset if 2 * offset == ring.size else -offset: value
             for offset, value in zip(offsets[1:], results)}
    found[0] = send_of(0)
    finish([found[offset] for offset in offsets])


def ring_scatter(ring, blocks, halve, axis, finish):
    far = ring.size // 2
    first, second = halve(blocks[far])
    onward, back = yield [(ring.right, first.astype(BF)), (ring.left, second.astype(BF))]
    whole = False
    for step in range(far - 1, 0, -1):
        to_right, to_left = blocks[step], blocks[-step]
        if whole:
            to_right, to_left = plus(to_right, onward), plus(to_left, back)
        else:
            one, two = halve(to_right)
            to_right = jnp.concatenate([plus(one, onward), two.astype(F32)], axis)
            one, two = halve(to_left)
            to_left = jnp.concatenate([one.astype(F32), plus(two, back)], axis)
            whole = True
        onward, back = yield [(ring.right, to_right.astype(BF)), (ring.left, to_left.astype(BF))]
    if whole:
        total = plus(plus(blocks[0], onward), back)
    else:
        one, two = halve(blocks[0])
        total = jnp.concatenate([plus(one, onward), plus(two, back)], axis)
    more = finish(total)
    if more is not None:
        yield from more


def direct_scatter(ring, blocks, finish):
    offsets = [offset for offset in blocks if offset != 0]
    results = yield [
        (functools.partial(ring.shift, offset=-offset), blocks[offset].astype(BF))
        for offset in offsets
    ]
    total = blocks[0].astype(F32)
    for value in results:
        total = total + value.astype(F32)
    more = finish(total)
    if more is not None:
        yield from more


GELU_SCALE = 0.7978845608028654
GELU_CUBE = 0.044715
VMEM_LIMIT = 56 << 20
ANYWHERE = pl.BlockSpec(memory_space=pl.ANY)
SCALARS = pl.BlockSpec(memory_space=pltpu.SMEM)


def part_rows(index_ref, entry, part):
    return pl.ds(pl.multiple_of(index_ref[entry] * part, 8 if part % 8 == 0 else 1), part)


def chunk_copies(widths, groups, mats, sems, number, slot, mat):
    columns = mats.shape[3]
    first, last = number * columns, (number + 1) * columns
    copies, begin = [], 0
    for entry, (wide, ref) in enumerate(zip(widths, groups)):
        low, high = max(first, begin), min(last, begin + wide)
        if low < high:
            copies.append(
                pltpu.make_async_copy(
                    ref.at[:, pl.ds(mat * wide + low - begin, high - low)],
                    mats.at[slot, mat, :, pl.ds(low - first, high - low)],
                    sems.at[slot, mat, entry],
                )
            )
        begin += wide
    return copies


def stream_chunks(widths, numbers, groups, mats, sems, order):
    chunk, tile = pl.program_id(0), pl.program_id(1)

    def each(position, act):
        for mat in order:
            for copy in chunk_copies(
                widths, groups, mats, sems, numbers[position], position % 2, mat
            ):
                act(copy)

    for position in range(len(numbers)):
        @pl.when((tile == 0) & (chunk == position))
        def _(position=position):
            if position == 0:
                each(0, lambda copy: copy.start())
            if position + 1 < len(numbers):
                each(position + 1, lambda copy: copy.start())
            each(position, lambda copy: copy.wait())

    return lax.rem(chunk, 2)


def ffn_forward_kernel(widths, numbers, kept, mid_ref, in_ref, *refs):
    groups, rest = refs[: len(widths)], refs[len(widths) + kept :]
    to_gate_ref, to_up_ref, act_ref, out_ref, mats, total, sems = rest
    slot = stream_chunks(widths, numbers, groups, mats, sems, (0, 1, 2))
    chunk, tile = pl.program_id(0), pl.program_id(1)
    rows = mid_ref.shape[0]
    span = pl.ds(pl.multiple_of(tile * rows, rows), rows)
    mid = mid_ref[...]
    gate = jnp.dot(mid, mats[slot, 0], preferred_element_type=F32)
    up = jnp.dot(mid, mats[slot, 1], preferred_element_type=F32)
    square = gate * gate
    bend = jnp.tanh(GELU_SCALE * (gate + GELU_CUBE * (square * gate)))
    half = 0.5 * (1.0 + bend)
    gelu = half * gate
    slope = half + (0.5 * GELU_SCALE) * gate * (1.0 - bend * bend) * (
        1.0 + (3.0 * GELU_CUBE) * square
    )
    act = (gelu * up).astype(BF)
    to_gate_ref[...] = slope * up
    to_up_ref[...] = gelu
    act_ref[...] = act
    product = lax.dot_general(act, mats[slot, 2], NT, preferred_element_type=F32)

    @pl.when(chunk == 0)
    def _():
        total[span] = in_ref[...] + product

    @pl.when(chunk > 0)
    def _():
        total[span] = total[span] + product

    @pl.when(chunk == pl.num_programs(0) - 1)
    def _():
        out_ref[...] = total[span]


def ffn_backward_kernel(widths, numbers, kept, grad_ref, to_gate_ref, to_up_ref, *refs):
    groups, rest = refs[: len(widths)], refs[len(widths) + kept :]
    grad_gate_ref, grad_up_ref, out_ref, mats, total, sems = rest
    slot = stream_chunks(widths, numbers, groups, mats, sems, (2, 0, 1))
    chunk, tile = pl.program_id(0), pl.program_id(1)
    rows = grad_ref.shape[0]
    span = pl.ds(pl.multiple_of(tile * rows, rows), rows)
    grad_act = jnp.dot(grad_ref[...], mats[slot, 2], preferred_element_type=F32)
    grad_gate = (grad_act * to_gate_ref[...]).astype(BF)
    grad_up = (grad_act * to_up_ref[...]).astype(BF)
    grad_gate_ref[...] = grad_gate
    grad_up_ref[...] = grad_up
    product = lax.dot_general(grad_gate, mats[slot, 0], NT, preferred_element_type=F32)
    product = product + lax.dot_general(grad_up, mats[slot, 1], NT, preferred_element_type=F32)

    @pl.when(chunk == 0)
    def _():
        total[span] = product

    @pl.when(chunk > 0)
    def _():
        total[span] = total[span] + product

    @pl.when(chunk == pl.num_programs(0) - 1)
    def _():
        out_ref[...] = total[span]


def row_tile(tokens):
    for tile in (384, 256):
        if tokens % tile == 0:
            return tile
    return tokens


def chunk_of(width):
    for columns in (512, 256, LANES):
        if width % columns == 0:
            return columns
    return width


def ffn_call(forward, args, groups, hidden_units, numbers=None, kept=()):
    tokens, width = args[0].shape
    widths = [group.shape[1] // 3 for group in groups]
    columns = chunk_of(hidden_units)
    numbers = list(range(hidden_units // columns)) if numbers is None else list(numbers)
    count = len(numbers)
    tile = row_tile(tokens)
    tiles = tokens // tile
    once = pl.BlockSpec((tile, width), lambda d, i: (jnp.where(d == 0, i, tiles - 1), 0))
    last = pl.BlockSpec((tile, width), lambda d, i: (jnp.where(d == count - 1, i, 0), 0))
    each = pl.BlockSpec((tile, width), lambda d, i: (i, 0))
    chunked = pl.BlockSpec((tile, columns), lambda d, i: (i, d + numbers[0]))
    stack = (tokens, hidden_units)
    if forward:
        kernel, specs = ffn_forward_kernel, [each, once]
        outs = [jax.ShapeDtypeStruct(stack, F32)] * 2 + [jax.ShapeDtypeStruct(stack, BF)]
    else:
        kernel, specs = ffn_backward_kernel, [each, chunked, chunked]
        outs = [jax.ShapeDtypeStruct(stack, BF)] * 2
    first_kept = len(args) + len(groups)
    return pl.pallas_call(
        functools.partial(kernel, widths, numbers, len(kept)),
        grid=(count, tiles),
        out_shape=outs + [jax.ShapeDtypeStruct((tokens, width), F32)],
        in_specs=specs + [ANYWHERE] * (len(groups) + len(kept)),
        out_specs=[chunked] * len(outs) + [last],
        scratch_shapes=[
            pltpu.VMEM((2, 3, width, columns), BF),
            pltpu.VMEM((tokens, width), F32),
            pltpu.SemaphoreType.DMA((2, 3, len(groups))),
        ],
        input_output_aliases={first_kept + i: i for i in range(len(kept))},
        compiler_params=pltpu.CompilerParams(vmem_limit_bytes=VMEM_LIMIT),
        cost_estimate=pl.CostEstimate(
            flops=6 * count * tokens * width * columns,
            bytes_accessed=6 * count * width * columns + 10 * tokens * (count * columns + width),
            transcendentals=0,
        ),
        name="ffn_forward" if forward else "ffn_backward",
    )(*args, *groups, *kept)


def weight_grad_kernel(count, part, has_sum, has_base, index_ref, *refs):
    lefts, rights, rest = refs[:count], refs[count : 2 * count], refs[2 * count :]
    if has_sum:
        sum_ref, rest = rest[0], rest[1:]
    if has_base:
        rest = rest[1:]
    out_ref, held, sems = rest
    entries = held.shape[1] // part

    def copies():
        return [
            pltpu.make_async_copy(
                lefts[which].at[part_rows(index_ref, entry, part)],
                held.at[which, pl.ds(entry * part, part)],
                sems.at[which, entry],
            )
            for which in range(count)
            for entry in range(entries)
        ]

    @pl.when(pl.program_id(0) == 0)
    def _():
        for copy in copies():
            copy.start()
        for copy in copies():
            copy.wait()

    product = jnp.dot(held[0], rights[0][...], preferred_element_type=F32)
    for which in range(1, count):
        product = product + jnp.dot(held[which], rights[which][...], preferred_element_type=F32)
    if has_sum:
        product = product + sum_ref[...].astype(F32)
    out_ref[...] = product.astype(BF)


def weight_grad(lefts, rights, index=None, part=None, arrived=None, within=None):
    features, tokens = lefts[0].shape
    if index is None:
        index, part = jnp.zeros((1,), jnp.int32), features
    elif part % 8 != 0:
        lefts = [left.reshape(-1, part, tokens)[index].reshape(-1, tokens) for left in lefts]
        index, part = jnp.zeros((1,), jnp.int32), lefts[0].shape[0]
    rows, wide = index.shape[0] * part, rights[0].shape[1]
    columns = chunk_of(wide)
    whole_wide, first, base = (wide, 0, None) if within is None else within
    block = pl.BlockSpec((rows, columns), lambda i: (0, i + first // columns))
    args = [*lefts, *rights]
    in_specs = [ANYWHERE] * len(lefts)
    in_specs += [pl.BlockSpec((tokens, columns), lambda i: (0, i))] * len(rights)
    if arrived is not None:
        args.append(arrived)
        in_specs.append(block)
    aliases = {}
    if base is not None:
        aliases = {1 + len(args): 0}
        args.append(base)
        in_specs.append(ANYWHERE)
    return pl.pallas_call(
        functools.partial(
            weight_grad_kernel, len(lefts), part, arrived is not None, base is not None
        ),
        grid=(wide // columns,),
        out_shape=jax.ShapeDtypeStruct((rows, whole_wide), BF),
        in_specs=[SCALARS] + in_specs,
        out_specs=block,
        input_output_aliases=aliases,
        scratch_shapes=[
            pltpu.VMEM((len(lefts), rows, tokens), BF),
            pltpu.SemaphoreType.DMA((len(lefts), index.shape[0])),
        ],
        compiler_params=pltpu.CompilerParams(vmem_limit_bytes=VMEM_LIMIT),
        cost_estimate=pl.CostEstimate(
            flops=2 * rows * tokens * wide * len(lefts),
            bytes_accessed=2 * len(lefts) * (rows + wide) * tokens + 4 * rows * wide,
            transcendentals=0,
        ),
        name="weight_grad",
    )(index, *args)


def picked(value, unit, seq, slots):
    return [
        jnp.concatenate(
            [value[:, (4 * z + slot) * unit : (4 * z + slot + 1) * unit] for z in range(seq)], axis=1
        )
        for slot in slots
    ]


def spread(parts, unit, seq, rows):
    empty = jnp.zeros((rows, unit), BF)
    columns = []
    for z in range(seq):
        for slot in range(4):
            part = parts.get(slot)
            columns.append(empty if part is None else part[:, z * unit : (z + 1) * unit])
    return jnp.concatenate(columns, axis=1)


def row_scale(value):
    return lax.rsqrt(jnp.mean(value * value, axis=-1, keepdims=True) + EPSILON)


def scale_backward(value, gain, grad):
    scale = row_scale(value)
    unit_value = value * scale
    inner = grad * gain
    back = scale * (inner - unit_value * jnp.mean(inner * unit_value, axis=-1, keepdims=True))
    return back, grad * unit_value


def add_rows(step, ref, row, value):
    total = jnp.sum(value, axis=0, keepdims=True)

    @pl.when(step == 0)
    def _():
        ref[row : row + 1, :] = total

    @pl.when(step > 0)
    def _():
        ref[row : row + 1, :] = ref[row : row + 1, :] + total


def project_kernel(shape, unit, seq, index_ref, z_ref, in_ref, gain_ref, *refs):
    part, columns, chips, groups, cores = shape
    pieces, refs = refs[:cores], refs[cores:]
    turned_ref, units_ref, weight_ref, sems = refs
    step = pl.program_id(0)

    def copies():
        made = []
        for other, piece in enumerate(pieces):
            for entry in range(chips):
                for group in range(groups):
                    first = z_ref[group] * columns
                    if columns % LANES == 0:
                        first = pl.multiple_of(first, LANES)
                    lead = entry + other * chips
                    made.append(
                        pltpu.make_async_copy(
                            piece.at[entry, group],
                            weight_ref.at[part_rows(index_ref, lead, part), pl.ds(first, columns)],
                            sems.at[lead * groups + group],
                        )
                    )
        return made

    @pl.when(step == 0)
    def _():
        for copy in copies():
            copy.start()

    value = in_ref[0, 0].astype(F32)
    scale = lax.rsqrt(jnp.mean(value * value, axis=0, keepdims=True) + EPSILON)
    turned = (value * scale * gain_ref[:, 0:1]).astype(BF)
    turned_ref[...] = turned

    @pl.when(step == 0)
    def _():
        for copy in copies():
            copy.wait()

    product = lax.dot_general(turned, weight_ref[...], TN, preferred_element_type=F32).astype(BF)
    for slot, value in enumerate(picked(product, unit, seq, (0, 1, 2))):
        for pair in range(units_ref.shape[0]):
            units_ref[pair, slot] = value[:, pair * LANES : (pair + 1) * LANES]


def out_kernel(unit, seq, pairs, table_ref, weight_ref, in_ref, gain_ref, *refs):
    mixed_refs, (spread_ref, hidden_ref, mid_ref, turned_ref) = refs[:pairs], refs[pairs:]
    mixed = jnp.concatenate([ref[0] for ref in mixed_refs], axis=1)
    wide = spread({3: mixed}, unit, seq, mixed.shape[0])
    spread_ref[...] = wide
    hidden = in_ref[0, 0].astype(F32) + lax.dot_general(
        wide, weight_ref[...], NT, preferred_element_type=F32
    )
    hidden_ref[...] = hidden
    mid = hidden * row_scale(hidden) * gain_ref[1:2, :]
    mid_ref[...] = mid.astype(BF)
    turned_ref[...] = mid.T.astype(BF)


def gate_kernel(out_ref, grad_ref, grad_gate_ref, gain_ref, act_ref, mask_ref, grad_y_ref, low_ref,
                turned_ref, sums_ref):
    step = pl.program_id(0)
    output = out_ref[...]
    act_ref[0, 0] = output.astype(BF)
    gain, weight = gain_ref[2:3, :], gain_ref[3:4, :]
    scale = row_scale(output)
    unit_value = output * scale
    logit = jnp.sum(unit_value * gain * weight, axis=-1, keepdims=True)
    gate = 1.0 / (1.0 + jnp.exp(-logit))
    mask_ref[...] = DELETE_SCALE * gate
    slope = grad_gate_ref[...] * DELETE_SCALE * (gate * (1.0 - gate))
    width = output.shape[1]
    grad_y = grad_ref[0, 0].astype(F32) + (scale * slope) * (
        gain * weight - unit_value * (logit / width)
    )
    grad_y_ref[...] = grad_y
    low_ref[...] = grad_y.astype(BF)
    turned_ref[...] = grad_y.T.astype(BF)
    moved = slope * unit_value
    add_rows(step, sums_ref, 0, moved * weight)
    add_rows(step, sums_ref, 1, moved * gain)


def mid_kernel(unit, seq, weight_ref, grad_mid_ref, hidden_ref, grad_y_ref, gain_ref,
               grad_hidden_ref, turned_ref, grad_mixed_ref, sums_ref):
    step = pl.program_id(0)
    back, moved = scale_backward(hidden_ref[...], gain_ref[1:2, :], grad_mid_ref[...])
    grad_hidden = grad_y_ref[...] + back
    grad_hidden_ref[...] = grad_hidden
    turned_ref[...] = grad_hidden.T.astype(BF)
    product = jnp.dot(grad_hidden.astype(BF), weight_ref[...], preferred_element_type=F32)
    grad_mixed = picked(product.astype(BF), unit, seq, (3,))[0]
    for pair in range(grad_mixed_ref.shape[0]):
        grad_mixed_ref[pair] = grad_mixed[:, pair * LANES : (pair + 1) * LANES]
    add_rows(step, sums_ref, 0, moved)


def spread_kernel(unit, seq, table_ref, *refs):
    unit_refs, spread_ref = refs[:-1], refs[-1]
    parts = {
        slot: jnp.concatenate([ref[0, slot] for ref in unit_refs], axis=1) for slot in range(3)
    }
    spread_ref[...] = spread(parts, unit, seq, spread_ref.shape[0])


def in_kernel(weight_ref, spread_ref, in_ref, grad_hidden_ref, gain_ref, grad_x_ref, sums_ref):
    step = pl.program_id(0)
    grad_in = lax.dot_general(spread_ref[...], weight_ref[...], NT, preferred_element_type=F32)
    back, moved = scale_backward(in_ref[0, 0].astype(F32), gain_ref[0:1, :], grad_in)
    grad_x_ref[0, 0] = (grad_hidden_ref[...] + back).astype(BF)
    add_rows(step, sums_ref, 0, moved)


def row_call(kernel, name, micro_count, rows, ins, outs, scratch=(), flops=0, table=None):
    def spec(shape, kind):
        rest = (0,) * (len(shape) - 1)
        if kind == "rows":
            return pl.BlockSpec((rows, shape[1]), lambda m, *t: (m, 0))
        if kind == "columns":
            return pl.BlockSpec((shape[0], rows), lambda m, *t: (0, m))
        if kind == "micro":
            return pl.BlockSpec(
                (shape[0] // micro_count,) + tuple(shape[1:]), lambda m, *t: (m,) + rest
            )
        if kind == "whole":
            return pl.BlockSpec(tuple(shape), lambda m, *t: (0,) + rest)
        if isinstance(kind, int):
            each = table.shape[0] // micro_count
            return pl.BlockSpec((1,) + tuple(shape[1:]), lambda m, t: (t[m * each + kind],) + rest)
        return SCALARS if kind == "scalars" else ANYWHERE

    moved = sum(value.size * value.dtype.itemsize for value, _ in ins)
    return pl.pallas_call(
        kernel,
        grid_spec=pltpu.PrefetchScalarGridSpec(
            num_scalar_prefetch=0 if table is None else 1,
            grid=(micro_count,),
            in_specs=[spec(value.shape, kind) for value, kind in ins],
            out_specs=[spec(shape, kind) for shape, _, kind in outs],
            scratch_shapes=list(scratch),
        ),
        out_shape=[jax.ShapeDtypeStruct(shape, dtype) for shape, dtype, _ in outs],
        compiler_params=pltpu.CompilerParams(vmem_limit_bytes=VMEM_LIMIT),
        cost_estimate=pl.CostEstimate(flops=flops, bytes_accessed=2 * moved, transcendentals=0),
        name=name,
    )(*([] if table is None else [table]), *[value for value, _ in ins])


def bias_kernel(vector_ref, out_ref):
    slots, rows = out_ref.shape[1:3]
    for slot in range(slots):
        spread_rows = jnp.broadcast_to(vector_ref[0, slot : slot + 1], (rows, 2 * rows))
        if slot in (0, slots - 1):
            out_ref[0, slot] = spread_rows[:, :rows]
        else:
            rolled = pltpu.roll(spread_rows, rows + 1, 1, stride=1, stride_axis=0)
            out_ref[0, slot] = rolled[:, :rows]


def bias_tiles(vectors, rows):
    head_count, slots = vectors.shape[:2]
    return pl.pallas_call(
        bias_kernel,
        grid=(head_count,),
        out_shape=jax.ShapeDtypeStruct((head_count, slots, rows, rows), F32),
        in_specs=[pl.BlockSpec((1, slots, 2 * rows), lambda h: (h, 0, 0))],
        out_specs=pl.BlockSpec((1, slots, rows, rows), lambda h: (h, 0, 0, 0)),
        name="bias",
    )(vectors)


def diagonal_kernel(scores_ref, out_ref):
    slots, rows = scores_ref.shape[1:3]
    for slot in range(slots):
        value = scores_ref[0, slot]
        if slot in (0, slots - 1):
            total = jnp.sum(jnp.sum(value, axis=0, keepdims=True), axis=1, keepdims=True)
            lane = lax.broadcasted_iota(jnp.int32, (1, 2 * rows), 1)
            out_ref[0, slot : slot + 1] = jnp.where(lane == 0, total, 0.0)
        else:
            value = jnp.concatenate([value, jnp.zeros((rows, rows), F32)], axis=1)
            height = rows
            while height > 1:
                height //= 2
                value = value[:height] + pltpu.roll(value[height:], 2 * rows - height, 1)
            out_ref[0, slot : slot + 1] = value


def diagonal_sums(scores):
    head_count, slots, rows, _ = scores.shape
    return pl.pallas_call(
        diagonal_kernel,
        grid=(head_count,),
        out_shape=jax.ShapeDtypeStruct((head_count, slots, 2 * rows), F32),
        in_specs=[pl.BlockSpec((1, slots, rows, rows), lambda h: (h, 0, 0, 0))],
        out_specs=pl.BlockSpec((1, slots, 2 * rows), lambda h: (h, 0, 0)),
        name="diagonals",
    )(scores)


def lane_half(value, half):
    lane = lax.broadcasted_iota(jnp.int32, value.shape, 1)
    return jnp.where((lane >= LANES // 2) == (half == 1), value, jnp.zeros_like(value))


def join_halves(one, two):
    lane = lax.broadcasted_iota(jnp.int32, one.shape, 1)
    return jnp.where(lane >= LANES // 2, two, one)


MICRO, PAIR, PLACE, UNIT, FIRST, LAST, SLOTS = range(7)
SLOT_COUNT = 5


def unit_scores(table_ref, step, half, span, query, keys, same, bias_ref):
    rows = bias_ref.shape[2]
    scores = lax.dot_general(lane_half(query, half), keys, NT, preferred_element_type=F32)
    bias = jnp.concatenate(
        [
            bias_ref[half, table_ref[step, SLOTS + block], span, :]
            for block in range(keys.shape[0] // rows)
        ],
        axis=1,
    )
    return jnp.where(same, scores + bias, MASKED_SCORE)


def forward_kernel(tile, table_ref, query_ref, key_ref, value_ref, query_seg_ref, key_seg_ref,
                   bias_ref, mixed_ref, log_ref):
    step = pl.program_id(0)
    keys, values = key_ref[0], value_ref[0]
    for start in range(0, query_ref.shape[1], tile):
        span = slice(start, start + tile)
        query = query_ref[0, span, :]
        same = query_seg_ref[0, 0, span, :] == key_seg_ref[0]
        mixed, logs = [], []
        for half in range(2):
            scores = unit_scores(table_ref, step, half, span, query, keys, same, bias_ref)
            row_max = jnp.max(scores, axis=1, keepdims=True)
            weight = jnp.exp(scores - row_max)
            total = jnp.sum(weight, axis=1, keepdims=True)
            probs_low = (weight * (1.0 / total)).astype(BF)
            mixed.append(jnp.dot(probs_low, values, preferred_element_type=F32))
            logs.append(row_max + jnp.log(total))
        mixed_ref[0, span, :] = join_halves(mixed[0], mixed[1]).astype(BF)
        log_ref[0, span, :] = jnp.concatenate(logs, axis=1)


def backward_kernel(tile, table_ref, query_ref, grad_ref, log_ref, key_ref, value_ref,
                    query_seg_ref, key_seg_ref, bias_ref, grad_query_ref, grad_kv_ref, sums_ref,
                    key_acc, value_acc):
    step = pl.program_id(0)
    keys, values = key_ref[0], value_ref[0]
    rows = bias_ref.shape[2]

    @pl.when(step == 0)
    def _():
        sums_ref[...] = jnp.zeros(sums_ref.shape, F32)

    @pl.when(table_ref[step, FIRST] == 1)
    def _():
        key_acc[...] = jnp.zeros(key_acc.shape, F32)
        value_acc[...] = jnp.zeros(value_acc.shape, F32)

    for start in range(0, query_ref.shape[1], tile):
        span = slice(start, start + tile)
        query, grad = query_ref[0, span, :], grad_ref[0, span, :]
        same = query_seg_ref[0, 0, span, :] == key_seg_ref[0]
        grad_query, grad_key, grad_value = [], [], []
        for half in range(2):
            scores = unit_scores(table_ref, step, half, span, query, keys, same, bias_ref)
            probs = jnp.exp(scores - log_ref[0, span, half : half + 1])
            grad_probs = lax.dot_general(
                lane_half(grad, half), values, NT, preferred_element_type=F32
            )
            delta = jnp.sum(probs * grad_probs, axis=1, keepdims=True)
            grad_scores = (probs * (grad_probs - delta)).astype(BF)
            head = 2 * table_ref[step, PAIR] + half
            for block in range(keys.shape[0] // rows):
                slot = table_ref[step, SLOTS + block]
                sums_ref[head, slot, span, :] = sums_ref[head, slot, span, :] + grad_scores[
                    :, block * rows : (block + 1) * rows
                ].astype(F32)
            grad_query.append(jnp.dot(grad_scores, keys, preferred_element_type=F32))
            grad_key.append(lax.dot_general(grad_scores, query, TN, preferred_element_type=F32))
            grad_value.append(
                lax.dot_general(probs.astype(BF), grad, TN, preferred_element_type=F32)
            )
        grad_query_ref[0, span, :] = join_halves(*grad_query).astype(BF)
        key_acc[...] = key_acc[...] + join_halves(*grad_key)
        value_acc[...] = value_acc[...] + join_halves(*grad_value)

    @pl.when(table_ref[step, LAST] == 1)
    def _():
        grad_kv_ref[0, 0] = key_acc[...].astype(BF)
        grad_kv_ref[0, 1] = value_acc[...].astype(BF)


def attention(backward, table, query, grads, keys, values, query_seg, key_seg, bias):
    steps, rows, _ = query.shape
    units, key_count, _ = keys.shape
    tile = max(8, min(rows, rows * 1024 // key_count))
    by_step = pl.BlockSpec((1, rows, LANES), lambda s, t: (s, 0, 0))
    log_spec = pl.BlockSpec((1, rows, 2), lambda s, t: (s, 0, 0))
    by_unit = pl.BlockSpec((1, key_count, LANES), lambda s, t: (t[s, UNIT], 0, 0))
    shared = [
        by_unit,
        by_unit,
        pl.BlockSpec((1, 1, rows, 1), lambda s, t: (t[s, MICRO], t[s, PLACE], 0, 0)),
        pl.BlockSpec((1, 1, key_count), lambda s, t: (t[s, MICRO], 0, 0)),
        pl.BlockSpec((2, SLOT_COUNT, rows, rows), lambda s, t: (t[s, PAIR], 0, 0, 0)),
    ]
    if backward:
        kernel = backward_kernel
        in_specs = [by_step, by_step, log_spec] + shared
        out_shape = [
            jax.ShapeDtypeStruct(query.shape, BF),
            jax.ShapeDtypeStruct((units, 2, key_count, LANES), BF),
            jax.ShapeDtypeStruct(bias.shape, F32),
        ]
        out_specs = [
            by_step,
            pl.BlockSpec((1, 2, key_count, LANES), lambda s, t: (t[s, UNIT], 0, 0, 0)),
            pl.BlockSpec(bias.shape, lambda s, t: (0, 0, 0, 0)),
        ]
        scratch = [pltpu.VMEM((key_count, LANES), F32), pltpu.VMEM((key_count, LANES), F32)]
    else:
        kernel = forward_kernel
        in_specs = [by_step] + shared
        out_shape = [
            jax.ShapeDtypeStruct(query.shape, BF), jax.ShapeDtypeStruct((steps, rows, 2), F32)
        ]
        out_specs = [by_step, log_spec]
        scratch = []
    return pl.pallas_call(
        functools.partial(kernel, tile),
        grid_spec=pltpu.PrefetchScalarGridSpec(
            num_scalar_prefetch=1, grid=(steps,), in_specs=in_specs, out_specs=out_specs,
            scratch_shapes=scratch,
        ),
        out_shape=out_shape,
        compiler_params=pltpu.CompilerParams(vmem_limit_bytes=56 << 20),
        cost_estimate=pl.CostEstimate(
            flops=(40 if backward else 16) * steps * rows * key_count * LANES,
            bytes_accessed=8 * steps * rows * key_count,
            transcendentals=0,
        ),
        name="attention_backward" if backward else "attention_forward",
    )(table, query, *grads, keys, values, query_seg, key_seg, bias)


def shards(
    layer_input,
    segment_ids,
    grad_out,
    grad_gate,
    attn_gain,
    w_query,
    w_key,
    w_value,
    w_out,
    rel_table,
    ffn_gain,
    w_gate,
    w_up,
    w_down,
    delete_gain,
    w_delete,
):
    micro_count, _, rows, width = layer_input.shape
    tokens = micro_count * rows
    fsdp, seq = lax.axis_size("fsdp"), lax.axis_size("seq")
    chips = fsdp // 2
    me, place_z = lax.axis_index("fsdp"), lax.axis_index("seq")
    my_chip, my_core = me // 2, me % 2
    part, ff_part = w_gate.shape
    unit = w_query.shape[1]
    heads_width = unit * seq

    order = list(range(0, chips, 2)) + list(range(1, chips, 2))[::-1]
    spot_of = [order.index(chip) for chip in range(chips)]
    my_spot = jnp.asarray(spot_of, jnp.int32)[my_chip]
    ring_xy = Ring("fsdp", order, [lambda chip: 2 * chip, lambda chip: 2 * chip + 1])
    ring_z = Ring("seq", list(range(seq)), [lambda member: member])

    def swap(value):
        return lax.ppermute(value, "fsdp", [(i, i ^ 1) for i in range(fsdp)])

    def offsets_of(size):
        return [0] + [s * k for k in range(1, size // 2) for s in (-1, 1)] + [size // 2]

    z_offsets, xy_offsets = offsets_of(seq), offsets_of(chips)
    z_index = (place_z + jnp.asarray(z_offsets, jnp.int32)) % seq
    chip_index = jnp.asarray(order, jnp.int32)[
        (my_spot + jnp.asarray(xy_offsets, jnp.int32)) % chips
    ]
    my_parts = (2 * chip_index + my_core).astype(jnp.int32)
    other_parts = (2 * chip_index + 1 - my_core).astype(jnp.int32)
    xy_index = jnp.concatenate([my_parts, other_parts])
    aligned = part % 8 == 0 and (4 * unit) % LANES == 0
    piece_index = xy_index if aligned else jnp.zeros((1,), jnp.int32)
    flow = Flow()

    def in_order(mine, other):
        return jnp.concatenate([mine, other])[jnp.argsort(xy_index)]

    def joined(found, offsets, axis, join):
        return join([
            jnp.concatenate(found[k], axis=axis) if isinstance(found[k], tuple) else found[k]
            for k in offsets
        ])

    def beside(values):
        return jnp.concatenate(values, axis=1)

    gain_rows = jnp.stack([attn_gain, ffn_gain, delete_gain, w_delete]).astype(BF)
    seg_local = segment_ids[:, 0]
    extra_rows = -(-tokens // (4 * unit * 8)) * 8
    extra = jnp.pad(seg_local.astype(BF).reshape(-1), (0, extra_rows * 4 * unit - tokens))
    attn_block = jnp.concatenate([w_query, w_key, w_value, w_out.T], axis=1).astype(BF)
    attn_block = jnp.concatenate([attn_block, extra.reshape(extra_rows, 4 * unit)], axis=0)
    ready = {}

    def attn_over_z(found):
        whole = joined(found, z_offsets, 1, jnp.stack)
        ready["seg"] = whole[:, part:]
        return ring_gather(ring_xy, whole[:, :part], halve_first, attn_over_xy)

    def attn_over_xy(found):
        mine = joined(found, xy_offsets, 0, jnp.stack)
        (other,) = yield [(swap, mine)]
        if aligned:
            ready["attn"] = (mine, other)
        else:
            all_parts = in_order(mine, other)[:, jnp.argsort(z_index)].transpose(0, 2, 1, 3)
            ready["attn"] = (all_parts.reshape(1, 1, width, 4 * heads_width),)

    attn = Chain(direct_gather(ring_z, attn_block, attn_over_z))

    def gains_over_xy(found):
        mine = joined(found, xy_offsets, 0, jnp.stack)
        (other,) = yield [(swap, mine)]
        rows_of = in_order(mine, other).astype(F32)
        ready["gains"] = rows_of.transpose(1, 0, 2).reshape(4, width)
        ready["gain_columns"] = rows_of.transpose(0, 2, 1).reshape(width, 4)

    gain_chain = Chain(direct_gather(ring_xy, gain_rows, gains_over_xy))

    ff_block = jnp.concatenate([w_gate, w_up, w_down.T], axis=1).astype(BF)
    z_found = {}

    def over_z(name, value):
        z_found[name] = {}
        return Chain(ring_gather(ring_z, value, halve_last, lambda found: None, z_found[name]))

    def over_fsdp(value):
        return lax.all_gather(value, "fsdp", axis=0, tiled=True)

    def group_of(offsets):
        blocks = []
        for k in offsets:
            pieces = []
            for name in ("left", "right"):
                found = z_found[name][k]
                pieces += list(found) if isinstance(found, tuple) else [found]
            blocks.append(jnp.concatenate(pieces, axis=1))
        return jnp.concatenate(
            [block[:, i * ff_part : (i + 1) * ff_part] for i in range(3) for block in blocks], axis=1
        )

    ff_left, ff_right = (over_z(n, v) for n, v in zip(("left", "right"), halve_last(ff_block)))

    base = (jnp.arange(SLOT_COUNT, dtype=jnp.int32) - SLOT_COUNT // 2) * rows
    distance = base[:, None] + jnp.arange(2 * rows, dtype=jnp.int32)[None, :] - (rows - 1)
    bucket_ids = jnp.arange(rel_table.shape[0], dtype=jnp.int32)
    one_hot = (bucket_of(distance)[:, :, None] == bucket_ids).astype(F32)
    vectors = jnp.einsum(
        "nkb,bh->hnk", one_hot, rel_table, precision=lax.Precision.HIGHEST,
        preferred_element_type=F32,
    )

    pairs = heads_width // LANES
    unit_count = micro_count * pairs
    whole_each = unit_count // seq
    whole_count = whole_each * seq
    rest_count = unit_count - whole_count
    steps = jnp.arange(whole_count + rest_count, dtype=jnp.int32)
    is_whole = steps < whole_count
    step_place = jnp.where(is_whole, steps % seq, 0)
    step_unit = jnp.where(is_whole, place_z * whole_each + steps // seq, steps)
    far = SLOT_COUNT // 2
    table = jnp.concatenate([
        jnp.stack([
            step_unit // pairs,
            step_unit % pairs,
            step_place,
            jnp.where(is_whole, steps // seq, steps - whole_count + whole_each),
            (~is_whole | (step_place == 0)).astype(jnp.int32),
            (~is_whole | (step_place == seq - 1)).astype(jnp.int32),
        ], axis=1),
        jnp.clip(z_index[None, :] - z_index[step_place][:, None], -far, far) + far,
    ], axis=1).astype(jnp.int32)
    rel_of = jnp.argsort(z_index)
    units = jnp.arange(unit_count, dtype=jnp.int32)
    unit_entry = jnp.where(
        units < whole_count,
        rel_of[jnp.minimum(units // max(whole_each, 1), seq - 1)] * whole_each
        + units % max(whole_each, 1),
        units,
    ).astype(jnp.int32)

    def whole_of(value, offset):
        value = value[:whole_count].reshape((seq, whole_each) + value.shape[1:])
        return lax.dynamic_index_in_dim(value, (place_z + offset) % seq, 0, keepdims=False)

    ff_groups = [over_fsdp(ff_block)]
    bias = flow.slot([attn], lambda vectors: bias_tiles(vectors, rows), vectors)
    flow.slot([attn, gain_chain, ff_left])
    flow.slot([attn, gain_chain, ff_right])
    seg = ready["seg"].reshape(seq, -1)[:, :tokens].reshape(seq, micro_count, rows)
    seg = seg.astype(jnp.int32).transpose(1, 0, 2)
    key_seg, query_seg = seg.reshape(micro_count, 1, seq * rows), seg[:, :, :, None]

    turned_shape = ((width, tokens), BF, "columns")
    if aligned:
        project_shape, z_places = (part, 4 * unit, chips, seq, 2), z_index
    else:
        project_shape, z_places = (width, 4 * heads_width, 1, 1, 1), jnp.zeros((1,), jnp.int32)

    def project_step(x, gain_columns):
        return row_call(
            functools.partial(project_kernel, project_shape, unit, seq), "project",
            micro_count, rows,
            [(piece_index, "scalars"), (z_places, "scalars"), (x, "micro"), (gain_columns, "whole")]
            + [(piece, "any") for piece in ready["attn"]],
            [turned_shape, ((unit_count, 3, rows, LANES), BF, "micro"),
             ((width, 4 * heads_width), BF, "whole")],
            [pltpu.SemaphoreType.DMA((fsdp * seq if aligned else 1,))],
            8 * tokens * width * heads_width,
        )

    def project_rest(x, near):
        tied["near"] = near
        attn.run()
        gain_chain.run()
        return project_step(x, ready["gain_columns"])

    sent, tied = {}, {}
    near = [group_of((-step, step)) for step in range(1, seq // 2)] if seq == 4 else []
    in_turned, qkv, attn_weight = flow.slot(
        [attn, gain_chain], project_rest, jnp.swapaxes(layer_input, 2, 3), near
    )
    ff_groups += [over_fsdp(group) for group in tied["near"]]
    gains = ready["gains"]
    def qkv_to(offset):
        whole = whole_of(qkv, offset).reshape(3 * whole_each, rows, LANES)
        rest = qkv[whole_count:, 1:].reshape(2 * rest_count, rows, LANES)
        return jnp.concatenate([whole, rest])

    flow.slot([Chain(exchange(ring_z, z_offsets, qkv_to, lambda found: sent.update(qkv=found)))])
    blocks = sent["qkv"]
    queries = jnp.concatenate(
        [jnp.stack([block[3 * i] for block in blocks]) for i in range(whole_each)]
        + [qkv[whole_count:, 0]]
    )

    def all_blocks(entries):
        return jnp.stack([jnp.concatenate([block[e] for block in blocks]) for e in entries])

    rest_entries = range(3 * whole_each, 3 * whole_each + 2 * rest_count)
    keys = all_blocks([3 * i + 1 for i in range(whole_each)] + list(rest_entries[0::2]))
    values = all_blocks([3 * i + 2 for i in range(whole_each)] + list(rest_entries[1::2]))
    mixed_steps, log_sums = flow.slot(
        [ff_left, ff_right],
        lambda *args: attention(False, table, args[0], (), *args[1:], query_seg, key_seg, bias),
        queries, keys, values,
    )
    flow.finish(ff_left, ff_right)
    if seq != 4:
        ff_groups += [over_fsdp(group_of((-step, step))) for step in range(1, seq // 2)]

    def at_place(value, offset):
        place = z_offsets.index(offset)
        return value[place : whole_count : seq]

    flow.slot(
        [Chain(exchange(
            ring_z, z_offsets, functools.partial(at_place, mixed_steps),
            lambda found: sent.update(mixed=found),
        ))],
        lambda last: tied.update(last=last), group_of((seq // 2,)),
    )
    ff_groups.append(over_fsdp(tied["last"]))
    mixed = jnp.concatenate(sent["mixed"] + [mixed_steps[whole_count:]])
    mixed_spread, hidden, normed_mid, mid_turned = flow.slot(
        [],
        lambda mixed: row_call(
            functools.partial(out_kernel, unit, seq, pairs), "out", micro_count, rows,
            [(attn_weight, "whole"), (layer_input, "micro"), (gains, "whole")]
            + [(mixed, pair) for pair in range(pairs)],
            [((tokens, 4 * heads_width), BF, "rows"), ((tokens, width), F32, "rows"),
             ((tokens, width), BF, "rows"), turned_shape],
            (), 8 * tokens * width * heads_width, unit_entry,
        ),
        mixed,
    )
    hidden_units = seq * ff_part
    columns = chunk_of(hidden_units)
    if ff_part % LANES == 0:
        early = (hidden_units - ff_part) // columns
        *factors, output = flow.slot(
            [],
            lambda *args: ffn_call(
                True, args, ff_groups[:-1], hidden_units, range(early)
            ),
            normed_mid, hidden,
        )
        to_gate, to_up, act, output = flow.slot(
            [],
            lambda mid, output, *factors: ffn_call(
                True, (mid, output), ff_groups, hidden_units,
                range(early, hidden_units // columns), factors,
            ),
            normed_mid, output, *factors,
        )
    else:
        widths = [group.shape[1] // 3 for group in ff_groups]
        ff_groups = [jnp.concatenate(
            [
                group[:, i * wide : (i + 1) * wide]
                for i in range(3) for group, wide in zip(ff_groups, widths)
            ],
            axis=1,
        )]
        to_gate, to_up, act, output = flow.slot(
            [], lambda *args: ffn_call(True, args, ff_groups, hidden_units), normed_mid, hidden
        )

    activations, gate_mask, grad_y, grad_y_low, y_turned, gate_sums = flow.slot(
        [],
        lambda output: row_call(
            gate_kernel, "gate", micro_count, rows,
            [(output, "rows"), (grad_out, "micro"), (grad_gate.reshape(tokens, 1), "rows"),
             (gains, "whole")],
            [(layer_input.shape, BF, "micro"), ((tokens, 1), F32, "rows"),
             ((tokens, width), F32, "rows"), ((tokens, width), BF, "rows"), turned_shape,
             ((2, width), F32, "whole")],
        ),
        output,
    )
    ff_grad = {}

    def over_z_back(name, value):
        blocks = {
            k: value[:, i * ff_part : (i + 1) * ff_part] for i, k in enumerate(z_offsets)
        }
        return Chain(
            direct_scatter(ring_z, blocks, lambda total: ff_grad.update({name: total}))
        )

    def scattered(value):
        return lax.optimization_barrier(
            lax.psum_scatter(value, "fsdp", scatter_dimension=0, tiled=True)
        )

    grad_down = scattered(flow.slot([], lambda *args: weight_grad(args[:1], args[1:]), y_turned, act))
    grad_gate_pre, grad_up_pre, grad_mid = flow.slot(
        [], lambda *args: ffn_call(False, args, ff_groups, hidden_units), grad_y_low, to_gate, to_up
    )
    def mid_step(grad_mid, hidden, grad_y, mid_turned, grad_up_pre):
        return weight_grad(
            (mid_turned,), (grad_up_pre,), within=(2 * hidden_units, hidden_units, None)
        ), row_call(
            functools.partial(mid_kernel, unit, seq), "mid", micro_count, rows,
            [(attn_weight, "whole"), (grad_mid, "rows"), (hidden, "rows"), (grad_y, "rows"),
             (gains, "whole")],
            [((tokens, width), F32, "rows"), turned_shape, ((unit_count, rows, LANES), BF, "micro"),
             ((1, width), F32, "whole")],
            (), 8 * tokens * width * heads_width,
        )

    half_full, (grad_hidden, hidden_turned, grad_mixed, mid_sums) = flow.slot(
        [], mid_step, grad_mid, hidden, grad_y, mid_turned, grad_up_pre
    )
    pair_full = flow.slot(
        [Chain(exchange(
            ring_z, z_offsets, functools.partial(whole_of, grad_mixed),
            lambda found: sent.update(grad=found),
        ))],
        lambda mid_turned, grad_gate_pre, base: weight_grad(
            (mid_turned,), (grad_gate_pre,), within=(2 * hidden_units, 0, base)
        ),
        mid_turned, grad_gate_pre, half_full,
    )
    grad_steps = jnp.concatenate(
        [jnp.stack([block[i] for block in sent["grad"]]) for i in range(whole_each)]
        + [grad_mixed[whole_count:]]
    )
    down_back = over_z_back("down", grad_down)

    def attention_step(pair_full, query, grads, logs, keys, values):
        tied["pair"] = pair_full
        return attention(True, table, query, (grads, logs), keys, values, query_seg, key_seg, bias)

    grad_q, grad_kv, sums = flow.slot(
        [down_back], attention_step, pair_full, queries, grad_steps, log_sums, keys, values
    )
    grad_pair_mat = scattered(tied["pair"])
    kv_blocks = grad_kv.reshape(whole_each + rest_count, 2, seq, rows, LANES)

    def grads_to(offset):
        place = z_offsets.index(offset)
        kv = kv_blocks[:, :, place]
        whole = jnp.concatenate([at_place(grad_q, offset)[:, None], kv[:whole_each]], axis=1)
        return jnp.concatenate([
            whole.reshape(3 * whole_each, rows, LANES),
            kv[whole_each:].reshape(2 * rest_count, rows, LANES),
        ])

    diagonals = flow.slot(
        [Chain(exchange(ring_z, z_offsets, grads_to, lambda found: sent.update(back=found)))],
        diagonal_sums, sums,
    )
    wrapped = jnp.arange(2 * rows, dtype=jnp.int32)
    wrapped = jnp.where(wrapped < rows, wrapped, wrapped - 2 * rows)
    buckets = bucket_of(base[:, None] + wrapped[None, :])
    one_hot = (buckets[:, :, None] == bucket_ids).astype(F32)
    table_grad = jnp.einsum(
        "hnk,nkb->bh", diagonals, one_hot, precision=lax.Precision.HIGHEST,
        preferred_element_type=F32,
    )
    back = sent["back"]
    whole_back = [
        block[: 3 * whole_each].reshape(whole_each, 3, rows, LANES) for block in back
    ]
    rest_sum = sum(block[3 * whole_each :].astype(F32) for block in back).astype(BF)
    rest_back = jnp.concatenate([
        grad_q[whole_count:, None], rest_sum.reshape(rest_count, 2, rows, LANES)
    ], axis=1)
    grad_units = jnp.concatenate(whole_back + [rest_back])
    def spread_step(grad_units):
        (grad_spread,) = row_call(
            functools.partial(spread_kernel, unit, seq), "spread", micro_count, rows,
            [(grad_units, pair) for pair in range(pairs)],
            [((tokens, 4 * heads_width), BF, "rows")], (), 0, unit_entry,
        )
        return grad_spread, weight_grad((in_turned, hidden_turned), (grad_spread, mixed_spread))

    grad_spread, attn_full = flow.slot([], spread_step, grad_units)

    def in_step(attn_full, grad_spread, grad_hidden):
        tied["attn"] = attn_full
        return row_call(
            in_kernel, "in", micro_count, rows,
            [(attn_weight, "whole"), (grad_spread, "rows"), (layer_input, "micro"),
             (grad_hidden, "rows"), (gains, "whole")],
            [(layer_input.shape, BF, "micro"), ((1, width), F32, "whole")],
            (), 8 * tokens * width * heads_width,
        )

    grad_x, in_sums = flow.slot([], in_step, attn_full, grad_spread, grad_hidden)
    attn_mat = scattered(tied["attn"])
    vector = jnp.concatenate([
        in_sums.reshape(-1), mid_sums.reshape(-1), gate_sums.reshape(-1), table_grad.reshape(-1)
    ])
    vector = jnp.pad(vector, (0, -vector.shape[0] % 1024)).reshape(-1, LANES)
    summed = []

    def sum_steps(vector):
        for axis, size in (("fsdp", fsdp), ("seq", seq)):
            step = 1
            while step < size:
                pairs = [(i, i ^ step) for i in range(size)]
                (other,) = yield [(functools.partial(lax.ppermute, axis_name=axis, perm=pairs), vector)]
                vector = vector + other
                step *= 2
        summed.append(vector)

    sum_chain = Chain(sum_steps(vector))
    def pair_finish(total):
        ff_grad.update(gate=total[:, :ff_part], up=total[:, ff_part:])

    pair_back = Chain(ring_scatter(
        ring_z,
        {
            k: jnp.concatenate(
                [
                    grad_pair_mat[:, first + i * ff_part : first + (i + 1) * ff_part]
                    for first in (0, hidden_units)
                ],
                axis=1,
            )
            for i, k in enumerate(z_offsets)
        },
        lambda value: (value[:, :ff_part], value[:, ff_part:]), 1, pair_finish,
    ))
    flow.slot([pair_back, sum_chain], lambda: sum_chain.run())
    flow.finish(pair_back)
    attn_grad = []
    by_offset = {
        k: lax.dynamic_slice_in_dim(attn_mat, z_index[i] * (4 * unit), 4 * unit, 1)
        for i, k in enumerate(z_offsets)
    }
    flow.slot([Chain(direct_scatter(ring_z, by_offset, attn_grad.append))])
    vector = summed[0].reshape(-1)
    gains_sum = vector[: 4 * width].reshape(4, width)
    table_sum = vector[4 * width : 4 * width + table_grad.size].reshape(table_grad.shape)
    gains_part = lax.dynamic_slice_in_dim(gains_sum, me * part, part, 1)
    attn_grad = attn_grad[0]

    return (
        activations,
        gate_mask.reshape(micro_count, 1, rows),
        grad_x,
        gains_part[0],
        attn_grad[:, :unit],
        attn_grad[:, unit : 2 * unit],
        attn_grad[:, 2 * unit : 3 * unit],
        attn_grad[:, 3 * unit :].T,
        table_sum,
        gains_part[1],
        ff_grad["gate"],
        ff_grad["up"],
        ff_grad["down"].T,
        gains_part[2],
        gains_part[3],
    )


def solution(mesh):
    return jax.shard_map(
        shards,
        mesh=mesh,
        in_specs=(
            P(None, "fsdp", "seq", None),
            P(None, "fsdp", "seq"),
            P(None, "fsdp", "seq", None),
            P(None, "fsdp", "seq"),
            P("fsdp"),
            P("fsdp", "seq"),
            P("fsdp", "seq"),
            P("fsdp", "seq"),
            P("seq", "fsdp"),
            P(),
            P("fsdp"),
            P("fsdp", "seq"),
            P("fsdp", "seq"),
            P("seq", "fsdp"),
            P("fsdp"),
            P("fsdp"),
        ),
        out_specs=(
            P(None, "fsdp", "seq", None),
            P(None, "fsdp", "seq"),
            P(None, "fsdp", "seq", None),
            P("fsdp"),
            P("fsdp", "seq"),
            P("fsdp", "seq"),
            P("fsdp", "seq"),
            P("seq", "fsdp"),
            P(),
            P("fsdp"),
            P("fsdp", "seq"),
            P("fsdp", "seq"),
            P("seq", "fsdp"),
            P("fsdp"),
            P("fsdp"),
        ),
        check_vma=False,
    )
```

profile of v0, /device:TPU:0, one launch (start us, length us, event | category | flops | bytes accessed | tf_op | source)
XLA Modules:
  0.0 609.7 jit_solution(17418692515687795305)
XLA Ops:
  12.8 3.1 collective-permute-start
  19.1 5.5 bias.1.bias_ref
  24.8 6.4 %collective-permute-done.2 = bf16[192,384]{1,0:T(8,128)(2,1)S(1)} collective-permute-done((bf16[192,384]{1,0:T(8,128)(2,1)S(1)}, bf16[192,384]{1,0:T(8,128)(2,1)S(1)}, u32[]{:S(2)}, u32[]{:S(2)}) %collective-permute-start.2) | collective-permute-done | bytes 147488 | tf_op jit(solution)/shard_map/ppermute | solution.py:55
  33.6 3.8 collective-permute-start.4
  38.9 11.2 %collective-permute-done.8 = bf16[4,184]{1,0:T(4,128)(2,1)S(1)} collective-permute-done((bf16[4,184]{1,0:T(4,128)(2,1)S(1)}, bf16[4,184]{1,0:T(4,128)(2,1)S(1)}, u32[]{:S(2)}, u32[]{:S(2)}) %collective-permute-start.8) | collective-permute-done | bytes 1504 | tf_op jit(solution)/shard_map/ppermute | solution.py:55
  51.5 3.2 collective-permute-done.9
  61.2 3.2 collective-permute-start.11
  64.5 8.0 %collective-permute-done.12 = bf16[2,184,384]{2,1,0:T(8,128)(2,1)S(1)} collective-permute-done((bf16[2,184,384]{2,1,0:T(8,128)(2,1)S(1)}, bf16[2,184,384]{2,1,0:T(8,128)(2,1)S(1)}, u32[]{:S(2)}, u32[]{:S(2)}) %collective-permute-start.12) | collective-permute-done | bytes 282656 | tf_op jit(solution)/shard_map/ppermute | solution.py:45
  77.1 4.7 collective-permute-done.11
  90.6 11.2 %project.1 = (bf16[1472,768]{1,0:T(8,128)(2,1)}, bf16[9,3,256,128]{3,2,1,0:T(8,128)(2,1)}, bf16[1472,1536]{1,0:T(8,128)(2,1)}) custom-call(s32[8]{0:T(128)} %copy-done.39, s32[4]{0:T(128)} %copy-done.2, bf16[3,1,1472,256]{3,2,1,0:T(8,128)(2,1)} %bitcast.207, f32[1472,4]{1,0:T(8,128)} %bitcast.227, bf16[4,4,184,384]{3,2,1,0:T(8,128)(2,1)} %pad_maximum_fusion.refs_0_, ...), custom_call_target="tpu_custom_call" | custom-call | flops 3472883712 | bytes 13613152 | tf_op jit(solution)/shard_map/project/pallas_call | solution.py:616
  110.1 2.5 collective-permute-start.17
  113.8 8.4 %collective-permute-done.16 = bf16[8,256,128]{2,1,0:T(8,128)(2,1)S(1)} collective-permute-done((bf16[8,256,128]{2,1,0:T(8,128)(2,1)}, bf16[8,256,128]{2,1,0:T(8,128)(2,1)S(1)}, u32[]{:S(2)}, u32[]{:S(2)}) %collective-permute-start.16) | collective-permute-done | bytes 524320 | tf_op jit(solution)/shard_map/ppermute | solution.py:55
  122.2 10.7 %collective-permute-done.17 = bf16[8,256,128]{2,1,0:T(8,128)(2,1)S(1)} collective-permute-done((bf16[8,256,128]{2,1,0:T(8,128)(2,1)S(1)}, bf16[8,256,128]{2,1,0:T(8,128)(2,1)S(1)}, u32[]{:S(2)}, u32[]{:S(2)}) %collective-permute-start.17) | collective-permute-done | bytes 524320 | tf_op jit(solution)/shard_map/ppermute | solution.py:55
  132.9 22.5 %collective-permute-done.18 = bf16[8,256,128]{2,1,0:T(8,128)(2,1)S(1)} collective-permute-done((bf16[8,256,128]{2,1,0:T(8,128)(2,1)S(1)}, bf16[8,256,128]{2,1,0:T(8,128)(2,1)S(1)}, u32[]{:S(2)}, u32[]{:S(2)}) %collective-permute-start.18) | collective-permute-done | bytes 524320 | tf_op jit(solution)/shard_map/ppermute | solution.py:55
  160.6 2.9 collective-permute-start.20
  163.5 18.7 %attention_forward.1 = (bf16[9,256,128]{2,1,0:T(8,128)(2,1)}, f32[9,256,2]{2,1,0:T(8,128)}) custom-call(s32[9,10]{1,0:T(8,128)} %concatenate.147.table_ref, bf16[9,256,128]{2,1,0:T(8,128)(2,1)} %copy-done.28, bf16[3,1024,128]{2,1,0:T(8,128)(2,1)} %pad_maximum_fusion.5.key_ref, bf16[3,1024,128]{2,1,0:T(8,128)(2,1)} %pad_maximum_fusion.6.value_ref, ...), custom_call_target="tpu_custom_call" | custom-call | flops 4831838208 | bytes 18874368 | tf_op jit(solution)/shard_map/attention_forward/pallas_call | solution.py:818
  186.8 4.0 collective-permute-start.24
  193.8 4.4 copy.76.grad_ref
  201.6 4.5 collective-permute-done.25
  208.3 10.6 %out.1 = (bf16[768,1536]{1,0:T(8,128)(2,1)}, f32[768,1472]{1,0:T(8,128)}, bf16[768,1472]{1,0:T(8,128)(2,1)}, bf16[1472,768]{1,0:T(8,128)(2,1)}) custom-call(s32[9]{0:T(128)} %compare_select_fusion.11.table_ref, bf16[1472,1536]{1,0:T(8,128)(2,1)} %get-tuple-element.155.weight_ref, bf16[3,1,256,1472]{3,2,1,0:T(8,128)(2,1)} %copy.75.in_ref, ...), custom_call_target="tpu_custom_call" | custom-call | flops 3472883712 | bytes 17152000 | tf_op jit(solution)/shard_map/out/pallas_call | solution.py:616
  218.9 31.9 %ffn_forward.2 = (f32[768,3584]{1,0:T(8,128)}, f32[768,3584]{1,0:T(8,128)}, bf16[768,3584]{1,0:T(8,128)(2,1)}, f32[768,1472]{1,0:T(8,128)}) custom-call(bf16[768,1472]{1,0:T(8,128)(2,1)} %get-tuple-element.185.mid_ref, f32[768,1472]{1,0:T(8,128)} %get-tuple-element.211.in_ref.hidden_ref, bf16[1472,2688]{1,0:T(8,128)(2,1)} %all-gather.4.cloned.1.call-done.refs_0_, ...), custom_call_target="tpu_custom_call" | custom-call | flops 17364418560 | bytes 53575680 | tf_op jit(solution)/shard_map/ffn_forward/pallas_call | solution.py:339
  250.9 16.8 %ffn_forward.3 = (f32[768,3584]{1,0:T(8,128)}, f32[768,3584]{1,0:T(8,128)}, bf16[768,3584]{1,0:T(8,128)(2,1)}, f32[768,1472]{1,0:T(8,128)}) custom-call(bf16[768,1472]{1,0:T(8,128)(2,1)} %get-tuple-element.185.mid_ref, f32[768,1472]{1,0:T(8,128)} %get-tuple-element.186.in_ref, ...), custom_call_target="tpu_custom_call", output_to_operand_aliasing={{0}: (5, {}), {1}: (6, {}), {2}: (7, {})} | custom-call | flops 6945767424 | bytes 28213248 | tf_op jit(solution)/shard_map/ffn_forward/pallas_call | solution.py:339
  267.7 9.9 %gate.1 = (bf16[3,1,256,1472]{3,2,1,0:T(8,128)(2,1)}, f32[768,1]{1,0:T(8,128)}, f32[768,1472]{1,0:T(8,128)}, bf16[768,1472]{1,0:T(8,128)(2,1)}, bf16[1472,768]{1,0:T(8,128)(2,1)}, /*index=5*/f32[2,1472]{1,0:T(2,128)}) custom-call(f32[768,1472]{1,0:T(8,128)} %get-tuple-element.195.out_ref, bf16[3,1,256,1472]{3,2,1,0:T(8,128)(2,1)} %copy.76.grad_ref, ...), custom_call_target="tpu_custom_call" | custom-call | bytes 13619200 | tf_op jit(solution)/shard_map/gate/pallas_call | solution.py:616
  277.6 14.5 %weight_grad.4 = bf16[1472,3584]{1,0:T(8,128)(2,1)} custom-call(s32[1]{0:T(128)} %constant.216.clone.1.index_ref, bf16[1472,768]{1,0:T(8,128)(2,1)} %get-tuple-element.202.refs_0_, bf16[768,3584]{1,0:T(8,128)(2,1)} %get-tuple-element.203.refs_1_), custom_call_target="tpu_custom_call" | custom-call | flops 8103395328 | bytes 28868608 | tf_op jit(solution)/shard_map/weight_grad/pallas_call | solution.py:418
  292.4 42.8 %ffn_backward.1 = (bf16[768,3584]{1,0:T(8,128)(2,1)}, bf16[768,3584]{1,0:T(8,128)(2,1)}, f32[768,1472]{1,0:T(8,128)}) custom-call(bf16[768,1472]{1,0:T(8,128)(2,1)} %get-tuple-element.204.grad_ref, f32[768,3584]{1,0:T(8,128)} %get-tuple-element.205.to_gate_ref, f32[768,3584]{1,0:T(8,128)} %get-tuple-element.206.to_up_ref, ...), custom_call_target="tpu_custom_call" | custom-call | flops 24310185984 | bytes 70483968 | tf_op jit(solution)/shard_map/ffn_backward/pallas_call | solution.py:339
  335.2 13.7 %mid.1 = (f32[768,1472]{1,0:T(8,128)}, bf16[1472,768]{1,0:T(8,128)(2,1)}, bf16[9,256,128]{2,1,0:T(8,128)(2,1)}, f32[1,1472]{1,0:T(1,128)}) custom-call(bf16[1472,1536]{1,0:T(8,128)(2,1)} %get-tuple-element.155.weight_ref, f32[768,1472]{1,0:T(8,128)} %get-tuple-element.210.grad_mid_ref, f32[768,1472]{1,0:T(8,128)} %get-tuple-element.211.in_ref.hidden_ref, ...), custom_call_target="tpu_custom_call" | custom-call | flops 3472883712 | bytes 36222976 | tf_op jit(solution)/shard_map/mid/pallas_call | solution.py:616
  350.0 14.6 %weight_grad.5.refs_2_ = bf16[1472,7168]{1,0:T(8,128)(2,1)} custom-call(s32[1]{0:T(128)} %constant.216.clone.1.index_ref, bf16[1472,768]{1,0:T(8,128)(2,1)} %get-tuple-element.219.refs_0_, bf16[768,3584]{1,0:T(8,128)(2,1)} %get-tuple-element.215.refs_1_), custom_call_target="tpu_custom_call" | custom-call | flops 8103395328 | bytes 28868608 | tf_op jit(solution)/shard_map/weight_grad/pallas_call | solution.py:418
  364.6 3.8 collective-permute-start.27
  368.4 14.6 %weight_grad.6 = bf16[1472,7168]{1,0:T(8,128)(2,1)} custom-call(s32[1]{0:T(128)} %constant.216.clone.1.index_ref, bf16[1472,768]{1,0:T(8,128)(2,1)} %get-tuple-element.219.refs_0_, bf16[768,3584]{1,0:T(8,128)(2,1)} %get-tuple-element.220.refs_1_, bf16[1472,7168]{1,0:T(8,128)(2,1)} %weight_grad.5.refs_2_), custom_call_target="tpu_custom_call", output_to_operand_aliasing={{}: (3, {})} | custom-call | flops 8103395328 | bytes 28868608 | tf_op jit(solution)/shard_map/weight_grad/pallas_call | solution.py:418
  387.7 2.8 collective-permute-start.31
  390.6 30.8 %attention_backward.1 = (bf16[9,256,128]{2,1,0:T(8,128)(2,1)}, bf16[3,2,1024,128]{3,2,1,0:T(8,128)(2,1)}, f32[6,5,256,256]{3,2,1,0:T(8,128)}) custom-call(s32[9,10]{1,0:T(8,128)} %concatenate.147.table_ref, bf16[9,256,128]{2,1,0:T(8,128)(2,1)} %copy-done.28, bf16[9,256,128]{2,1,0:T(8,128)(2,1)} %copy-done.29, f32[9,256,2]{2,1,0:T(8,128)} %get-tuple-element.227.log_ref, ...), custom_call_target="tpu_custom_call" | custom-call | flops 12079595520 | bytes 18874368 | tf_op jit(solution)/shard_map/attention_backward/pallas_call | solution.py:818
  427.9 3.8 collective-permute-start.33
  432.6 7.1 %diagonals.1 = f32[6,5,512]{2,1,0:T(8,128)} custom-call(f32[6,5,256,256]{3,2,1,0:T(8,128)} %get-tuple-element.239.scores_ref), custom_call_target="tpu_custom_call" | custom-call | tf_op jit(solution)/shard_map/diagonals/pallas_call | solution.py:674
  439.7 4.8 collective-permute-done.32
  444.6 7.3 %collective-permute-done.33 = bf16[8,256,128]{2,1,0:T(8,128)(2,1)S(1)} collective-permute-done((bf16[8,256,128]{2,1,0:T(8,128)(2,1)}, bf16[8,256,128]{2,1,0:T(8,128)(2,1)S(1)}, u32[]{:S(2)}, u32[]{:S(2)}) %collective-permute-start.33) | collective-permute-done | bytes 524320 | tf_op jit(solution)/shard_map/ppermute | solution.py:55
  451.9 20.1 %collective-permute-done.34 = bf16[8,256,128]{2,1,0:T(8,128)(2,1)S(1)} collective-permute-done((bf16[8,256,128]{2,1,0:T(8,128)(2,1)}, bf16[8,256,128]{2,1,0:T(8,128)(2,1)S(1)}, u32[]{:S(2)}, u32[]{:S(2)}) %collective-permute-start.34) | collective-permute-done | bytes 524320 | tf_op jit(solution)/shard_map/ppermute | solution.py:55
  474.4 5.0 spread.1.refs_2_.spread_ref
  479.4 12.7 %weight_grad.7 = bf16[1472,1536]{1,0:T(8,128)(2,1)} custom-call(s32[1]{0:T(128)} %constant.216.clone.1.index_ref, bf16[1472,768]{1,0:T(8,128)(2,1)} %get-tuple-element.157.refs_0_, bf16[1472,768]{1,0:T(8,128)(2,1)} %get-tuple-element.213.refs_1_, bf16[768,1536]{1,0:T(8,128)(2,1)} %spread.1.refs_2_.spread_ref, bf16[768,1536]{1,0:T(8,128)(2,1)} %get-tuple-element.176.refs_3_), custom_call_target="tpu_custom_call" | custom-call | flops 6945767424 | bytes 18284544 | tf_op jit(solution)/shard_map/weight_grad/pallas_call | solution.py:418
  493.5 10.1 %in.1 = (bf16[3,1,256,1472]{3,2,1,0:T(8,128)(2,1)}, f32[1,1472]{1,0:T(1,128)}) custom-call(bf16[1472,1536]{1,0:T(8,128)(2,1)} %get-tuple-element.155.weight_ref, bf16[768,1536]{1,0:T(8,128)(2,1)} %spread.1.refs_2_.spread_ref, bf16[3,1,256,1472]{3,2,1,0:T(8,128)(2,1)} %copy.75.in_ref, f32[768,1472]{1,0:T(8,128)} %get-tuple-element.242.grad_hidden_ref, ...), custom_call_target="tpu_custom_call" | custom-call | flops 3472883712 | bytes 27375616 | tf_op jit(solution)/shard_map/in/pallas_call | solution.py:616
  504.4 18.3 %reduce-scatter.10.cloned.1.call-done = bf16[184,7168]{1,0:T(8,128)(2,1)} async-done(((bf16[1472,7168]{1,0:T(8,128)(2,1)}), bf16[184,7168]{1,0:T(8,128)(2,1)}) %reduce-scatter.10.cloned.1.call-update) | async-done | bytes 2637840
  530.9 6.0 collective-permute-done.40
  536.9 5.2 collective-permute-done.41
  546.4 2.6 collective-permute-start.43
  561.7 17.4 %reduce-scatter.8.cloned.1.call-done = bf16[184,1536]{1,0:T(8,128)(2,1)} async-done(((bf16[1472,1536]{1,0:T(8,128)(2,1)}), bf16[184,1536]{1,0:T(8,128)(2,1)}) %reduce-scatter.8.cloned.1.call-update) | async-done | bytes 565264 | tf_op jit(solution)/shard_map/reduce_scatter | solution.py:1146
  579.1 2.5 collective-permute-start.39
  585.5 3.6 collective-permute-start.44
  593.3 3.7 collective-permute-done.45
  597.0 3.6 collective-permute-done.46
  (345 shorter events, 111.4 us)
Async XLA Ops:
  7.2 211.7 %all-gather.4.cloned.1.call-start = ((), (), s32[]{:S(2)}) async-start(), calls=%async_computation.3 | async-start | bytes 8902656 | tf_op jit(solution)/shard_map/all_gather | solution.py:940
  10.8 208.1 %all-gather.6.cloned.1.call-start = ((), (), s32[]{:S(2)}) async-start(), calls=%async_computation.4 | async-start | bytes 17805312 | tf_op jit(solution)/shard_map/all_gather | solution.py:940
  12.8 12.0 %collective-permute-start = (bf16[192,384]{1,0:T(8,128)(2,1)S(1)}, bf16[192,384]{1,0:T(8,128)(2,1)S(1)}, u32[]{:S(2)}, u32[]{:S(2)}) collective-permute-start(bf16[192,384]{1,0:T(8,128)(2,1)S(1)} %pad_maximum_fusion.20), channel_id=1, source_target_pairs={{3,0},{0,1},{1,2},{2,3},{7,4},{4,5},{5,6},{6,7},{11,8},{8,9},{9,10... | collective-permute-start | bytes 442376 | tf_op jit(solution)/shard_map/ppermute | solution.py:55
  15.9 8.9 %collective-permute-start.1 = (bf16[192,384]{1,0:T(8,128)(2,1)S(1)}, bf16[192,384]{1,0:T(8,128)(2,1)S(1)}, u32[]{:S(2)}, u32[]{:S(2)}) collective-permute-start(bf16[192,384]{1,0:T(8,128)(2,1)S(1)} %pad_maximum_fusion.20), channel_id=1, source_target_pairs={{1,0},{2,1},{3,2},{0,3},{5,4},{6,5},{7,6},{4,7},{9,8},{10,9},{11,1... | collective-permute-start | bytes 442376 | tf_op jit(solution)/shard_map/ppermute | solution.py:55
  18.0 13.3 %collective-permute-start.2 = (bf16[192,384]{1,0:T(8,128)(2,1)S(1)}, bf16[192,384]{1,0:T(8,128)(2,1)S(1)}, u32[]{:S(2)}, u32[]{:S(2)}) collective-permute-start(bf16[192,384]{1,0:T(8,128)(2,1)S(1)} %pad_maximum_fusion.20), channel_id=1, source_target_pairs={{2,0},{3,1},{0,2},{1,3},{6,4},{7,5},{4,6},{5,7},{10,8},{11,9},{8,1... | collective-permute-start | bytes 442376 | tf_op jit(solution)/shard_map/ppermute | solution.py:55
  31.5 26.8 %collective-permute-start.5 = (bf16[4,184,384]{2,1,0:T(8,128)(2,1)S(1)}, bf16[4,184,384]{2,1,0:T(8,128)(2,1)S(1)}, u32[]{:S(2)}, u32[]{:S(2)}) collective-permute-start(bf16[4,184,384]{2,1,0:T(8,128)(2,1)S(1)} %get-tuple-element.143), channel_id=1, source_target_pairs={{0,16},{16,24},{24,8},{8,0},{4,20},{20,28},{28,12},{12,4},{1,17},{... | collective-permute-start | bytes 1695752 | tf_op jit(solution)/shard_map/ppermute | solution.py:45
  33.0 25.3 %collective-permute-start.6 = (bf16[4,184,384]{2,1,0:T(8,128)(2,1)S(1)}, bf16[4,184,384]{2,1,0:T(8,128)(2,1)S(1)}, u32[]{:S(2)}, u32[]{:S(2)}) collective-permute-start(bf16[4,184,384]{2,1,0:T(8,128)(2,1)S(1)} %get-tuple-element.143), channel_id=1, source_target_pairs={{16,0},{24,16},{8,24},{0,8},{20,4},{28,20},{12,28},{4,12},{17,1},{... | collective-permute-start | bytes 1695752 | tf_op jit(solution)/shard_map/ppermute | solution.py:48
  33.5 24.8 %collective-permute-start.3 = (bf16[184,1280]{1,0:T(8,128)(2,1)S(1)}, bf16[184,1280]{1,0:T(8,128)(2,1)S(1)}, u32[]{:S(2)}, u32[]{:S(2)}) collective-permute-start(bf16[184,1280]{1,0:T(8,128)(2,1)S(1)} %pad_maximum_fusion.14), channel_id=1, source_target_pairs={{0,1},{1,2},{2,3},{3,0},{4,5},{5,6},{6,7},{7,4},{8,9},{9,10},{10,1... | collective-permute-start | bytes 1413128 | tf_op jit(solution)/shard_map/ppermute | solution.py:45
  33.6 24.8 %collective-permute-start.4 = (bf16[184,1280]{1,0:T(8,128)(2,1)S(1)}, bf16[184,1280]{1,0:T(8,128)(2,1)S(1)}, u32[]{:S(2)}, u32[]{:S(2)}) collective-permute-start(bf16[184,1280]{1,0:T(8,128)(2,1)S(1)} %pad_maximum_fusion.14), channel_id=1, source_target_pairs={{1,0},{2,1},{3,2},{0,3},{5,4},{6,5},{7,6},{4,7},{9,8},{10,9},{11,1... | collective-permute-start | bytes 1413128 | tf_op jit(solution)/shard_map/ppermute | solution.py:48
  37.4 12.7 %collective-permute-start.8 = (bf16[4,184]{1,0:T(4,128)(2,1)S(1)}, bf16[4,184]{1,0:T(4,128)(2,1)S(1)}, u32[]{:S(2)}, u32[]{:S(2)}) collective-permute-start(bf16[4,184]{1,0:T(4,128)(2,1)S(1)} %pad_maximum_fusion.22), channel_id=1, source_target_pairs={{16,0},{24,16},{8,24},{0,8},{20,4},{28,20},{12,28},{4,12},{17,1},{... | collective-permute-start | bytes 4424 | tf_op jit(solution)/shard_map/ppermute | solution.py:55
  58.4 14.1 %collective-permute-start.12 = (bf16[2,184,384]{2,1,0:T(8,128)(2,1)S(1)}, bf16[2,184,384]{2,1,0:T(8,128)(2,1)S(1)}, u32[]{:S(2)}, u32[]{:S(2)}) collective-permute-start(bf16[2,184,384]{2,1,0:T(8,128)(2,1)S(1)} %slice.538), channel_id=1, source_target_pairs={{0,16},{16,24},{24,8},{8,0},{4,20},{20,28},{28,12},{12,4},{1,17},{... | collective-permute-start | bytes 847880 | tf_op jit(solution)/shard_map/ppermute | solution.py:45
  59.9 13.9 %collective-permute-start.13 = (bf16[2,184,384]{2,1,0:T(8,128)(2,1)S(1)}, bf16[2,184,384]{2,1,0:T(8,128)(2,1)S(1)}, u32[]{:S(2)}, u32[]{:S(2)}) collective-permute-start(bf16[2,184,384]{2,1,0:T(8,128)(2,1)S(1)} %slice.539), channel_id=1, source_target_pairs={{16,0},{24,16},{8,24},{0,8},{20,4},{28,20},{12,28},{4,12},{17,1},{... | collective-permute-start | bytes 847880 | tf_op jit(solution)/shard_map/ppermute | solution.py:48
  60.5 16.6 %collective-permute-start.10 = (bf16[184,1408]{1,0:T(8,128)(2,1)S(1)}, bf16[184,1408]{1,0:T(8,128)(2,1)S(1)}, u32[]{:S(2)}, u32[]{:S(2)}) collective-permute-start(bf16[184,1408]{1,0:T(8,128)(2,1)S(1)} %pad_maximum_fusion.13), channel_id=1, source_target_pairs={{0,1},{1,2},{2,3},{3,0},{4,5},{5,6},{6,7},{7,4},{8,9},{9,10},{10,1... | collective-permute-start | bytes 1554440 | tf_op jit(solution)/shard_map/ppermute | solution.py:45
  61.2 20.6 %collective-permute-start.11 = (bf16[184,1408]{1,0:T(8,128)(2,1)S(1)}, bf16[184,1408]{1,0:T(8,128)(2,1)S(1)}, u32[]{:S(2)}, u32[]{:S(2)}) collective-permute-start(bf16[184,1408]{1,0:T(8,128)(2,1)S(1)} %pad_maximum_fusion.13), channel_id=1, source_target_pairs={{1,0},{2,1},{3,2},{0,3},{5,4},{6,5},{7,6},{4,7},{9,8},{10,9},{11,1... | collective-permute-start | bytes 1554440 | tf_op jit(solution)/shard_map/ppermute | solution.py:48
  64.4 17.6 %collective-permute-start.14 = (bf16[4,4,184]{2,1,0:T(4,128)(2,1)S(1)}, bf16[4,4,184]{2,1,0:T(4,128)(2,1)S(1)}, u32[]{:S(2)}, u32[]{:S(2)}) collective-permute-start(bf16[4,4,184]{2,1,0:T(4,128)(2,1)S(1)} %pad_maximum_fusion.21), channel_id=1, source_target_pairs={{0,4},{4,0},{8,12},{12,8},{16,20},{20,16},{24,28},{28,24},{1,5},{5... | collective-permute-start | bytes 17672 | tf_op jit(solution)/shard_map/ppermute | solution.py:870
  83.2 167.6 %all-gather.8.cloned.1.call-start = ((), (), s32[]{:S(2)}) async-start(), calls=%async_computation.5 | async-start | bytes 8902656 | tf_op jit(solution)/shard_map/all_gather | solution.py:940
  105.4 16.8 %collective-permute-start.16 = (bf16[8,256,128]{2,1,0:T(8,128)(2,1)}, bf16[8,256,128]{2,1,0:T(8,128)(2,1)S(1)}, u32[]{:S(2)}, u32[]{:S(2)}) collective-permute-start(bf16[8,256,128]{2,1,0:T(8,128)(2,1)} %get-tuple-element.158), channel_id=1, source_target_pairs={{3,0},{0,1},{1,2},{2,3},{7,4},{4,5},{5,6},{6,7},{11,8},{8,9},{9,10... | collective-permute-start | bytes 1572872 | tf_op jit(solution)/shard_map/ppermute | solution.py:55
  110.1 22.8 %collective-permute-start.17 = (bf16[8,256,128]{2,1,0:T(8,128)(2,1)S(1)}, bf16[8,256,128]{2,1,0:T(8,128)(2,1)S(1)}, u32[]{:S(2)}, u32[]{:S(2)}) collective-permute-start(bf16[8,256,128]{2,1,0:T(8,128)(2,1)S(1)} %get-tuple-element.159), channel_id=1, source_target_pairs={{1,0},{2,1},{3,2},{0,3},{5,4},{6,5},{7,6},{4,7},{9,8},{10,9},{11,1... | collective-permute-start | bytes 1572872 | tf_op jit(solution)/shard_map/ppermute | solution.py:55
  113.5 41.9 %collective-permute-start.18 = (bf16[8,256,128]{2,1,0:T(8,128)(2,1)S(1)}, bf16[8,256,128]{2,1,0:T(8,128)(2,1)S(1)}, u32[]{:S(2)}, u32[]{:S(2)}) collective-permute-start(bf16[8,256,128]{2,1,0:T(8,128)(2,1)S(1)} %get-tuple-element.160), channel_id=1, source_target_pairs={{2,0},{3,1},{0,2},{1,3},{6,4},{7,5},{4,6},{5,7},{10,8},{11,9},{8,1... | collective-permute-start | bytes 1572872 | tf_op jit(solution)/shard_map/ppermute | solution.py:55
  158.5 25.5 %collective-permute-start.22 = (bf16[184,768]{1,0:T(8,128)(2,1)S(1)}, bf16[184,768]{1,0:T(8,128)(2,1)S(1)}, u32[]{:S(2)}, u32[]{:S(2)}) collective-permute-start(bf16[184,768]{1,0:T(8,128)(2,1)S(1)} %slice.575), channel_id=1, source_target_pairs={{1,0},{2,1},{3,2},{0,3},{5,4},{6,5},{7,6},{4,7},{9,8},{10,9},{11,1... | collective-permute-start | bytes 847880 | tf_op jit(solution)/shard_map/ppermute | solution.py:48
  159.7 24.3 %collective-permute-start.19 = (bf16[184,640]{1,0:T(8,128)(2,1)S(1)}, bf16[184,640]{1,0:T(8,128)(2,1)S(1)}, u32[]{:S(2)}, u32[]{:S(2)}) collective-permute-start(bf16[184,640]{1,0:T(8,128)(2,1)S(1)} %slice.572), channel_id=1, source_target_pairs={{0,1},{1,2},{2,3},{3,0},{4,5},{5,6},{6,7},{7,4},{8,9},{9,10},{10,1... | collective-permute-start | bytes 706568 | tf_op jit(solution)/shard_map/ppermute | solution.py:45
  160.6 23.4 %collective-permute-start.20 = (bf16[184,640]{1,0:T(8,128)(2,1)S(1)}, bf16[184,640]{1,0:T(8,128)(2,1)S(1)}, u32[]{:S(2)}, u32[]{:S(2)}) collective-permute-start(bf16[184,640]{1,0:T(8,128)(2,1)S(1)} %slice.573), channel_id=1, source_target_pairs={{1,0},{2,1},{3,2},{0,3},{5,4},{6,5},{7,6},{4,7},{9,8},{10,9},{11,1... | collective-permute-start | bytes 706568 | tf_op jit(solution)/shard_map/ppermute | solution.py:48
  163.5 20.5 %collective-permute-start.21 = (bf16[184,640]{1,0:T(8,128)(2,1)S(1)}, bf16[184,640]{1,0:T(8,128)(2,1)S(1)}, u32[]{:S(2)}, u32[]{:S(2)}) collective-permute-start(bf16[184,640]{1,0:T(8,128)(2,1)S(1)} %slice.574), channel_id=1, source_target_pairs={{0,1},{1,2},{2,3},{3,0},{4,5},{5,6},{6,7},{7,4},{8,9},{9,10},{10,1... | collective-permute-start | bytes 706568 | tf_op jit(solution)/shard_map/ppermute | solution.py:45
  185.1 198.9 %reduce-scatter.6.cloned.1.call-start = ((), (), s32[]{:S(2)}) async-start(), calls=%async_computation.6 | async-start | bytes 11870208 | tf_op jit(solution)/shard_map/reduce_scatter | solution.py:1146
  186.8 13.5 %collective-permute-start.23 = (bf16[2,256,128]{2,1,0:T(8,128)(2,1)S(1)}, bf16[2,256,128]{2,1,0:T(8,128)(2,1)S(1)}, u32[]{:S(2)}, u32[]{:S(2)}) collective-permute-start(bf16[2,256,128]{2,1,0:T(8,128)(2,1)S(1)} %get-tuple-element.170), channel_id=1, source_target_pairs={{3,0},{0,1},{1,2},{2,3},{7,4},{4,5},{5,6},{6,7},{11,8},{8,9},{9,10... | collective-permute-start | bytes 393224 | tf_op jit(solution)/shard_map/ppermute | solution.py:55
  186.8 14.1 %collective-permute-start.24 = (bf16[2,256,128]{2,1,0:T(8,128)(2,1)S(1)}, bf16[2,256,128]{2,1,0:T(8,128)(2,1)S(1)}, u32[]{:S(2)}, u32[]{:S(2)}) collective-permute-start(bf16[2,256,128]{2,1,0:T(8,128)(2,1)S(1)} %get-tuple-element.171), channel_id=1, source_target_pairs={{1,0},{2,1},{3,2},{0,3},{5,4},{6,5},{7,6},{4,7},{9,8},{10,9},{11,1... | collective-permute-start | bytes 393224 | tf_op jit(solution)/shard_map/ppermute | solution.py:55
  199.9 6.2 %collective-permute-start.25 = (bf16[2,256,128]{2,1,0:T(8,128)(2,1)S(1)}, bf16[2,256,128]{2,1,0:T(8,128)(2,1)S(1)}, u32[]{:S(2)}, u32[]{:S(2)}) collective-permute-start(bf16[2,256,128]{2,1,0:T(8,128)(2,1)S(1)} %get-tuple-element.172), channel_id=1, source_target_pairs={{2,0},{3,1},{0,2},{1,3},{6,4},{7,5},{4,6},{5,7},{10,8},{11,9},{8,1... | collective-permute-start | bytes 393224 | tf_op jit(solution)/shard_map/ppermute | solution.py:55
  292.1 230.6 %reduce-scatter.10.cloned.1.call-start = ((), (), s32[]{:S(2)}) async-start(), calls=%async_computation.8 | async-start | bytes 23740416
  364.5 18.5 %collective-permute-start.26 = (bf16[2,256,128]{2,1,0:T(8,128)(2,1)S(1)}, bf16[2,256,128]{2,1,0:T(8,128)(2,1)S(1)}, u32[]{:S(2)}, u32[]{:S(2)}) collective-permute-start(bf16[2,256,128]{2,1,0:T(8,128)(2,1)S(1)} %get-tuple-element.222), channel_id=1, source_target_pairs={{3,0},{0,1},{1,2},{2,3},{7,4},{4,5},{5,6},{6,7},{11,8},{8,9},{9,10... | collective-permute-start | bytes 393224 | tf_op jit(solution)/shard_map/ppermute | solution.py:55
  364.6 18.5 %collective-permute-start.27 = (bf16[2,256,128]{2,1,0:T(8,128)(2,1)S(1)}, bf16[2,256,128]{2,1,0:T(8,128)(2,1)S(1)}, u32[]{:S(2)}, u32[]{:S(2)}) collective-permute-start(bf16[2,256,128]{2,1,0:T(8,128)(2,1)S(1)} %get-tuple-element.223), channel_id=1, source_target_pairs={{1,0},{2,1},{3,2},{0,3},{5,4},{6,5},{7,6},{4,7},{9,8},{10,9},{11,1... | collective-permute-start | bytes 393224 | tf_op jit(solution)/shard_map/ppermute | solution.py:55
  368.4 14.7 %collective-permute-start.28 = (bf16[2,256,128]{2,1,0:T(8,128)(2,1)S(1)}, bf16[2,256,128]{2,1,0:T(8,128)(2,1)S(1)}, u32[]{:S(2)}, u32[]{:S(2)}) collective-permute-start(bf16[2,256,128]{2,1,0:T(8,128)(2,1)S(1)} %get-tuple-element.224), channel_id=1, source_target_pairs={{2,0},{3,1},{0,2},{1,3},{6,4},{7,5},{4,6},{5,7},{10,8},{11,9},{8,1... | collective-permute-start | bytes 393224 | tf_op jit(solution)/shard_map/ppermute | solution.py:55
  385.6 193.5 %reduce-scatter.8.cloned.1.call-start = ((), (), s32[]{:S(2)}) async-start(), calls=%async_computation.7 | async-start | bytes 5087232 | tf_op jit(solution)/shard_map/reduce_scatter | solution.py:1146
  385.6 41.9 %collective-permute-start.29 = (bf16[184,896]{1,0:T(8,128)(2,1)S(1)}, bf16[184,896]{1,0:T(8,128)(2,1)S(1)}, u32[]{:S(2)}, u32[]{:S(2)}) collective-permute-start(bf16[184,896]{1,0:T(8,128)(2,1)S(1)} %get-tuple-element.233), channel_id=1, source_target_pairs={{1,0},{2,1},{3,2},{0,3},{5,4},{6,5},{7,6},{4,7},{9,8},{10,9},{11,1... | collective-permute-start | bytes 989192 | tf_op jit(solution)/shard_map/ppermute | solution.py:55
  386.2 41.4 %collective-permute-start.30 = (bf16[184,896]{1,0:T(8,128)(2,1)S(1)}, bf16[184,896]{1,0:T(8,128)(2,1)S(1)}, u32[]{:S(2)}, u32[]{:S(2)}) collective-permute-start(bf16[184,896]{1,0:T(8,128)(2,1)S(1)} %get-tuple-element.234), channel_id=1, source_target_pairs={{3,0},{0,1},{1,2},{2,3},{7,4},{4,5},{5,6},{6,7},{11,8},{8,9},{9,10... | collective-permute-start | bytes 989192 | tf_op jit(solution)/shard_map/ppermute | solution.py:55
  387.7 39.9 %collective-permute-start.31 = (bf16[184,896]{1,0:T(8,128)(2,1)S(1)}, bf16[184,896]{1,0:T(8,128)(2,1)S(1)}, u32[]{:S(2)}, u32[]{:S(2)}) collective-permute-start(bf16[184,896]{1,0:T(8,128)(2,1)S(1)} %get-tuple-element.235), channel_id=1, source_target_pairs={{2,0},{3,1},{0,2},{1,3},{6,4},{7,5},{4,6},{5,7},{10,8},{11,9},{8,1... | collective-permute-start | bytes 989192 | tf_op jit(solution)/shard_map/ppermute | solution.py:55
  427.6 16.9 %collective-permute-start.32 = (bf16[8,256,128]{2,1,0:T(8,128)(2,1)}, bf16[8,256,128]{2,1,0:T(8,128)(2,1)S(1)}, u32[]{:S(2)}, u32[]{:S(2)}) collective-permute-start(bf16[8,256,128]{2,1,0:T(8,128)(2,1)} %pad_maximum_fusion.11), channel_id=1, source_target_pairs={{3,0},{0,1},{1,2},{2,3},{7,4},{4,5},{5,6},{6,7},{11,8},{8,9},{9,10... | collective-permute-start | bytes 1572872 | tf_op jit(solution)/shard_map/ppermute | solution.py:55
  427.9 24.0 %collective-permute-start.33 = (bf16[8,256,128]{2,1,0:T(8,128)(2,1)}, bf16[8,256,128]{2,1,0:T(8,128)(2,1)S(1)}, u32[]{:S(2)}, u32[]{:S(2)}) collective-permute-start(bf16[8,256,128]{2,1,0:T(8,128)(2,1)} %pad_maximum_fusion.10), channel_id=1, source_target_pairs={{1,0},{2,1},{3,2},{0,3},{5,4},{6,5},{7,6},{4,7},{9,8},{10,9},{11,1... | collective-permute-start | bytes 1572872 | tf_op jit(solution)/shard_map/ppermute | solution.py:55
  431.7 40.3 %collective-permute-start.34 = (bf16[8,256,128]{2,1,0:T(8,128)(2,1)}, bf16[8,256,128]{2,1,0:T(8,128)(2,1)S(1)}, u32[]{:S(2)}, u32[]{:S(2)}) collective-permute-start(bf16[8,256,128]{2,1,0:T(8,128)(2,1)} %pad_maximum_fusion.12), channel_id=1, source_target_pairs={{2,0},{3,1},{0,2},{1,3},{6,4},{7,5},{4,6},{5,7},{10,8},{11,9},{8,1... | collective-permute-start | bytes 1572872 | tf_op jit(solution)/shard_map/ppermute | solution.py:55
  524.4 12.5 %collective-permute-start.40 = (bf16[184,896]{1,0:T(8,128)(2,1)S(1)}, bf16[184,896]{1,0:T(8,128)(2,1)S(1)}, u32[]{:S(2)}, u32[]{:S(2)}) collective-permute-start(bf16[184,896]{1,0:T(8,128)(2,1)S(1)} %get-tuple-element.248), channel_id=1, source_target_pairs={{0,1},{1,2},{2,3},{3,0},{4,5},{5,6},{6,7},{7,4},{8,9},{9,10},{10,1... | collective-permute-start | bytes 989192 | tf_op jit(solution)/shard_map/ppermute | solution.py:45
  525.9 16.2 %collective-permute-start.41 = (bf16[184,896]{1,0:T(8,128)(2,1)S(1)}, bf16[184,896]{1,0:T(8,128)(2,1)S(1)}, u32[]{:S(2)}, u32[]{:S(2)}) collective-permute-start(bf16[184,896]{1,0:T(8,128)(2,1)S(1)} %get-tuple-element.249), channel_id=1, source_target_pairs={{1,0},{2,1},{3,2},{0,3},{5,4},{6,5},{7,6},{4,7},{9,8},{10,9},{11,1... | collective-permute-start | bytes 989192 | tf_op jit(solution)/shard_map/ppermute | solution.py:48
  529.5 19.5 %collective-permute-start.36 = (f32[48,128]{1,0:T(8,128)S(1)}, f32[48,128]{1,0:T(8,128)S(1)}, u32[]{:S(2)}, u32[]{:S(2)}) collective-permute-start(f32[48,128]{1,0:T(8,128)S(1)} %fusion.64), channel_id=1, source_target_pairs={{0,8},{4,12},{8,0},{12,4},{16,24},{20,28},{24,16},{28,20},{1,9},{5... | collective-permute-start | bytes 73736 | tf_op jit(solution)/shard_map/ppermute | solution.py:79
  545.2 40.3 %collective-permute-start.42 = (bf16[184,1792]{1,0:T(8,128)(2,1)}, bf16[184,1792]{1,0:T(8,128)(2,1)}, u32[]{:S(2)}, u32[]{:S(2)}) collective-permute-start(bf16[184,1792]{1,0:T(8,128)(2,1)} %pad_maximum_fusion.7), channel_id=1, source_target_pairs={{0,1},{1,2},{2,3},{3,0},{4,5},{5,6},{6,7},{7,4},{8,9},{9,10},{10,1... | collective-permute-start | bytes 1978376 | tf_op jit(solution)/shard_map/ppermute | solution.py:45
  546.4 39.1 %collective-permute-start.43 = (bf16[184,1792]{1,0:T(8,128)(2,1)}, bf16[184,1792]{1,0:T(8,128)(2,1)}, u32[]{:S(2)}, u32[]{:S(2)}) collective-permute-start(bf16[184,1792]{1,0:T(8,128)(2,1)} %pad_maximum_fusion.8), channel_id=1, source_target_pairs={{1,0},{2,1},{3,2},{0,3},{5,4},{6,5},{7,6},{4,7},{9,8},{10,9},{11,1... | collective-permute-start | bytes 1978376 | tf_op jit(solution)/shard_map/ppermute | solution.py:48
  549.0 7.9 %collective-permute-start.37 = (f32[48,128]{1,0:T(8,128)S(1)}, f32[48,128]{1,0:T(8,128)S(1)}, u32[]{:S(2)}, u32[]{:S(2)}) collective-permute-start(f32[48,128]{1,0:T(8,128)S(1)} %fusion.71), channel_id=1, source_target_pairs={{0,16},{4,20},{8,24},{12,28},{16,0},{20,4},{24,8},{28,12},{1,17},{... | collective-permute-start | bytes 73736 | tf_op jit(solution)/shard_map/ppermute | solution.py:79
  556.9 22.2 %collective-permute-start.38 = (f32[48,128]{1,0:T(8,128)S(1)}, f32[48,128]{1,0:T(8,128)S(1)}, u32[]{:S(2)}, u32[]{:S(2)}) collective-permute-start(f32[48,128]{1,0:T(8,128)S(1)} %add.530), channel_id=1, source_target_pairs={{0,1},{1,0},{2,3},{3,2},{4,5},{5,4},{6,7},{7,6},{8,9},{9,8},{10,11... | collective-permute-start | bytes 73736 | tf_op jit(solution)/shard_map/ppermute | solution.py:79
  585.5 7.8 %collective-permute-start.44 = (bf16[184,384]{1,0:T(8,128)(2,1)S(1)}, bf16[184,384]{1,0:T(8,128)(2,1)S(1)}, u32[]{:S(2)}, u32[]{:S(2)}) collective-permute-start(bf16[184,384]{1,0:T(8,128)(2,1)S(1)} %get-tuple-element.252), channel_id=1, source_target_pairs={{1,0},{2,1},{3,2},{0,3},{5,4},{6,5},{7,6},{4,7},{9,8},{10,9},{11,1... | collective-permute-start | bytes 423944 | tf_op jit(solution)/shard_map/ppermute | solution.py:55
  589.1 7.9 %collective-permute-start.45 = (bf16[184,384]{1,0:T(8,128)(2,1)S(1)}, bf16[184,384]{1,0:T(8,128)(2,1)S(1)}, u32[]{:S(2)}, u32[]{:S(2)}) collective-permute-start(bf16[184,384]{1,0:T(8,128)(2,1)S(1)} %get-tuple-element.253), channel_id=1, source_target_pairs={{3,0},{0,1},{1,2},{2,3},{7,4},{4,5},{5,6},{6,7},{11,8},{8,9},{9,10... | collective-permute-start | bytes 423944 | tf_op jit(solution)/shard_map/ppermute | solution.py:55
  589.1 11.5 %collective-permute-start.46 = (bf16[184,384]{1,0:T(8,128)(2,1)S(1)}, bf16[184,384]{1,0:T(8,128)(2,1)S(1)}, u32[]{:S(2)}, u32[]{:S(2)}) collective-permute-start(bf16[184,384]{1,0:T(8,128)(2,1)S(1)} %get-tuple-element.254), channel_id=1, source_target_pairs={{2,0},{3,1},{0,2},{1,3},{6,4},{7,5},{4,6},{5,7},{10,8},{11,9},{8,1... | collective-permute-start | bytes 423944 | tf_op jit(solution)/shard_map/ppermute | solution.py:55
  (45 other events, 247.8 us)
Sparse Core Ops, SparseCore 0:
  11.0 65.7 all-gather.3
  83.4 85.6 all-gather.5
  185.3 53.8 all-gather.7
  292.2 81.5 reduce-scatter.5
  385.7 137.0 reduce-scatter.9
  526.1 52.9 reduce-scatter.7
where the time goes:
time: 620 us; the launch traced here: 610 us
  Pallas kernels  270 us (44%)
  waiting for transfers between devices  174 us (28%)
  starting transfers between devices  67.1 us (11%)
  local copies, waits for them, and re-layouts  51.7 us (8%)
  other arithmetic  27.2 us (4%)
  between operations  18.6 us (3%)
    ppermute x24, waiting for transfers between devices, shift(): return lax.ppermute(value, self.axis, pairs)  109 us
    pallas_call x3, Pallas kernels, ffn_call(): pl.pallas_call(functools.partial(kernel, widths, numbers, len(kept)), gri...  91.5 us
    pallas_call x6, Pallas kernels, row_call(): pl.pallas_call(kernel, grid_spec=pltpu.PrefetchScalarGridSpec(num_scalar_...  60.6 us
    pallas_call x4, Pallas kernels, weight_grad(): pl.pallas_call(functools.partial(weight_grad_kernel, len(lefts), part, ar...  56.3 us
    pallas_call x2, Pallas kernels, attention(): pl.pallas_call(functools.partial(kernel, tile), grid_spec=pltpu.PrefetchS...  49.5 us
    ppermute x24, starting transfers between devices, shift(): return lax.ppermute(value, self.axis, pairs)  36.5 us
    unnamed x7, waiting for transfers between devices  18.4 us
    unnamed x110, local copies, waits for them, and re-layouts  18.2 us
  transfers between devices with their start and end apart: 53, of which 24 were waited for; matrix products, arithmetic and copies ran while one was open for 11% of the time, Pallas kernels for 38%

commit v1 on v0

--- a/solution.py
+++ b/solution.py
@@ -239,8 +239,13 @@
 
 
 def ffn_forward_kernel(widths, numbers, kept, mid_ref, in_ref, *refs):
+    ends = len(refs) - len(widths) - kept > 7
+    if ends:
+        gate_ins, refs = refs[:3], refs[3:]
     groups, rest = refs[: len(widths)], refs[len(widths) + kept :]
-    to_gate_ref, to_up_ref, act_ref, out_ref, mats, total, sems = rest
+    to_gate_ref, to_up_ref, act_ref = rest[:3]
+    mats, total, sems = rest[-3:]
+    out_refs = rest[3:-3]
     slot = stream_chunks(widths, numbers, groups, mats, sems, (0, 1, 2))
     chunk, tile = pl.program_id(0), pl.program_id(1)
     rows = mid_ref.shape[0]
@@ -271,7 +276,10 @@
 
     @pl.when(chunk == pl.num_programs(0) - 1)
     def _():
-        out_ref[...] = total[span]
+        if ends:
+            gate_step(tile, total[span], *gate_ins, *out_refs)
+        else:
+            out_refs[0][...] = total[span]
 
 
 def ffn_backward_kernel(widths, numbers, kept, grad_ref, to_gate_ref, to_up_ref, *refs):
@@ -316,7 +324,7 @@
     return width
 
 
-def ffn_call(forward, args, groups, hidden_units, numbers=None, kept=()):
+def ffn_call(forward, args, groups, hidden_units, numbers=None, kept=(), gate=None):
     tokens, width = args[0].shape
     widths = [group.shape[1] // 3 for group in groups]
     columns = chunk_of(hidden_units)
@@ -335,13 +343,30 @@
     else:
         kernel, specs = ffn_backward_kernel, [each, chunked, chunked]
         outs = [jax.ShapeDtypeStruct(stack, BF)] * 2
+    ends, end_specs = [jax.ShapeDtypeStruct((tokens, width), F32)], [last]
+    if gate is not None:
+        args = (*args, *gate)
+        column = pl.BlockSpec((tile, 1), lambda d, i: (jnp.where(d == count - 1, i, 0), 0))
+        turned = pl.BlockSpec((width, tile), lambda d, i: (0, jnp.where(d == count - 1, i, 0)))
+        specs = specs + [last, column, pl.BlockSpec(gate[2].shape, lambda d, i: (0, 0))]
+        ends = [
+            jax.ShapeDtypeStruct((tokens, width), BF),
+            jax.ShapeDtypeStruct((tokens, 1), F32),
+            jax.ShapeDtypeStruct((tokens, width), F32),
+            jax.ShapeDtypeStruct((tokens, width), BF),
+            jax.ShapeDtypeStruct((width, tokens), BF),
+            jax.ShapeDtypeStruct((2, width), F32),
+        ]
+        end_specs = [
+            last, column, last, last, turned, pl.BlockSpec((2, width), lambda d, i: (0, 0))
+        ]
     first_kept = len(args) + len(groups)
     return pl.pallas_call(
         functools.partial(kernel, widths, numbers, len(kept)),
         grid=(count, tiles),
-        out_shape=outs + [jax.ShapeDtypeStruct((tokens, width), F32)],
+        out_shape=outs + ends,
         in_specs=specs + [ANYWHERE] * (len(groups) + len(kept)),
-        out_specs=[chunked] * len(outs) + [last],
+        out_specs=[chunked] * len(outs) + end_specs,
         scratch_shapes=[
             pltpu.VMEM((2, 3, width, columns), BF),
             pltpu.VMEM((tokens, width), F32),
@@ -481,6 +506,18 @@
         ref[row : row + 1, :] = ref[row : row + 1, :] + total
 
 
+def upright_kernel(in_ref, out_ref):
+    out_ref[...] = in_ref[0, 0].astype(F32).T.astype(BF)
+
+
+def upright(value, micro_count, rows):
+    width = value.shape[2]
+    return row_call(
+        upright_kernel, "upright", micro_count, rows, [(value, "micro")],
+        [((micro_count * rows, width), BF, "rows")],
+    )[0]
+
+
 def project_kernel(shape, unit, seq, index_ref, z_ref, in_ref, gain_ref, *refs):
     part, columns, chips, groups, cores = shape
     pieces, refs = refs[:cores], refs[cores:]
@@ -531,7 +568,7 @@
     mixed = jnp.concatenate([ref[0] for ref in mixed_refs], axis=1)
     wide = spread({3: mixed}, unit, seq, mixed.shape[0])
     spread_ref[...] = wide
-    hidden = in_ref[0, 0].astype(F32) + lax.dot_general(
+    hidden = in_ref[...].astype(F32) + lax.dot_general(
         wide, weight_ref[...], NT, preferred_element_type=F32
     )
     hidden_ref[...] = hidden
@@ -540,11 +577,9 @@
     turned_ref[...] = mid.T.astype(BF)
 
 
-def gate_kernel(out_ref, grad_ref, grad_gate_ref, gain_ref, act_ref, mask_ref, grad_y_ref, low_ref,
-                turned_ref, sums_ref):
-    step = pl.program_id(0)
-    output = out_ref[...]
-    act_ref[0, 0] = output.astype(BF)
+def gate_step(step, output, grad_ref, grad_gate_ref, gain_ref, act_ref, mask_ref, grad_y_ref,
+              low_ref, turned_ref, sums_ref):
+    act_ref[...] = output.astype(BF)
     gain, weight = gain_ref[2:3, :], gain_ref[3:4, :]
     scale = row_scale(output)
     unit_value = output * scale
@@ -553,7 +588,7 @@
     mask_ref[...] = DELETE_SCALE * gate
     slope = grad_gate_ref[...] * DELETE_SCALE * (gate * (1.0 - gate))
     width = output.shape[1]
-    grad_y = grad_ref[0, 0].astype(F32) + (scale * slope) * (
+    grad_y = grad_ref[...].astype(F32) + (scale * slope) * (
         gain * weight - unit_value * (logit / width)
     )
     grad_y_ref[...] = grad_y
@@ -589,8 +624,8 @@
 def in_kernel(weight_ref, spread_ref, in_ref, grad_hidden_ref, gain_ref, grad_x_ref, sums_ref):
     step = pl.program_id(0)
     grad_in = lax.dot_general(spread_ref[...], weight_ref[...], NT, preferred_element_type=F32)
-    back, moved = scale_backward(in_ref[0, 0].astype(F32), gain_ref[0:1, :], grad_in)
-    grad_x_ref[0, 0] = (grad_hidden_ref[...] + back).astype(BF)
+    back, moved = scale_backward(in_ref[...].astype(F32), gain_ref[0:1, :], grad_in)
+    grad_x_ref[...] = (grad_hidden_ref[...] + back).astype(BF)
     add_rows(step, sums_ref, 0, moved)
 
 
@@ -998,12 +1033,16 @@
 
     ff_groups = [over_fsdp(ff_block)]
     bias = flow.slot([attn], lambda vectors: bias_tiles(vectors, rows), vectors)
-    flow.slot([attn, gain_chain, ff_left])
-    flow.slot([attn, gain_chain, ff_right])
+    x_turned, grad_turned = (jnp.swapaxes(v, 2, 3) for v in (layer_input, grad_out))
+    table, unit_entry = flow.slot(
+        [attn, gain_chain, ff_left], lambda *tables: tables, table, unit_entry
+    )
     seg = ready["seg"].reshape(seq, -1)[:, :tokens].reshape(seq, micro_count, rows)
     seg = seg.astype(jnp.int32).transpose(1, 0, 2)
-    key_seg, query_seg = seg.reshape(micro_count, 1, seq * rows), seg[:, :, :, None]
-
+    key_seg, query_seg = flow.slot(
+        [attn, gain_chain, ff_right], lambda *segs: segs,
+        seg.reshape(micro_count, 1, seq * rows), seg[:, :, :, None],
+    )
     turned_shape = ((width, tokens), BF, "columns")
     if aligned:
         project_shape, z_places = (part, 4 * unit, chips, seq, 2), z_index
@@ -1031,7 +1070,7 @@
     sent, tied = {}, {}
     near = [group_of((-step, step)) for step in range(1, seq // 2)] if seq == 4 else []
     in_turned, qkv, attn_weight = flow.slot(
-        [attn, gain_chain], project_rest, jnp.swapaxes(layer_input, 2, 3), near
+        [attn, gain_chain], project_rest, x_turned, near
     )
     ff_groups += [over_fsdp(group) for group in tied["near"]]
     gains = ready["gains"]
@@ -1040,7 +1079,11 @@
         rest = qkv[whole_count:, 1:].reshape(2 * rest_count, rows, LANES)
         return jnp.concatenate([whole, rest])
 
-    flow.slot([Chain(exchange(ring_z, z_offsets, qkv_to, lambda found: sent.update(qkv=found)))])
+    x_rows, grad_rows = flow.slot(
+        [Chain(exchange(ring_z, z_offsets, qkv_to, lambda found: sent.update(qkv=found)))],
+        lambda *values: [upright(value, micro_count, rows) for value in values],
+        x_turned, grad_turned,
+    )
     blocks = sent["qkv"]
     queries = jnp.concatenate(
         [jnp.stack([block[3 * i] for block in blocks]) for i in range(whole_each)]
@@ -1079,7 +1122,7 @@
         [],
         lambda mixed: row_call(
             functools.partial(out_kernel, unit, seq, pairs), "out", micro_count, rows,
-            [(attn_weight, "whole"), (layer_input, "micro"), (gains, "whole")]
+            [(attn_weight, "whole"), (x_rows, "rows"), (gains, "whole")]
             + [(mixed, pair) for pair in range(pairs)],
             [((tokens, 4 * heads_width), BF, "rows"), ((tokens, width), F32, "rows"),
              ((tokens, width), BF, "rows"), turned_shape],
@@ -1087,6 +1130,7 @@
         ),
         mixed,
     )
+    gate_args = (grad_rows, grad_gate.reshape(tokens, 1), gains)
     hidden_units = seq * ff_part
     columns = chunk_of(hidden_units)
     if ff_part % LANES == 0:
@@ -1098,11 +1142,11 @@
             ),
             normed_mid, hidden,
         )
-        to_gate, to_up, act, output = flow.slot(
+        to_gate, to_up, act, *ends = flow.slot(
             [],
             lambda mid, output, *factors: ffn_call(
                 True, (mid, output), ff_groups, hidden_units,
-                range(early, hidden_units // columns), factors,
+                range(early, hidden_units // columns), factors, gate_args,
             ),
             normed_mid, output, *factors,
         )
@@ -1115,22 +1159,13 @@
             ],
             axis=1,
         )]
-        to_gate, to_up, act, output = flow.slot(
-            [], lambda *args: ffn_call(True, args, ff_groups, hidden_units), normed_mid, hidden
+        to_gate, to_up, act, *ends = flow.slot(
+            [],
+            lambda *args: ffn_call(True, args, ff_groups, hidden_units, gate=gate_args),
+            normed_mid, hidden,
         )
 
-    activations, gate_mask, grad_y, grad_y_low, y_turned, gate_sums = flow.slot(
-        [],
-        lambda output: row_call(
-            gate_kernel, "gate", micro_count, rows,
-            [(output, "rows"), (grad_out, "micro"), (grad_gate.reshape(tokens, 1), "rows"),
-             (gains, "whole")],
-            [(layer_input.shape, BF, "micro"), ((tokens, 1), F32, "rows"),
-             ((tokens, width), F32, "rows"), ((tokens, width), BF, "rows"), turned_shape,
-             ((2, width), F32, "whole")],
-        ),
-        output,
-    )
+    activations, gate_mask, grad_y, grad_y_low, y_turned, gate_sums = ends
     ff_grad = {}
 
     def over_z_back(name, value):
@@ -1150,10 +1185,19 @@
     grad_gate_pre, grad_up_pre, grad_mid = flow.slot(
         [], lambda *args: ffn_call(False, args, ff_groups, hidden_units), grad_y_low, to_gate, to_up
     )
-    def mid_step(grad_mid, hidden, grad_y, mid_turned, grad_up_pre):
+    def pair_step(mid_turned, grad_gate_pre, grad_up_pre):
+        half_full = weight_grad(
+            (mid_turned,), (grad_up_pre,), within=(2 * hidden_units, hidden_units, None)
+        )
         return weight_grad(
-            (mid_turned,), (grad_up_pre,), within=(2 * hidden_units, hidden_units, None)
-        ), row_call(
+            (mid_turned,), (grad_gate_pre,), within=(2 * hidden_units, 0, half_full)
+        )
+
+    pair_full = flow.slot([], pair_step, mid_turned, grad_gate_pre, grad_up_pre)
+
+    def mid_step(pair_full, grad_mid, hidden, grad_y):
+        tied["pair"] = pair_full
+        return row_call(
             functools.partial(mid_kernel, unit, seq), "mid", micro_count, rows,
             [(attn_weight, "whole"), (grad_mid, "rows"), (hidden, "rows"), (grad_y, "rows"),
              (gains, "whole")],
@@ -1162,33 +1206,29 @@
             (), 8 * tokens * width * heads_width,
         )
 
-    half_full, (grad_hidden, hidden_turned, grad_mixed, mid_sums) = flow.slot(
-        [], mid_step, grad_mid, hidden, grad_y, mid_turned, grad_up_pre
-    )
-    pair_full = flow.slot(
+    grad_hidden, hidden_turned, grad_mixed, mid_sums = flow.slot(
+        [], mid_step, pair_full, grad_mid, hidden, grad_y
+    )
+    flow.slot(
         [Chain(exchange(
             ring_z, z_offsets, functools.partial(whole_of, grad_mixed),
             lambda found: sent.update(grad=found),
         ))],
-        lambda mid_turned, grad_gate_pre, base: weight_grad(
-            (mid_turned,), (grad_gate_pre,), within=(2 * hidden_units, 0, base)
-        ),
-        mid_turned, grad_gate_pre, half_full,
-    )
+        lambda pair_full: tied.update(pair=pair_full), tied["pair"],
+    )
+    grad_pair_mat = scattered(tied["pair"])
     grad_steps = jnp.concatenate(
         [jnp.stack([block[i] for block in sent["grad"]]) for i in range(whole_each)]
         + [grad_mixed[whole_count:]]
     )
     down_back = over_z_back("down", grad_down)
 
-    def attention_step(pair_full, query, grads, logs, keys, values):
-        tied["pair"] = pair_full
+    def attention_step(query, grads, logs, keys, values):
         return attention(True, table, query, (grads, logs), keys, values, query_seg, key_seg, bias)
 
     grad_q, grad_kv, sums = flow.slot(
-        [down_back], attention_step, pair_full, queries, grad_steps, log_sums, keys, values
-    )
-    grad_pair_mat = scattered(tied["pair"])
+        [down_back], attention_step, queries, grad_steps, log_sums, keys, values
+    )
     kv_blocks = grad_kv.reshape(whole_each + rest_count, 2, seq, rows, LANES)
 
     def grads_to(offset):
@@ -1235,9 +1275,9 @@
         tied["attn"] = attn_full
         return row_call(
             in_kernel, "in", micro_count, rows,
-            [(attn_weight, "whole"), (grad_spread, "rows"), (layer_input, "micro"),
+            [(attn_weight, "whole"), (grad_spread, "rows"), (x_rows, "rows"),
              (grad_hidden, "rows"), (gains, "whole")],
-            [(layer_input.shape, BF, "micro"), ((1, width), F32, "whole")],
+            [((tokens, width), BF, "rows"), ((1, width), F32, "whole")],
             (), 8 * tokens * width * heads_width,
         )
 
@@ -1292,9 +1332,9 @@
     attn_grad = attn_grad[0]
 
     return (
-        activations,
+        activations.reshape(layer_input.shape),
         gate_mask.reshape(micro_count, 1, rows),
-        grad_x,
+        grad_x.reshape(layer_input.shape),
         gains_part[0],
         attn_grad[:, :unit],
         attn_grad[:, unit : 2 * unit],

time: 620 us -> 599 us (0.966)
  waiting for transfers between devices: 174 us -> 156 us
    unnamed x7, waiting for transfers between devices: 18.4 us -> 0.12 us
    pallas_call x3, Pallas kernels: 91.5 us -> 98.2 us  [ffn_call(): pl.pallas_call(functools.partial(kernel, widths, numbers, len(kept)), gri...]
    unnamed x110 -> x108, local copies, waits for them, and re-layouts: 18.2 us -> 12.9 us
    pallas_call x6 -> x7, Pallas kernels: 60.6 us -> 58.7 us  [row_call(): pl.pallas_call(kernel, grid_spec=pltpu.PrefetchScalarGridSpec(num_scalar_...]
  transfers between devices with their start and end apart: 53 -> 53, of which waited for: 24 -> 25; matrix products, arithmetic and copies ran while one was open for 11% -> 11% of each run, Pallas kernels for 38% -> 41%
where the time goes in v1:
time: 599 us; the launch traced here: 588 us
  Pallas kernels  276 us (46%)
  waiting for transfers between devices  156 us (26%)
  starting transfers between devices  61.8 us (10%)
  local copies, waits for them, and re-layouts  46.9 us (8%)
  other arithmetic  28.9 us (5%)
  between operations  18.6 us (3%)
    ppermute x24, waiting for transfers between devices, shift(): return lax.ppermute(value, self.axis, pairs)  113 us
    pallas_call x3, Pallas kernels, ffn_call(): pl.pallas_call(functools.partial(kernel, widths, numbers, len(kept)), gri...  98.2 us
    pallas_call x7, Pallas kernels, row_call(): pl.pallas_call(kernel, grid_spec=pltpu.PrefetchScalarGridSpec(num_scalar_...  58.7 us
    pallas_call x4, Pallas kernels, weight_grad(): pl.pallas_call(functools.partial(weight_grad_kernel, len(lefts), part, ar...  56.5 us
    pallas_call x2, Pallas kernels, attention(): pl.pallas_call(functools.partial(kernel, tile), grid_spec=pltpu.PrefetchS...  49.8 us
    ppermute x24, starting transfers between devices, shift(): return lax.ppermute(value, self.axis, pairs)  33 us
    ppermute x8, starting transfers between devices, left(): return lax.ppermute(value, self.axis, self.back)  20 us
    ppermute x8, waiting for transfers between devices, right(): return lax.ppermute(value, self.axis, self.onward)  15.4 us
  transfers between devices with their start and end apart: 53, of which 25 were waited for; matrix products, arithmetic and copies ran while one was open for 11% of the time, Pallas kernels for 41%

profile of v1, /device:TPU:0, one launch (start us, length us, event | category | flops | bytes accessed | tf_op | source)
XLA Modules:
  0.0 588.5 jit_solution(2067829210565529161)
XLA Ops:
  12.8 3.1 collective-permute-start
  24.1 5.6 bias.1.bias_ref
  36.9 2.9 collective-permute-start.4
  41.3 15.2 %collective-permute-done.8 = bf16[4,184]{1,0:T(4,128)(2,1)S(1)} collective-permute-done((bf16[4,184]{1,0:T(4,128)(2,1)S(1)}, bf16[4,184]{1,0:T(4,128)(2,1)S(1)}, u32[]{:S(2)}, u32[]{:S(2)}) %collective-permute-start.8) | collective-permute-done | bytes 1504 | tf_op jit(solution)/shard_map/ppermute | solution.py:55
  57.1 3.9 collective-permute-done.9
  63.4 3.8 collective-permute-start.11
  67.3 7.6 %collective-permute-done.12 = bf16[2,184,384]{2,1,0:T(8,128)(2,1)S(1)} collective-permute-done((bf16[2,184,384]{2,1,0:T(8,128)(2,1)S(1)}, bf16[2,184,384]{2,1,0:T(8,128)(2,1)S(1)}, u32[]{:S(2)}, u32[]{:S(2)}) %collective-permute-start.12) | collective-permute-done | bytes 282656 | tf_op jit(solution)/shard_map/ppermute | solution.py:45
  76.0 2.8 pad_maximum_fusion.refs_0_
  79.4 4.7 collective-permute-done.11
  90.4 11.2 %project.1 = (bf16[1472,768]{1,0:T(8,128)(2,1)}, bf16[9,3,256,128]{3,2,1,0:T(8,128)(2,1)}, bf16[1472,1536]{1,0:T(8,128)(2,1)}) custom-call(s32[8]{0:T(128)} %copy-done.39, s32[4]{0:T(128)} %copy-done.2, bf16[3,1,1472,256]{3,2,1,0:T(8,128)(2,1)} %bitcast.212, f32[1472,4]{1,0:T(8,128)} %bitcast.234, bf16[4,4,184,384]{3,2,1,0:T(8,128)(2,1)} %pad_maximum_fusion.refs_0_, ...), custom_call_target="tpu_custom_call" | custom-call | flops 3472883712 | bytes 13613152 | tf_op jit(solution)/shard_map/project/pallas_call | solution.py:651
  109.8 2.6 collective-permute-start.17
  113.7 4.3 upright.2.in_ref
  118.0 4.3 upright.3.refs_0_
  122.3 10.0 %collective-permute-done.17 = bf16[8,256,128]{2,1,0:T(8,128)(2,1)S(1)} collective-permute-done((bf16[8,256,128]{2,1,0:T(8,128)(2,1)S(1)}, bf16[8,256,128]{2,1,0:T(8,128)(2,1)S(1)}, u32[]{:S(2)}, u32[]{:S(2)}) %collective-permute-start.17) | collective-permute-done | bytes 524320 | tf_op jit(solution)/shard_map/ppermute | solution.py:55
  132.4 22.5 %collective-permute-done.18 = bf16[8,256,128]{2,1,0:T(8,128)(2,1)S(1)} collective-permute-done((bf16[8,256,128]{2,1,0:T(8,128)(2,1)S(1)}, bf16[8,256,128]{2,1,0:T(8,128)(2,1)S(1)}, u32[]{:S(2)}, u32[]{:S(2)}) %collective-permute-start.18) | collective-permute-done | bytes 524320 | tf_op jit(solution)/shard_map/ppermute | solution.py:55
  160.1 3.0 collective-permute-start.20
  163.1 18.7 %attention_forward.1 = (bf16[9,256,128]{2,1,0:T(8,128)(2,1)}, f32[9,256,2]{2,1,0:T(8,128)}) custom-call(s32[9,10]{1,0:T(8,128)} %concatenate.137.table_ref, bf16[9,256,128]{2,1,0:T(8,128)(2,1)} %copy-done.28, bf16[3,1024,128]{2,1,0:T(8,128)(2,1)} %pad_maximum_fusion.5.key_ref, bf16[3,1024,128]{2,1,0:T(8,128)(2,1)} %pad_maximum_fusion.6.value_ref, ...), custom_call_target="tpu_custom_call" | custom-call | flops 4831838208 | bytes 18874368 | tf_op jit(solution)/shard_map/attention_forward/pallas_call | solution.py:853
  184.1 4.0 collective-permute-start.24
  192.4 5.9 collective-permute-done.25
  199.9 10.3 %out.1 = (bf16[768,1536]{1,0:T(8,128)(2,1)}, f32[768,1472]{1,0:T(8,128)}, bf16[768,1472]{1,0:T(8,128)(2,1)}, bf16[1472,768]{1,0:T(8,128)(2,1)}) custom-call(s32[9]{0:T(128)} %compare_select_fusion.11.table_ref, bf16[1472,1536]{1,0:T(8,128)(2,1)} %get-tuple-element.162.weight_ref, bf16[768,1472]{1,0:T(8,128)(2,1)} %upright.2.in_ref, ...), custom_call_target="tpu_custom_call" | custom-call | flops 3472883712 | bytes 17152000 | tf_op jit(solution)/shard_map/out/pallas_call | solution.py:651
  210.2 32.9 %ffn_forward.2 = (f32[768,3584]{1,0:T(8,128)}, f32[768,3584]{1,0:T(8,128)}, bf16[768,3584]{1,0:T(8,128)(2,1)}, f32[768,1472]{1,0:T(8,128)}) custom-call(bf16[768,1472]{1,0:T(8,128)(2,1)} %get-tuple-element.194.mid_ref, f32[768,1472]{1,0:T(8,128)} %get-tuple-element.221.in_ref.hidden_ref, bf16[1472,2688]{1,0:T(8,128)(2,1)} %all-gather.4.cloned.1.call-done.refs_0_.refs_3_, ...), custom_call_target="tpu_custom_call" | custom-call | flops 17364418560 | bytes 53575680 | tf_op jit(solution)/shard_map/ffn_forward/pallas_call | solution.py:364
  243.2 22.5 %ffn_forward.3 = (f32[768,3584]{1,0:T(8,128)}, f32[768,3584]{1,0:T(8,128)}, bf16[768,3584]{1,0:T(8,128)(2,1)}, bf16[768,1472]{1,0:T(8,128)(2,1)}, f32[768,1]{1,0...) custom-call(bf16[768,1472]{1,0:T(8,128)(2,1)} %get-tuple-element.194, ...), custom_call_target="tpu_custom_call", output_to_operand_aliasing={{0}: (8, {}), {1}: (9, {}), {2}: (10, {})} | custom-call | flops 6945767424 | bytes 28213248 | tf_op jit(solution)/shard_map/ffn_forward/pallas_call | solution.py:364
  265.7 14.5 %weight_grad.4 = bf16[1472,3584]{1,0:T(8,128)(2,1)} custom-call(s32[1]{0:T(128)} %constant.216.clone.1.index_ref, bf16[1472,768]{1,0:T(8,128)(2,1)} %get-tuple-element.209.refs_0_, bf16[768,3584]{1,0:T(8,128)(2,1)} %get-tuple-element.210.refs_1_), custom_call_target="tpu_custom_call" | custom-call | flops 8103395328 | bytes 28868608 | tf_op jit(solution)/shard_map/weight_grad/pallas_call | solution.py:443
  280.5 42.8 %ffn_backward.1 = (bf16[768,3584]{1,0:T(8,128)(2,1)}, bf16[768,3584]{1,0:T(8,128)(2,1)}, f32[768,1472]{1,0:T(8,128)}) custom-call(bf16[768,1472]{1,0:T(8,128)(2,1)} %get-tuple-element.211.grad_ref, f32[768,3584]{1,0:T(8,128)} %get-tuple-element.212.to_gate_ref, f32[768,3584]{1,0:T(8,128)} %get-tuple-element.213.to_up_ref, ...), custom_call_target="tpu_custom_call" | custom-call | flops 24310185984 | bytes 70483968 | tf_op jit(solution)/shard_map/ffn_backward/pallas_call | solution.py:364
  323.3 14.5 %weight_grad.5.refs_2_ = bf16[1472,7168]{1,0:T(8,128)(2,1)} custom-call(s32[1]{0:T(128)} %constant.216.clone.1.index_ref, bf16[1472,768]{1,0:T(8,128)(2,1)} %get-tuple-element.217.refs_0_, bf16[768,3584]{1,0:T(8,128)(2,1)} %get-tuple-element.219.refs_1_), custom_call_target="tpu_custom_call" | custom-call | flops 8103395328 | bytes 28868608 | tf_op jit(solution)/shard_map/weight_grad/pallas_call | solution.py:443
  337.8 14.6 %weight_grad.6 = bf16[1472,7168]{1,0:T(8,128)(2,1)} custom-call(s32[1]{0:T(128)} %constant.216.clone.1.index_ref, bf16[1472,768]{1,0:T(8,128)(2,1)} %get-tuple-element.217.refs_0_, bf16[768,3584]{1,0:T(8,128)(2,1)} %get-tuple-element.218.refs_1_, bf16[1472,7168]{1,0:T(8,128)(2,1)} %weight_grad.5.refs_2_), custom_call_target="tpu_custom_call", output_to_operand_aliasing={{}: (3, {})} | custom-call | flops 8103395328 | bytes 28868608 | tf_op jit(solution)/shard_map/weight_grad/pallas_call | solution.py:443
  352.4 13.3 %mid.1 = (f32[768,1472]{1,0:T(8,128)}, bf16[1472,768]{1,0:T(8,128)(2,1)}, bf16[9,256,128]{2,1,0:T(8,128)(2,1)}, f32[1,1472]{1,0:T(1,128)}) custom-call(bf16[1472,1536]{1,0:T(8,128)(2,1)} %get-tuple-element.162.weight_ref, f32[768,1472]{1,0:T(8,128)} %get-tuple-element.220.grad_mid_ref, f32[768,1472]{1,0:T(8,128)} %get-tuple-element.221.in_ref.hidden_ref, ...), custom_call_target="tpu_custom_call" | custom-call | flops 3472883712 | bytes 36222976 | tf_op jit(solution)/shard_map/mid/pallas_call | solution.py:651
  367.0 3.8 collective-permute-start.27
  370.8 4.4 collective-permute-done.26
  375.2 5.0 collective-permute-done.28
  385.0 31.1 %attention_backward.1 = (bf16[9,256,128]{2,1,0:T(8,128)(2,1)}, bf16[3,2,1024,128]{3,2,1,0:T(8,128)(2,1)}, f32[6,5,256,256]{3,2,1,0:T(8,128)}) custom-call(s32[9,10]{1,0:T(8,128)} %concatenate.137.table_ref, bf16[9,256,128]{2,1,0:T(8,128)(2,1)} %copy-done.28, bf16[9,256,128]{2,1,0:T(8,128)(2,1)} %copy-done.29, f32[9,256,2]{2,1,0:T(8,128)} %get-tuple-element.233.log_ref, ...), custom_call_target="tpu_custom_call" | custom-call | flops 12079595520 | bytes 18874368 | tf_op jit(solution)/shard_map/attention_backward/pallas_call | solution.py:853
  422.3 3.7 collective-permute-start.32
  428.7 7.1 %diagonals.1 = f32[6,5,512]{2,1,0:T(8,128)} custom-call(f32[6,5,256,256]{3,2,1,0:T(8,128)} %get-tuple-element.245.scores_ref), custom_call_target="tpu_custom_call" | custom-call | tf_op jit(solution)/shard_map/diagonals/pallas_call | solution.py:709
  435.8 3.5 collective-permute-done.32
  439.3 10.7 %collective-permute-done.33 = bf16[8,256,128]{2,1,0:T(8,128)(2,1)S(1)} collective-permute-done((bf16[8,256,128]{2,1,0:T(8,128)(2,1)}, bf16[8,256,128]{2,1,0:T(8,128)(2,1)S(1)}, u32[]{:S(2)}, u32[]{:S(2)}) %collective-permute-start.33) | collective-permute-done | bytes 524320 | tf_op jit(solution)/shard_map/ppermute | solution.py:55
  450.1 20.8 %collective-permute-done.34 = bf16[8,256,128]{2,1,0:T(8,128)(2,1)S(1)} collective-permute-done((bf16[8,256,128]{2,1,0:T(8,128)(2,1)}, bf16[8,256,128]{2,1,0:T(8,128)(2,1)S(1)}, u32[]{:S(2)}, u32[]{:S(2)}) %collective-permute-start.34) | collective-permute-done | bytes 524320 | tf_op jit(solution)/shard_map/ppermute | solution.py:55
  473.4 5.0 spread.1.refs_2_.spread_ref
  478.4 12.9 %weight_grad.7 = bf16[1472,1536]{1,0:T(8,128)(2,1)} custom-call(s32[1]{0:T(128)} %constant.216.clone.1.index_ref, bf16[1472,768]{1,0:T(8,128)(2,1)} %get-tuple-element.164.refs_0_, bf16[1472,768]{1,0:T(8,128)(2,1)} %get-tuple-element.223.refs_1_, bf16[768,1536]{1,0:T(8,128)(2,1)} %spread.1.refs_2_.spread_ref, bf16[768,1536]{1,0:T(8,128)(2,1)} %get-tuple-element.185.refs_3_), custom_call_target="tpu_custom_call" | custom-call | flops 6945767424 | bytes 18284544 | tf_op jit(solution)/shard_map/weight_grad/pallas_call | solution.py:443
  492.6 10.3 %in.1 = (bf16[768,1472]{1,0:T(8,128)(2,1)}, f32[1,1472]{1,0:T(1,128)}) custom-call(bf16[1472,1536]{1,0:T(8,128)(2,1)} %get-tuple-element.162.weight_ref, bf16[768,1536]{1,0:T(8,128)(2,1)} %spread.1.refs_2_.spread_ref, bf16[768,1472]{1,0:T(8,128)(2,1)} %upright.2.in_ref, f32[768,1472]{1,0:T(8,128)} %get-tuple-element.248.grad_hidden_ref, ...), custom_call_target="tpu_custom_call" | custom-call | flops 3472883712 | bytes 27375616 | tf_op jit(solution)/shard_map/in/pallas_call | solution.py:651
  505.5 3.8 collective-permute-start.41
  510.8 7.1 %collective-permute-done.40 = bf16[184,896]{1,0:T(8,128)(2,1)S(1)} collective-permute-done((bf16[184,896]{1,0:T(8,128)(2,1)S(1)}, bf16[184,896]{1,0:T(8,128)(2,1)S(1)}, u32[]{:S(2)}, u32[]{:S(2)}) %collective-permute-start.40) | collective-permute-done | bytes 329760 | tf_op jit(solution)/shard_map/ppermute | solution.py:45
  517.9 4.3 collective-permute-done.41
  525.5 3.5 collective-permute-start.43
  539.4 4.2 copy.83
  543.7 14.2 %reduce-scatter.8.cloned.1.call-done = bf16[184,1536]{1,0:T(8,128)(2,1)} async-done(((bf16[1472,1536]{1,0:T(8,128)(2,1)}), bf16[184,1536]{1,0:T(8,128)(2,1)}) %reduce-scatter.8.cloned.1.call-update) | async-done | bytes 565264 | tf_op jit(solution)/shard_map/reduce_scatter | solution.py:1181
  564.3 3.5 collective-permute-start.44
  572.1 3.7 collective-permute-done.45
  575.8 3.6 collective-permute-done.46
  (344 shorter events, 102.1 us)
Async XLA Ops:
  7.2 203.0 %all-gather.4.cloned.1.call-start = ((), (), s32[]{:S(2)}) async-start(), calls=%async_computation.3 | async-start | bytes 8902656 | tf_op jit(solution)/shard_map/all_gather | solution.py:975
  10.8 199.4 %all-gather.6.cloned.1.call-start = ((), (), s32[]{:S(2)}) async-start(), calls=%async_computation.4 | async-start | bytes 17805312 | tf_op jit(solution)/shard_map/all_gather | solution.py:975
  12.8 17.8 %collective-permute-start = (bf16[192,384]{1,0:T(8,128)(2,1)S(1)}, bf16[192,384]{1,0:T(8,128)(2,1)S(1)}, u32[]{:S(2)}, u32[]{:S(2)}) collective-permute-start(bf16[192,384]{1,0:T(8,128)(2,1)S(1)} %pad_maximum_fusion.20), channel_id=1, source_target_pairs={{3,0},{0,1},{1,2},{2,3},{7,4},{4,5},{5,6},{6,7},{11,8},{8,9},{9,10... | collective-permute-start | bytes 442376 | tf_op jit(solution)/shard_map/ppermute | solution.py:55
  15.9 14.7 %collective-permute-start.1 = (bf16[192,384]{1,0:T(8,128)(2,1)S(1)}, bf16[192,384]{1,0:T(8,128)(2,1)S(1)}, u32[]{:S(2)}, u32[]{:S(2)}) collective-permute-start(bf16[192,384]{1,0:T(8,128)(2,1)S(1)} %pad_maximum_fusion.20), channel_id=1, source_target_pairs={{1,0},{2,1},{3,2},{0,3},{5,4},{6,5},{7,6},{4,7},{9,8},{10,9},{11,1... | collective-permute-start | bytes 442376 | tf_op jit(solution)/shard_map/ppermute | solution.py:55
  18.0 13.3 %collective-permute-start.2 = (bf16[192,384]{1,0:T(8,128)(2,1)S(1)}, bf16[192,384]{1,0:T(8,128)(2,1)S(1)}, u32[]{:S(2)}, u32[]{:S(2)}) collective-permute-start(bf16[192,384]{1,0:T(8,128)(2,1)S(1)} %pad_maximum_fusion.20), channel_id=1, source_target_pairs={{2,0},{3,1},{0,2},{1,3},{6,4},{7,5},{4,6},{5,7},{10,8},{11,9},{8,1... | collective-permute-start | bytes 442376 | tf_op jit(solution)/shard_map/ppermute | solution.py:55
  32.4 8.2 %collective-permute-start.7 = (bf16[4,184]{1,0:T(4,128)(2,1)S(1)}, bf16[4,184]{1,0:T(4,128)(2,1)S(1)}, u32[]{:S(2)}, u32[]{:S(2)}) collective-permute-start(bf16[4,184]{1,0:T(4,128)(2,1)S(1)} %pad_maximum_fusion.22), channel_id=1, source_target_pairs={{8,0},{0,16},{16,24},{24,8},{12,4},{4,20},{20,28},{28,12},{9,1},{1... | collective-permute-start | bytes 4424 | tf_op jit(solution)/shard_map/ppermute | solution.py:55
  34.0 27.1 %collective-permute-start.5 = (bf16[4,184,384]{2,1,0:T(8,128)(2,1)}, bf16[4,184,384]{2,1,0:T(8,128)(2,1)S(1)}, u32[]{:S(2)}, u32[]{:S(2)}) collective-permute-start(bf16[4,184,384]{2,1,0:T(8,128)(2,1)} %get-tuple-element.147), channel_id=1, source_target_pairs={{0,16},{16,24},{24,8},{8,0},{4,20},{20,28},{28,12},{12,4},{1,17},{... | collective-permute-start | bytes 1695752 | tf_op jit(solution)/shard_map/ppermute | solution.py:45
  35.5 25.7 %collective-permute-start.6 = (bf16[4,184,384]{2,1,0:T(8,128)(2,1)}, bf16[4,184,384]{2,1,0:T(8,128)(2,1)S(1)}, u32[]{:S(2)}, u32[]{:S(2)}) collective-permute-start(bf16[4,184,384]{2,1,0:T(8,128)(2,1)} %get-tuple-element.147), channel_id=1, source_target_pairs={{16,0},{24,16},{8,24},{0,8},{20,4},{28,20},{12,28},{4,12},{17,1},{... | collective-permute-start | bytes 1695752 | tf_op jit(solution)/shard_map/ppermute | solution.py:48
  36.0 25.2 %collective-permute-start.3 = (bf16[184,1280]{1,0:T(8,128)(2,1)}, bf16[184,1280]{1,0:T(8,128)(2,1)S(1)}, u32[]{:S(2)}, u32[]{:S(2)}) collective-permute-start(bf16[184,1280]{1,0:T(8,128)(2,1)} %pad_maximum_fusion.14), channel_id=1, source_target_pairs={{0,1},{1,2},{2,3},{3,0},{4,5},{5,6},{6,7},{7,4},{8,9},{9,10},{10,1... | collective-permute-start | bytes 1413128 | tf_op jit(solution)/shard_map/ppermute | solution.py:45
  36.9 24.3 %collective-permute-start.4 = (bf16[184,1280]{1,0:T(8,128)(2,1)}, bf16[184,1280]{1,0:T(8,128)(2,1)S(1)}, u32[]{:S(2)}, u32[]{:S(2)}) collective-permute-start(bf16[184,1280]{1,0:T(8,128)(2,1)} %pad_maximum_fusion.14), channel_id=1, source_target_pairs={{1,0},{2,1},{3,2},{0,3},{5,4},{6,5},{7,6},{4,7},{9,8},{10,9},{11,1... | collective-permute-start | bytes 1413128 | tf_op jit(solution)/shard_map/ppermute | solution.py:48
  40.7 15.8 %collective-permute-start.8 = (bf16[4,184]{1,0:T(4,128)(2,1)S(1)}, bf16[4,184]{1,0:T(4,128)(2,1)S(1)}, u32[]{:S(2)}, u32[]{:S(2)}) collective-permute-start(bf16[4,184]{1,0:T(4,128)(2,1)S(1)} %pad_maximum_fusion.22), channel_id=1, source_target_pairs={{16,0},{24,16},{8,24},{0,8},{20,4},{28,20},{12,28},{4,12},{17,1},{... | collective-permute-start | bytes 4424 | tf_op jit(solution)/shard_map/ppermute | solution.py:55
  61.2 13.7 %collective-permute-start.12 = (bf16[2,184,384]{2,1,0:T(8,128)(2,1)S(1)}, bf16[2,184,384]{2,1,0:T(8,128)(2,1)S(1)}, u32[]{:S(2)}, u32[]{:S(2)}) collective-permute-start(bf16[2,184,384]{2,1,0:T(8,128)(2,1)S(1)} %slice.539), channel_id=1, source_target_pairs={{0,16},{16,24},{24,8},{8,0},{4,20},{20,28},{28,12},{12,4},{1,17},{... | collective-permute-start | bytes 847880 | tf_op jit(solution)/shard_map/ppermute | solution.py:45
  62.1 13.8 %collective-permute-start.13 = (bf16[2,184,384]{2,1,0:T(8,128)(2,1)S(1)}, bf16[2,184,384]{2,1,0:T(8,128)(2,1)S(1)}, u32[]{:S(2)}, u32[]{:S(2)}) collective-permute-start(bf16[2,184,384]{2,1,0:T(8,128)(2,1)S(1)} %slice.540), channel_id=1, source_target_pairs={{16,0},{24,16},{8,24},{0,8},{20,4},{28,20},{12,28},{4,12},{17,1},{... | collective-permute-start | bytes 847880 | tf_op jit(solution)/shard_map/ppermute | solution.py:48
  63.3 16.1 %collective-permute-start.10 = (bf16[184,1408]{1,0:T(8,128)(2,1)}, bf16[184,1408]{1,0:T(8,128)(2,1)S(1)}, u32[]{:S(2)}, u32[]{:S(2)}) collective-permute-start(bf16[184,1408]{1,0:T(8,128)(2,1)} %pad_maximum_fusion.13), channel_id=1, source_target_pairs={{0,1},{1,2},{2,3},{3,0},{4,5},{5,6},{6,7},{7,4},{8,9},{9,10},{10,1... | collective-permute-start | bytes 1554440 | tf_op jit(solution)/shard_map/ppermute | solution.py:45
  63.4 20.7 %collective-permute-start.11 = (bf16[184,1408]{1,0:T(8,128)(2,1)}, bf16[184,1408]{1,0:T(8,128)(2,1)S(1)}, u32[]{:S(2)}, u32[]{:S(2)}) collective-permute-start(bf16[184,1408]{1,0:T(8,128)(2,1)} %pad_maximum_fusion.13), channel_id=1, source_target_pairs={{1,0},{2,1},{3,2},{0,3},{5,4},{6,5},{7,6},{4,7},{9,8},{10,9},{11,1... | collective-permute-start | bytes 1554440 | tf_op jit(solution)/shard_map/ppermute | solution.py:48
  67.2 17.0 %collective-permute-start.14 = (bf16[4,4,184]{2,1,0:T(4,128)(2,1)S(1)}, bf16[4,4,184]{2,1,0:T(4,128)(2,1)S(1)}, u32[]{:S(2)}, u32[]{:S(2)}) collective-permute-start(bf16[4,4,184]{2,1,0:T(4,128)(2,1)S(1)} %pad_maximum_fusion.21), channel_id=1, source_target_pairs={{0,4},{4,0},{8,12},{12,8},{16,20},{20,16},{24,28},{28,24},{1,5},{5... | collective-permute-start | bytes 17672 | tf_op jit(solution)/shard_map/ppermute | solution.py:905
  85.6 157.6 %all-gather.8.cloned.1.call-start = ((), (), s32[]{:S(2)}) async-start(), calls=%async_computation.5 | async-start | bytes 8902656 | tf_op jit(solution)/shard_map/all_gather | solution.py:975
  105.1 17.2 %collective-permute-start.16 = (bf16[8,256,128]{2,1,0:T(8,128)(2,1)}, bf16[8,256,128]{2,1,0:T(8,128)(2,1)S(1)}, u32[]{:S(2)}, u32[]{:S(2)}) collective-permute-start(bf16[8,256,128]{2,1,0:T(8,128)(2,1)} %get-tuple-element.166), channel_id=1, source_target_pairs={{3,0},{0,1},{1,2},{2,3},{7,4},{4,5},{5,6},{6,7},{11,8},{8,9},{9,10... | collective-permute-start | bytes 1572872 | tf_op jit(solution)/shard_map/ppermute | solution.py:55
  109.8 22.6 %collective-permute-start.17 = (bf16[8,256,128]{2,1,0:T(8,128)(2,1)S(1)}, bf16[8,256,128]{2,1,0:T(8,128)(2,1)S(1)}, u32[]{:S(2)}, u32[]{:S(2)}) collective-permute-start(bf16[8,256,128]{2,1,0:T(8,128)(2,1)S(1)} %get-tuple-element.167), channel_id=1, source_target_pairs={{1,0},{2,1},{3,2},{0,3},{5,4},{6,5},{7,6},{4,7},{9,8},{10,9},{11,1... | collective-permute-start | bytes 1572872 | tf_op jit(solution)/shard_map/ppermute | solution.py:55
  113.3 41.6 %collective-permute-start.18 = (bf16[8,256,128]{2,1,0:T(8,128)(2,1)S(1)}, bf16[8,256,128]{2,1,0:T(8,128)(2,1)S(1)}, u32[]{:S(2)}, u32[]{:S(2)}) collective-permute-start(bf16[8,256,128]{2,1,0:T(8,128)(2,1)S(1)} %get-tuple-element.168), channel_id=1, source_target_pairs={{2,0},{3,1},{0,2},{1,3},{6,4},{7,5},{4,6},{5,7},{10,8},{11,9},{8,1... | collective-permute-start | bytes 1572872 | tf_op jit(solution)/shard_map/ppermute | solution.py:55
  158.0 24.9 %collective-permute-start.22 = (bf16[184,768]{1,0:T(8,128)(2,1)S(1)}, bf16[184,768]{1,0:T(8,128)(2,1)S(1)}, u32[]{:S(2)}, u32[]{:S(2)}) collective-permute-start(bf16[184,768]{1,0:T(8,128)(2,1)S(1)} %slice.576), channel_id=1, source_target_pairs={{1,0},{2,1},{3,2},{0,3},{5,4},{6,5},{7,6},{4,7},{9,8},{10,9},{11,1... | collective-permute-start | bytes 847880 | tf_op jit(solution)/shard_map/ppermute | solution.py:48
  159.2 23.7 %collective-permute-start.19 = (bf16[184,640]{1,0:T(8,128)(2,1)S(1)}, bf16[184,640]{1,0:T(8,128)(2,1)S(1)}, u32[]{:S(2)}, u32[]{:S(2)}) collective-permute-start(bf16[184,640]{1,0:T(8,128)(2,1)S(1)} %copy-done.19), channel_id=1, source_target_pairs={{0,1},{1,2},{2,3},{3,0},{4,5},{5,6},{6,7},{7,4},{8,9},{9,10},{10,1... | collective-permute-start | bytes 706568 | tf_op jit(solution)/shard_map/ppermute | solution.py:45
  160.1 22.8 %collective-permute-start.20 = (bf16[184,640]{1,0:T(8,128)(2,1)S(1)}, bf16[184,640]{1,0:T(8,128)(2,1)S(1)}, u32[]{:S(2)}, u32[]{:S(2)}) collective-permute-start(bf16[184,640]{1,0:T(8,128)(2,1)S(1)} %slice.574), channel_id=1, source_target_pairs={{1,0},{2,1},{3,2},{0,3},{5,4},{6,5},{7,6},{4,7},{9,8},{10,9},{11,1... | collective-permute-start | bytes 706568 | tf_op jit(solution)/shard_map/ppermute | solution.py:48
  163.1 19.9 %collective-permute-start.21 = (bf16[184,640]{1,0:T(8,128)(2,1)S(1)}, bf16[184,640]{1,0:T(8,128)(2,1)S(1)}, u32[]{:S(2)}, u32[]{:S(2)}) collective-permute-start(bf16[184,640]{1,0:T(8,128)(2,1)S(1)} %slice.575), channel_id=1, source_target_pairs={{0,1},{1,2},{2,3},{3,0},{4,5},{5,6},{6,7},{7,4},{8,9},{9,10},{10,1... | collective-permute-start | bytes 706568 | tf_op jit(solution)/shard_map/ppermute | solution.py:45
  184.0 197.3 %reduce-scatter.6.cloned.1.call-start = ((), (), s32[]{:S(2)}) async-start(), calls=%async_computation.6 | async-start | bytes 11870208 | tf_op jit(solution)/shard_map/reduce_scatter | solution.py:1181
  184.0 8.3 %collective-permute-start.23 = (bf16[2,256,128]{2,1,0:T(8,128)(2,1)S(1)}, bf16[2,256,128]{2,1,0:T(8,128)(2,1)S(1)}, u32[]{:S(2)}, u32[]{:S(2)}) collective-permute-start(bf16[2,256,128]{2,1,0:T(8,128)(2,1)S(1)} %get-tuple-element.179), channel_id=1, source_target_pairs={{3,0},{0,1},{1,2},{2,3},{7,4},{4,5},{5,6},{6,7},{11,8},{8,9},{9,10... | collective-permute-start | bytes 393224 | tf_op jit(solution)/shard_map/ppermute | solution.py:55
  184.1 8.2 %collective-permute-start.24 = (bf16[2,256,128]{2,1,0:T(8,128)(2,1)S(1)}, bf16[2,256,128]{2,1,0:T(8,128)(2,1)S(1)}, u32[]{:S(2)}, u32[]{:S(2)}) collective-permute-start(bf16[2,256,128]{2,1,0:T(8,128)(2,1)S(1)} %get-tuple-element.180), channel_id=1, source_target_pairs={{1,0},{2,1},{3,2},{0,3},{5,4},{6,5},{7,6},{4,7},{9,8},{10,9},{11,1... | collective-permute-start | bytes 393224 | tf_op jit(solution)/shard_map/ppermute | solution.py:55
  189.8 8.4 %collective-permute-start.25 = (bf16[2,256,128]{2,1,0:T(8,128)(2,1)S(1)}, bf16[2,256,128]{2,1,0:T(8,128)(2,1)S(1)}, u32[]{:S(2)}, u32[]{:S(2)}) collective-permute-start(bf16[2,256,128]{2,1,0:T(8,128)(2,1)S(1)} %get-tuple-element.181), channel_id=1, source_target_pairs={{2,0},{3,1},{0,2},{1,3},{6,4},{7,5},{4,6},{5,7},{10,8},{11,9},{8,1... | collective-permute-start | bytes 393224 | tf_op jit(solution)/shard_map/ppermute | solution.py:55
  280.3 223.5 %reduce-scatter.10.cloned.1.call-start = ((), (), s32[]{:S(2)}) async-start(), calls=%async_computation.8 | async-start | bytes 23740416
  366.9 191.1 %reduce-scatter.8.cloned.1.call-start = ((), (), s32[]{:S(2)}) async-start(), calls=%async_computation.7 | async-start | bytes 5087232 | tf_op jit(solution)/shard_map/reduce_scatter | solution.py:1181
  366.9 8.3 %collective-permute-start.26 = (bf16[2,256,128]{2,1,0:T(8,128)(2,1)S(1)}, bf16[2,256,128]{2,1,0:T(8,128)(2,1)S(1)}, u32[]{:S(2)}, u32[]{:S(2)}) collective-permute-start(bf16[2,256,128]{2,1,0:T(8,128)(2,1)S(1)} %get-tuple-element.228), channel_id=1, source_target_pairs={{3,0},{0,1},{1,2},{2,3},{7,4},{4,5},{5,6},{6,7},{11,8},{8,9},{9,10... | collective-permute-start | bytes 393224 | tf_op jit(solution)/shard_map/ppermute | solution.py:55
  367.0 8.2 %collective-permute-start.27 = (bf16[2,256,128]{2,1,0:T(8,128)(2,1)S(1)}, bf16[2,256,128]{2,1,0:T(8,128)(2,1)S(1)}, u32[]{:S(2)}, u32[]{:S(2)}) collective-permute-start(bf16[2,256,128]{2,1,0:T(8,128)(2,1)S(1)} %get-tuple-element.229), channel_id=1, source_target_pairs={{1,0},{2,1},{3,2},{0,3},{5,4},{6,5},{7,6},{4,7},{9,8},{10,9},{11,1... | collective-permute-start | bytes 393224 | tf_op jit(solution)/shard_map/ppermute | solution.py:55
  370.8 9.5 %collective-permute-start.28 = (bf16[2,256,128]{2,1,0:T(8,128)(2,1)S(1)}, bf16[2,256,128]{2,1,0:T(8,128)(2,1)S(1)}, u32[]{:S(2)}, u32[]{:S(2)}) collective-permute-start(bf16[2,256,128]{2,1,0:T(8,128)(2,1)S(1)} %get-tuple-element.230), channel_id=1, source_target_pairs={{2,0},{3,1},{0,2},{1,3},{6,4},{7,5},{4,6},{5,7},{10,8},{11,9},{8,1... | collective-permute-start | bytes 393224 | tf_op jit(solution)/shard_map/ppermute | solution.py:55
  382.9 39.4 %collective-permute-start.29 = (bf16[184,896]{1,0:T(8,128)(2,1)S(1)}, bf16[184,896]{1,0:T(8,128)(2,1)S(1)}, u32[]{:S(2)}, u32[]{:S(2)}) collective-permute-start(bf16[184,896]{1,0:T(8,128)(2,1)S(1)} %get-tuple-element.239), channel_id=1, source_target_pairs={{1,0},{2,1},{3,2},{0,3},{5,4},{6,5},{7,6},{4,7},{9,8},{10,9},{11,1... | collective-permute-start | bytes 989192 | tf_op jit(solution)/shard_map/ppermute | solution.py:55
  384.3 38.0 %collective-permute-start.30 = (bf16[184,896]{1,0:T(8,128)(2,1)S(1)}, bf16[184,896]{1,0:T(8,128)(2,1)S(1)}, u32[]{:S(2)}, u32[]{:S(2)}) collective-permute-start(bf16[184,896]{1,0:T(8,128)(2,1)S(1)} %get-tuple-element.240), channel_id=1, source_target_pairs={{3,0},{0,1},{1,2},{2,3},{7,4},{4,5},{5,6},{6,7},{11,8},{8,9},{9,10... | collective-permute-start | bytes 989192 | tf_op jit(solution)/shard_map/ppermute | solution.py:55
  385.0 37.3 %collective-permute-start.31 = (bf16[184,896]{1,0:T(8,128)(2,1)S(1)}, bf16[184,896]{1,0:T(8,128)(2,1)S(1)}, u32[]{:S(2)}, u32[]{:S(2)}) collective-permute-start(bf16[184,896]{1,0:T(8,128)(2,1)S(1)} %get-tuple-element.241), channel_id=1, source_target_pairs={{2,0},{3,1},{0,2},{1,3},{6,4},{7,5},{4,6},{5,7},{10,8},{11,9},{8,1... | collective-permute-start | bytes 989192 | tf_op jit(solution)/shard_map/ppermute | solution.py:55
  422.3 17.0 %collective-permute-start.32 = (bf16[8,256,128]{2,1,0:T(8,128)(2,1)}, bf16[8,256,128]{2,1,0:T(8,128)(2,1)S(1)}, u32[]{:S(2)}, u32[]{:S(2)}) collective-permute-start(bf16[8,256,128]{2,1,0:T(8,128)(2,1)} %pad_maximum_fusion.11), channel_id=1, source_target_pairs={{3,0},{0,1},{1,2},{2,3},{7,4},{4,5},{5,6},{6,7},{11,8},{8,9},{9,10... | collective-permute-start | bytes 1572872 | tf_op jit(solution)/shard_map/ppermute | solution.py:55
  426.0 24.0 %collective-permute-start.33 = (bf16[8,256,128]{2,1,0:T(8,128)(2,1)}, bf16[8,256,128]{2,1,0:T(8,128)(2,1)S(1)}, u32[]{:S(2)}, u32[]{:S(2)}) collective-permute-start(bf16[8,256,128]{2,1,0:T(8,128)(2,1)} %pad_maximum_fusion.10), channel_id=1, source_target_pairs={{1,0},{2,1},{3,2},{0,3},{5,4},{6,5},{7,6},{4,7},{9,8},{10,9},{11,1... | collective-permute-start | bytes 1572872 | tf_op jit(solution)/shard_map/ppermute | solution.py:55
  426.4 44.5 %collective-permute-start.34 = (bf16[8,256,128]{2,1,0:T(8,128)(2,1)}, bf16[8,256,128]{2,1,0:T(8,128)(2,1)S(1)}, u32[]{:S(2)}, u32[]{:S(2)}) collective-permute-start(bf16[8,256,128]{2,1,0:T(8,128)(2,1)} %pad_maximum_fusion.12), channel_id=1, source_target_pairs={{2,0},{3,1},{0,2},{1,3},{6,4},{7,5},{4,6},{5,7},{10,8},{11,9},{8,1... | collective-permute-start | bytes 1572872 | tf_op jit(solution)/shard_map/ppermute | solution.py:55
  505.4 12.5 %collective-permute-start.40 = (bf16[184,896]{1,0:T(8,128)(2,1)S(1)}, bf16[184,896]{1,0:T(8,128)(2,1)S(1)}, u32[]{:S(2)}, u32[]{:S(2)}) collective-permute-start(bf16[184,896]{1,0:T(8,128)(2,1)S(1)} %get-tuple-element.254), channel_id=1, source_target_pairs={{0,1},{1,2},{2,3},{3,0},{4,5},{5,6},{6,7},{7,4},{8,9},{9,10},{10,1... | collective-permute-start | bytes 989192 | tf_op jit(solution)/shard_map/ppermute | solution.py:45
  505.5 16.7 %collective-permute-start.41 = (bf16[184,896]{1,0:T(8,128)(2,1)S(1)}, bf16[184,896]{1,0:T(8,128)(2,1)S(1)}, u32[]{:S(2)}, u32[]{:S(2)}) collective-permute-start(bf16[184,896]{1,0:T(8,128)(2,1)S(1)} %get-tuple-element.255), channel_id=1, source_target_pairs={{1,0},{2,1},{3,2},{0,3},{5,4},{6,5},{7,6},{4,7},{9,8},{10,9},{11,1... | collective-permute-start | bytes 989192 | tf_op jit(solution)/shard_map/ppermute | solution.py:48
  510.5 18.5 %collective-permute-start.36 = (f32[48,128]{1,0:T(8,128)S(1)}, f32[48,128]{1,0:T(8,128)S(1)}, u32[]{:S(2)}, u32[]{:S(2)}) collective-permute-start(f32[48,128]{1,0:T(8,128)S(1)} %fusion.66), channel_id=1, source_target_pairs={{0,8},{4,12},{8,0},{12,4},{16,24},{20,28},{24,16},{28,20},{1,9},{5... | collective-permute-start | bytes 73736 | tf_op jit(solution)/shard_map/ppermute | solution.py:79
  525.2 39.1 %collective-permute-start.42 = (bf16[184,1792]{1,0:T(8,128)(2,1)}, bf16[184,1792]{1,0:T(8,128)(2,1)}, u32[]{:S(2)}, u32[]{:S(2)}) collective-permute-start(bf16[184,1792]{1,0:T(8,128)(2,1)} %pad_maximum_fusion.7), channel_id=1, source_target_pairs={{0,1},{1,2},{2,3},{3,0},{4,5},{5,6},{6,7},{7,4},{8,9},{9,10},{10,1... | collective-permute-start | bytes 1978376 | tf_op jit(solution)/shard_map/ppermute | solution.py:45
  525.5 38.8 %collective-permute-start.43 = (bf16[184,1792]{1,0:T(8,128)(2,1)}, bf16[184,1792]{1,0:T(8,128)(2,1)}, u32[]{:S(2)}, u32[]{:S(2)}) collective-permute-start(bf16[184,1792]{1,0:T(8,128)(2,1)} %pad_maximum_fusion.8), channel_id=1, source_target_pairs={{1,0},{2,1},{3,2},{0,3},{5,4},{6,5},{7,6},{4,7},{9,8},{10,9},{11,1... | collective-permute-start | bytes 1978376 | tf_op jit(solution)/shard_map/ppermute | solution.py:48
  529.0 8.1 %collective-permute-start.37 = (f32[48,128]{1,0:T(8,128)S(1)}, f32[48,128]{1,0:T(8,128)S(1)}, u32[]{:S(2)}, u32[]{:S(2)}) collective-permute-start(f32[48,128]{1,0:T(8,128)S(1)} %fusion.73), channel_id=1, source_target_pairs={{0,16},{4,20},{8,24},{12,28},{16,0},{20,4},{24,8},{28,12},{1,17},{... | collective-permute-start | bytes 73736 | tf_op jit(solution)/shard_map/ppermute | solution.py:79
  537.1 20.8 %collective-permute-start.38 = (f32[48,128]{1,0:T(8,128)S(1)}, f32[48,128]{1,0:T(8,128)S(1)}, u32[]{:S(2)}, u32[]{:S(2)}) collective-permute-start(f32[48,128]{1,0:T(8,128)S(1)} %add.530), channel_id=1, source_target_pairs={{0,1},{1,0},{2,3},{3,2},{4,5},{5,4},{6,7},{7,6},{8,9},{9,8},{10,11... | collective-permute-start | bytes 73736 | tf_op jit(solution)/shard_map/ppermute | solution.py:79
  567.9 7.9 %collective-permute-start.45 = (bf16[184,384]{1,0:T(8,128)(2,1)S(1)}, bf16[184,384]{1,0:T(8,128)(2,1)S(1)}, u32[]{:S(2)}, u32[]{:S(2)}) collective-permute-start(bf16[184,384]{1,0:T(8,128)(2,1)S(1)} %get-tuple-element.259), channel_id=1, source_target_pairs={{3,0},{0,1},{1,2},{2,3},{7,4},{4,5},{5,6},{6,7},{11,8},{8,9},{9,10... | collective-permute-start | bytes 423944 | tf_op jit(solution)/shard_map/ppermute | solution.py:55
  567.9 11.5 %collective-permute-start.46 = (bf16[184,384]{1,0:T(8,128)(2,1)S(1)}, bf16[184,384]{1,0:T(8,128)(2,1)S(1)}, u32[]{:S(2)}, u32[]{:S(2)}) collective-permute-start(bf16[184,384]{1,0:T(8,128)(2,1)S(1)} %get-tuple-element.260), channel_id=1, source_target_pairs={{2,0},{3,1},{0,2},{1,3},{6,4},{7,5},{4,6},{5,7},{10,8},{11,9},{8,1... | collective-permute-start | bytes 423944 | tf_op jit(solution)/shard_map/ppermute | solution.py:55
  (45 other events, 265.4 us)
Sparse Core Ops, SparseCore 0:
  11.0 68.1 all-gather.3
  85.7 84.6 all-gather.5
  184.1 52.8 all-gather.7
  280.4 79.3 reduce-scatter.5
  367.0 134.5 reduce-scatter.9
  504.9 52.9 reduce-scatter.7

commit v2 on v1

--- a/solution.py
+++ b/solution.py
@@ -1317,7 +1317,13 @@
         },
         lambda value: (value[:, :ff_part], value[:, ff_part:]), 1, pair_finish,
     ))
-    flow.slot([pair_back, sum_chain], lambda: sum_chain.run())
+    flow.slot([pair_back, sum_chain])
+
+    def sum_rest():
+        sum_chain.run()
+        return summed[0]
+
+    flow.slot([pair_back, sum_chain], sum_rest)
     flow.finish(pair_back)
     attn_grad = []
     by_offset = {

time: 599 us -> 599 us (level)
  no operation moved by 1% of the time
where the time goes in v2:
time: 599 us; the launch traced here: 589 us
  Pallas kernels  276 us (46%)
  waiting for transfers between devices  156 us (26%)
  starting transfers between devices  61.8 us (10%)
  local copies, waits for them, and re-layouts  46.9 us (8%)
  other arithmetic  28.9 us (5%)
  between operations  18.6 us (3%)
    ppermute x24, waiting for transfers between devices, shift(): return lax.ppermute(value, self.axis, pairs)  113 us
    pallas_call x3, Pallas kernels, ffn_call(): pl.pallas_call(functools.partial(kernel, widths, numbers, len(kept)), gri...  98.2 us
    pallas_call x7, Pallas kernels, row_call(): pl.pallas_call(kernel, grid_spec=pltpu.PrefetchScalarGridSpec(num_scalar_...  58.7 us
    pallas_call x4, Pallas kernels, weight_grad(): pl.pallas_call(functools.partial(weight_grad_kernel, len(lefts), part, ar...  56.5 us
    pallas_call x2, Pallas kernels, attention(): pl.pallas_call(functools.partial(kernel, tile), grid_spec=pltpu.PrefetchS...  49.8 us
    ppermute x24, starting transfers between devices, shift(): return lax.ppermute(value, self.axis, pairs)  33 us
    ppermute x8, starting transfers between devices, left(): return lax.ppermute(value, self.axis, self.back)  19.1 us
    ppermute x8, waiting for transfers between devices, right(): return lax.ppermute(value, self.axis, self.onward)  15.6 us
  transfers between devices with their start and end apart: 53, of which 25 were waited for; matrix products, arithmetic and copies ran while one was open for 11% of the time, Pallas kernels for 41%

profile of v2, /device:TPU:0, one launch (start us, length us, event | category | flops | bytes accessed | tf_op | source)
XLA Modules:
  0.0 588.7 jit_solution(5502033907011741575)
XLA Ops:
  12.8 3.1 collective-permute-start
  24.1 5.6 bias.1.bias_ref
  36.9 2.9 collective-permute-start.4
  41.3 15.2 %collective-permute-done.8 = bf16[4,184]{1,0:T(4,128)(2,1)S(1)} collective-permute-done((bf16[4,184]{1,0:T(4,128)(2,1)S(1)}, bf16[4,184]{1,0:T(4,128)(2,1)S(1)}, u32[]{:S(2)}, u32[]{:S(2)}) %collective-permute-start.8) | collective-permute-done | bytes 1504 | tf_op jit(solution)/shard_map/ppermute | solution.py:55
  57.1 3.9 collective-permute-done.9
  63.4 3.8 collective-permute-start.11
  67.3 7.6 %collective-permute-done.12 = bf16[2,184,384]{2,1,0:T(8,128)(2,1)S(1)} collective-permute-done((bf16[2,184,384]{2,1,0:T(8,128)(2,1)S(1)}, bf16[2,184,384]{2,1,0:T(8,128)(2,1)S(1)}, u32[]{:S(2)}, u32[]{:S(2)}) %collective-permute-start.12) | collective-permute-done | bytes 282656 | tf_op jit(solution)/shard_map/ppermute | solution.py:45
  76.0 2.8 pad_maximum_fusion.refs_0_
  79.4 4.7 collective-permute-done.11
  90.4 11.2 %project.1 = (bf16[1472,768]{1,0:T(8,128)(2,1)}, bf16[9,3,256,128]{3,2,1,0:T(8,128)(2,1)}, bf16[1472,1536]{1,0:T(8,128)(2,1)}) custom-call(s32[8]{0:T(128)} %copy-done.39, s32[4]{0:T(128)} %copy-done.2, bf16[3,1,1472,256]{3,2,1,0:T(8,128)(2,1)} %bitcast.212, f32[1472,4]{1,0:T(8,128)} %bitcast.234, bf16[4,4,184,384]{3,2,1,0:T(8,128)(2,1)} %pad_maximum_fusion.refs_0_, ...), custom_call_target="tpu_custom_call" | custom-call | flops 3472883712 | bytes 13613152 | tf_op jit(solution)/shard_map/project/pallas_call | solution.py:651
  109.8 2.6 collective-permute-start.17
  113.7 4.3 upright.2.in_ref
  118.0 4.3 upright.3.refs_0_
  122.3 10.0 %collective-permute-done.17 = bf16[8,256,128]{2,1,0:T(8,128)(2,1)S(1)} collective-permute-done((bf16[8,256,128]{2,1,0:T(8,128)(2,1)S(1)}, bf16[8,256,128]{2,1,0:T(8,128)(2,1)S(1)}, u32[]{:S(2)}, u32[]{:S(2)}) %collective-permute-start.17) | collective-permute-done | bytes 524320 | tf_op jit(solution)/shard_map/ppermute | solution.py:55
  132.4 22.5 %collective-permute-done.18 = bf16[8,256,128]{2,1,0:T(8,128)(2,1)S(1)} collective-permute-done((bf16[8,256,128]{2,1,0:T(8,128)(2,1)S(1)}, bf16[8,256,128]{2,1,0:T(8,128)(2,1)S(1)}, u32[]{:S(2)}, u32[]{:S(2)}) %collective-permute-start.18) | collective-permute-done | bytes 524320 | tf_op jit(solution)/shard_map/ppermute | solution.py:55
  160.1 3.0 collective-permute-start.20
  163.1 18.7 %attention_forward.1 = (bf16[9,256,128]{2,1,0:T(8,128)(2,1)}, f32[9,256,2]{2,1,0:T(8,128)}) custom-call(s32[9,10]{1,0:T(8,128)} %concatenate.137.table_ref, bf16[9,256,128]{2,1,0:T(8,128)(2,1)} %copy-done.28, bf16[3,1024,128]{2,1,0:T(8,128)(2,1)} %pad_maximum_fusion.5.key_ref, bf16[3,1024,128]{2,1,0:T(8,128)(2,1)} %pad_maximum_fusion.6.value_ref, ...), custom_call_target="tpu_custom_call" | custom-call | flops 4831838208 | bytes 18874368 | tf_op jit(solution)/shard_map/attention_forward/pallas_call | solution.py:853
  184.1 4.0 collective-permute-start.24
  192.4 5.9 collective-permute-done.25
  199.9 10.3 %out.1 = (bf16[768,1536]{1,0:T(8,128)(2,1)}, f32[768,1472]{1,0:T(8,128)}, bf16[768,1472]{1,0:T(8,128)(2,1)}, bf16[1472,768]{1,0:T(8,128)(2,1)}) custom-call(s32[9]{0:T(128)} %compare_select_fusion.11.table_ref, bf16[1472,1536]{1,0:T(8,128)(2,1)} %get-tuple-element.163.weight_ref, bf16[768,1472]{1,0:T(8,128)(2,1)} %upright.2.in_ref, ...), custom_call_target="tpu_custom_call" | custom-call | flops 3472883712 | bytes 17152000 | tf_op jit(solution)/shard_map/out/pallas_call | solution.py:651
  210.2 32.9 %ffn_forward.2 = (f32[768,3584]{1,0:T(8,128)}, f32[768,3584]{1,0:T(8,128)}, bf16[768,3584]{1,0:T(8,128)(2,1)}, f32[768,1472]{1,0:T(8,128)}) custom-call(bf16[768,1472]{1,0:T(8,128)(2,1)} %get-tuple-element.195.mid_ref, f32[768,1472]{1,0:T(8,128)} %get-tuple-element.222.in_ref.hidden_ref, bf16[1472,2688]{1,0:T(8,128)(2,1)} %all-gather.4.cloned.1.call-done.refs_0_.refs_3_, ...), custom_call_target="tpu_custom_call" | custom-call | flops 17364418560 | bytes 53575680 | tf_op jit(solution)/shard_map/ffn_forward/pallas_call | solution.py:364
  243.2 22.5 %ffn_forward.3 = (f32[768,3584]{1,0:T(8,128)}, f32[768,3584]{1,0:T(8,128)}, bf16[768,3584]{1,0:T(8,128)(2,1)}, bf16[768,1472]{1,0:T(8,128)(2,1)}, f32[768,1]{1,0...) custom-call(bf16[768,1472]{1,0:T(8,128)(2,1)} %get-tuple-element.195, ...), custom_call_target="tpu_custom_call", output_to_operand_aliasing={{0}: (8, {}), {1}: (9, {}), {2}: (10, {})} | custom-call | flops 6945767424 | bytes 28213248 | tf_op jit(solution)/shard_map/ffn_forward/pallas_call | solution.py:364
  265.7 14.5 %weight_grad.4 = bf16[1472,3584]{1,0:T(8,128)(2,1)} custom-call(s32[1]{0:T(128)} %constant.216.clone.1.index_ref, bf16[1472,768]{1,0:T(8,128)(2,1)} %get-tuple-element.210.refs_0_, bf16[768,3584]{1,0:T(8,128)(2,1)} %get-tuple-element.211.refs_1_), custom_call_target="tpu_custom_call" | custom-call | flops 8103395328 | bytes 28868608 | tf_op jit(solution)/shard_map/weight_grad/pallas_call | solution.py:443
  280.5 42.8 %ffn_backward.1 = (bf16[768,3584]{1,0:T(8,128)(2,1)}, bf16[768,3584]{1,0:T(8,128)(2,1)}, f32[768,1472]{1,0:T(8,128)}) custom-call(bf16[768,1472]{1,0:T(8,128)(2,1)} %get-tuple-element.212.grad_ref, f32[768,3584]{1,0:T(8,128)} %get-tuple-element.213.to_gate_ref, f32[768,3584]{1,0:T(8,128)} %get-tuple-element.214.to_up_ref, ...), custom_call_target="tpu_custom_call" | custom-call | flops 24310185984 | bytes 70483968 | tf_op jit(solution)/shard_map/ffn_backward/pallas_call | solution.py:364
  323.3 14.5 %weight_grad.5.refs_2_ = bf16[1472,7168]{1,0:T(8,128)(2,1)} custom-call(s32[1]{0:T(128)} %constant.216.clone.1.index_ref, bf16[1472,768]{1,0:T(8,128)(2,1)} %get-tuple-element.218.refs_0_, bf16[768,3584]{1,0:T(8,128)(2,1)} %get-tuple-element.220.refs_1_), custom_call_target="tpu_custom_call" | custom-call | flops 8103395328 | bytes 28868608 | tf_op jit(solution)/shard_map/weight_grad/pallas_call | solution.py:443
  337.8 14.6 %weight_grad.6 = bf16[1472,7168]{1,0:T(8,128)(2,1)} custom-call(s32[1]{0:T(128)} %constant.216.clone.1.index_ref, bf16[1472,768]{1,0:T(8,128)(2,1)} %get-tuple-element.218.refs_0_, bf16[768,3584]{1,0:T(8,128)(2,1)} %get-tuple-element.219.refs_1_, bf16[1472,7168]{1,0:T(8,128)(2,1)} %weight_grad.5.refs_2_), custom_call_target="tpu_custom_call", output_to_operand_aliasing={{}: (3, {})} | custom-call | flops 8103395328 | bytes 28868608 | tf_op jit(solution)/shard_map/weight_grad/pallas_call | solution.py:443
  352.4 13.3 %mid.1 = (f32[768,1472]{1,0:T(8,128)}, bf16[1472,768]{1,0:T(8,128)(2,1)}, bf16[9,256,128]{2,1,0:T(8,128)(2,1)}, f32[1,1472]{1,0:T(1,128)}) custom-call(bf16[1472,1536]{1,0:T(8,128)(2,1)} %get-tuple-element.163.weight_ref, f32[768,1472]{1,0:T(8,128)} %get-tuple-element.221.grad_mid_ref, f32[768,1472]{1,0:T(8,128)} %get-tuple-element.222.in_ref.hidden_ref, ...), custom_call_target="tpu_custom_call" | custom-call | flops 3472883712 | bytes 36222976 | tf_op jit(solution)/shard_map/mid/pallas_call | solution.py:651
  367.0 3.8 collective-permute-start.27
  370.8 4.4 collective-permute-done.26
  375.2 5.0 collective-permute-done.28
  385.0 31.1 %attention_backward.1 = (bf16[9,256,128]{2,1,0:T(8,128)(2,1)}, bf16[3,2,1024,128]{3,2,1,0:T(8,128)(2,1)}, f32[6,5,256,256]{3,2,1,0:T(8,128)}) custom-call(s32[9,10]{1,0:T(8,128)} %concatenate.137.table_ref, bf16[9,256,128]{2,1,0:T(8,128)(2,1)} %copy-done.28, bf16[9,256,128]{2,1,0:T(8,128)(2,1)} %copy-done.29, f32[9,256,2]{2,1,0:T(8,128)} %get-tuple-element.234.log_ref, ...), custom_call_target="tpu_custom_call" | custom-call | flops 12079595520 | bytes 18874368 | tf_op jit(solution)/shard_map/attention_backward/pallas_call | solution.py:853
  422.3 3.7 collective-permute-start.32
  428.7 7.1 %diagonals.1 = f32[6,5,512]{2,1,0:T(8,128)} custom-call(f32[6,5,256,256]{3,2,1,0:T(8,128)} %get-tuple-element.246.scores_ref), custom_call_target="tpu_custom_call" | custom-call | tf_op jit(solution)/shard_map/diagonals/pallas_call | solution.py:709
  435.8 3.5 collective-permute-done.32
  439.3 10.7 %collective-permute-done.33 = bf16[8,256,128]{2,1,0:T(8,128)(2,1)S(1)} collective-permute-done((bf16[8,256,128]{2,1,0:T(8,128)(2,1)}, bf16[8,256,128]{2,1,0:T(8,128)(2,1)S(1)}, u32[]{:S(2)}, u32[]{:S(2)}) %collective-permute-start.33) | collective-permute-done | bytes 524320 | tf_op jit(solution)/shard_map/ppermute | solution.py:55
  450.1 20.8 %collective-permute-done.34 = bf16[8,256,128]{2,1,0:T(8,128)(2,1)S(1)} collective-permute-done((bf16[8,256,128]{2,1,0:T(8,128)(2,1)}, bf16[8,256,128]{2,1,0:T(8,128)(2,1)S(1)}, u32[]{:S(2)}, u32[]{:S(2)}) %collective-permute-start.34) | collective-permute-done | bytes 524320 | tf_op jit(solution)/shard_map/ppermute | solution.py:55
  473.4 5.0 spread.1.refs_2_.spread_ref
  478.4 12.9 %weight_grad.7 = bf16[1472,1536]{1,0:T(8,128)(2,1)} custom-call(s32[1]{0:T(128)} %constant.216.clone.1.index_ref, bf16[1472,768]{1,0:T(8,128)(2,1)} %get-tuple-element.165.refs_0_, bf16[1472,768]{1,0:T(8,128)(2,1)} %get-tuple-element.224.refs_1_, bf16[768,1536]{1,0:T(8,128)(2,1)} %spread.1.refs_2_.spread_ref, bf16[768,1536]{1,0:T(8,128)(2,1)} %get-tuple-element.186.refs_3_), custom_call_target="tpu_custom_call" | custom-call | flops 6945767424 | bytes 18284544 | tf_op jit(solution)/shard_map/weight_grad/pallas_call | solution.py:443
  492.6 10.3 %in.1 = (bf16[768,1472]{1,0:T(8,128)(2,1)}, f32[1,1472]{1,0:T(1,128)}) custom-call(bf16[1472,1536]{1,0:T(8,128)(2,1)} %get-tuple-element.163.weight_ref, bf16[768,1536]{1,0:T(8,128)(2,1)} %spread.1.refs_2_.spread_ref, bf16[768,1472]{1,0:T(8,128)(2,1)} %upright.2.in_ref, f32[768,1472]{1,0:T(8,128)} %get-tuple-element.249.grad_hidden_ref, ...), custom_call_target="tpu_custom_call" | custom-call | flops 3472883712 | bytes 27375616 | tf_op jit(solution)/shard_map/in/pallas_call | solution.py:651
  505.5 3.8 collective-permute-start.37
  510.5 7.4 %collective-permute-done.36 = bf16[184,896]{1,0:T(8,128)(2,1)S(1)} collective-permute-done((bf16[184,896]{1,0:T(8,128)(2,1)S(1)}, bf16[184,896]{1,0:T(8,128)(2,1)S(1)}, u32[]{:S(2)}, u32[]{:S(2)}) %collective-permute-start.36) | collective-permute-done | bytes 329760 | tf_op jit(solution)/shard_map/ppermute | solution.py:45
  517.9 4.3 collective-permute-done.37
  526.9 2.6 collective-permute-start.43
  539.6 4.2 copy.83
  543.9 14.2 %reduce-scatter.8.cloned.1.call-done = bf16[184,1536]{1,0:T(8,128)(2,1)} async-done(((bf16[1472,1536]{1,0:T(8,128)(2,1)}), bf16[184,1536]{1,0:T(8,128)(2,1)}) %reduce-scatter.8.cloned.1.call-update) | async-done | bytes 565264 | tf_op jit(solution)/shard_map/reduce_scatter | solution.py:1181
  564.5 3.6 collective-permute-start.44
  572.3 3.7 collective-permute-done.45
  576.0 3.6 collective-permute-done.46
  (344 shorter events, 102.9 us)
Async XLA Ops:
  7.2 203.0 %all-gather.4.cloned.1.call-start = ((), (), s32[]{:S(2)}) async-start(), calls=%async_computation.3 | async-start | bytes 8902656 | tf_op jit(solution)/shard_map/all_gather | solution.py:975
  10.8 199.4 %all-gather.6.cloned.1.call-start = ((), (), s32[]{:S(2)}) async-start(), calls=%async_computation.4 | async-start | bytes 17805312 | tf_op jit(solution)/shard_map/all_gather | solution.py:975
  12.8 17.8 %collective-permute-start = (bf16[192,384]{1,0:T(8,128)(2,1)S(1)}, bf16[192,384]{1,0:T(8,128)(2,1)S(1)}, u32[]{:S(2)}, u32[]{:S(2)}) collective-permute-start(bf16[192,384]{1,0:T(8,128)(2,1)S(1)} %pad_maximum_fusion.20), channel_id=1, source_target_pairs={{3,0},{0,1},{1,2},{2,3},{7,4},{4,5},{5,6},{6,7},{11,8},{8,9},{9,10... | collective-permute-start | bytes 442376 | tf_op jit(solution)/shard_map/ppermute | solution.py:55
  15.9 14.7 %collective-permute-start.1 = (bf16[192,384]{1,0:T(8,128)(2,1)S(1)}, bf16[192,384]{1,0:T(8,128)(2,1)S(1)}, u32[]{:S(2)}, u32[]{:S(2)}) collective-permute-start(bf16[192,384]{1,0:T(8,128)(2,1)S(1)} %pad_maximum_fusion.20), channel_id=1, source_target_pairs={{1,0},{2,1},{3,2},{0,3},{5,4},{6,5},{7,6},{4,7},{9,8},{10,9},{11,1... | collective-permute-start | bytes 442376 | tf_op jit(solution)/shard_map/ppermute | solution.py:55
  18.0 13.3 %collective-permute-start.2 = (bf16[192,384]{1,0:T(8,128)(2,1)S(1)}, bf16[192,384]{1,0:T(8,128)(2,1)S(1)}, u32[]{:S(2)}, u32[]{:S(2)}) collective-permute-start(bf16[192,384]{1,0:T(8,128)(2,1)S(1)} %pad_maximum_fusion.20), channel_id=1, source_target_pairs={{2,0},{3,1},{0,2},{1,3},{6,4},{7,5},{4,6},{5,7},{10,8},{11,9},{8,1... | collective-permute-start | bytes 442376 | tf_op jit(solution)/shard_map/ppermute | solution.py:55
  32.4 8.2 %collective-permute-start.7 = (bf16[4,184]{1,0:T(4,128)(2,1)S(1)}, bf16[4,184]{1,0:T(4,128)(2,1)S(1)}, u32[]{:S(2)}, u32[]{:S(2)}) collective-permute-start(bf16[4,184]{1,0:T(4,128)(2,1)S(1)} %pad_maximum_fusion.22), channel_id=1, source_target_pairs={{8,0},{0,16},{16,24},{24,8},{12,4},{4,20},{20,28},{28,12},{9,1},{1... | collective-permute-start | bytes 4424 | tf_op jit(solution)/shard_map/ppermute | solution.py:55
  34.0 27.1 %collective-permute-start.5 = (bf16[4,184,384]{2,1,0:T(8,128)(2,1)}, bf16[4,184,384]{2,1,0:T(8,128)(2,1)S(1)}, u32[]{:S(2)}, u32[]{:S(2)}) collective-permute-start(bf16[4,184,384]{2,1,0:T(8,128)(2,1)} %get-tuple-element.148), channel_id=1, source_target_pairs={{0,16},{16,24},{24,8},{8,0},{4,20},{20,28},{28,12},{12,4},{1,17},{... | collective-permute-start | bytes 1695752 | tf_op jit(solution)/shard_map/ppermute | solution.py:45
  35.5 25.7 %collective-permute-start.6 = (bf16[4,184,384]{2,1,0:T(8,128)(2,1)}, bf16[4,184,384]{2,1,0:T(8,128)(2,1)S(1)}, u32[]{:S(2)}, u32[]{:S(2)}) collective-permute-start(bf16[4,184,384]{2,1,0:T(8,128)(2,1)} %get-tuple-element.148), channel_id=1, source_target_pairs={{16,0},{24,16},{8,24},{0,8},{20,4},{28,20},{12,28},{4,12},{17,1},{... | collective-permute-start | bytes 1695752 | tf_op jit(solution)/shard_map/ppermute | solution.py:48
  36.0 25.2 %collective-permute-start.3 = (bf16[184,1280]{1,0:T(8,128)(2,1)}, bf16[184,1280]{1,0:T(8,128)(2,1)S(1)}, u32[]{:S(2)}, u32[]{:S(2)}) collective-permute-start(bf16[184,1280]{1,0:T(8,128)(2,1)} %pad_maximum_fusion.14), channel_id=1, source_target_pairs={{0,1},{1,2},{2,3},{3,0},{4,5},{5,6},{6,7},{7,4},{8,9},{9,10},{10,1... | collective-permute-start | bytes 1413128 | tf_op jit(solution)/shard_map/ppermute | solution.py:45
  36.9 24.3 %collective-permute-start.4 = (bf16[184,1280]{1,0:T(8,128)(2,1)}, bf16[184,1280]{1,0:T(8,128)(2,1)S(1)}, u32[]{:S(2)}, u32[]{:S(2)}) collective-permute-start(bf16[184,1280]{1,0:T(8,128)(2,1)} %pad_maximum_fusion.14), channel_id=1, source_target_pairs={{1,0},{2,1},{3,2},{0,3},{5,4},{6,5},{7,6},{4,7},{9,8},{10,9},{11,1... | collective-permute-start | bytes 1413128 | tf_op jit(solution)/shard_map/ppermute | solution.py:48
  40.7 15.8 %collective-permute-start.8 = (bf16[4,184]{1,0:T(4,128)(2,1)S(1)}, bf16[4,184]{1,0:T(4,128)(2,1)S(1)}, u32[]{:S(2)}, u32[]{:S(2)}) collective-permute-start(bf16[4,184]{1,0:T(4,128)(2,1)S(1)} %pad_maximum_fusion.22), channel_id=1, source_target_pairs={{16,0},{24,16},{8,24},{0,8},{20,4},{28,20},{12,28},{4,12},{17,1},{... | collective-permute-start | bytes 4424 | tf_op jit(solution)/shard_map/ppermute | solution.py:55
  61.2 13.7 %collective-permute-start.12 = (bf16[2,184,384]{2,1,0:T(8,128)(2,1)S(1)}, bf16[2,184,384]{2,1,0:T(8,128)(2,1)S(1)}, u32[]{:S(2)}, u32[]{:S(2)}) collective-permute-start(bf16[2,184,384]{2,1,0:T(8,128)(2,1)S(1)} %slice.539), channel_id=1, source_target_pairs={{0,16},{16,24},{24,8},{8,0},{4,20},{20,28},{28,12},{12,4},{1,17},{... | collective-permute-start | bytes 847880 | tf_op jit(solution)/shard_map/ppermute | solution.py:45
  62.1 13.8 %collective-permute-start.13 = (bf16[2,184,384]{2,1,0:T(8,128)(2,1)S(1)}, bf16[2,184,384]{2,1,0:T(8,128)(2,1)S(1)}, u32[]{:S(2)}, u32[]{:S(2)}) collective-permute-start(bf16[2,184,384]{2,1,0:T(8,128)(2,1)S(1)} %slice.540), channel_id=1, source_target_pairs={{16,0},{24,16},{8,24},{0,8},{20,4},{28,20},{12,28},{4,12},{17,1},{... | collective-permute-start | bytes 847880 | tf_op jit(solution)/shard_map/ppermute | solution.py:48
  63.3 16.1 %collective-permute-start.10 = (bf16[184,1408]{1,0:T(8,128)(2,1)}, bf16[184,1408]{1,0:T(8,128)(2,1)S(1)}, u32[]{:S(2)}, u32[]{:S(2)}) collective-permute-start(bf16[184,1408]{1,0:T(8,128)(2,1)} %pad_maximum_fusion.13), channel_id=1, source_target_pairs={{0,1},{1,2},{2,3},{3,0},{4,5},{5,6},{6,7},{7,4},{8,9},{9,10},{10,1... | collective-permute-start | bytes 1554440 | tf_op jit(solution)/shard_map/ppermute | solution.py:45
  63.4 20.7 %collective-permute-start.11 = (bf16[184,1408]{1,0:T(8,128)(2,1)}, bf16[184,1408]{1,0:T(8,128)(2,1)S(1)}, u32[]{:S(2)}, u32[]{:S(2)}) collective-permute-start(bf16[184,1408]{1,0:T(8,128)(2,1)} %pad_maximum_fusion.13), channel_id=1, source_target_pairs={{1,0},{2,1},{3,2},{0,3},{5,4},{6,5},{7,6},{4,7},{9,8},{10,9},{11,1... | collective-permute-start | bytes 1554440 | tf_op jit(solution)/shard_map/ppermute | solution.py:48
  67.2 17.0 %collective-permute-start.14 = (bf16[4,4,184]{2,1,0:T(4,128)(2,1)S(1)}, bf16[4,4,184]{2,1,0:T(4,128)(2,1)S(1)}, u32[]{:S(2)}, u32[]{:S(2)}) collective-permute-start(bf16[4,4,184]{2,1,0:T(4,128)(2,1)S(1)} %pad_maximum_fusion.21), channel_id=1, source_target_pairs={{0,4},{4,0},{8,12},{12,8},{16,20},{20,16},{24,28},{28,24},{1,5},{5... | collective-permute-start | bytes 17672 | tf_op jit(solution)/shard_map/ppermute | solution.py:905
  85.6 157.6 %all-gather.8.cloned.1.call-start = ((), (), s32[]{:S(2)}) async-start(), calls=%async_computation.5 | async-start | bytes 8902656 | tf_op jit(solution)/shard_map/all_gather | solution.py:975
  105.1 17.2 %collective-permute-start.16 = (bf16[8,256,128]{2,1,0:T(8,128)(2,1)}, bf16[8,256,128]{2,1,0:T(8,128)(2,1)S(1)}, u32[]{:S(2)}, u32[]{:S(2)}) collective-permute-start(bf16[8,256,128]{2,1,0:T(8,128)(2,1)} %get-tuple-element.167), channel_id=1, source_target_pairs={{3,0},{0,1},{1,2},{2,3},{7,4},{4,5},{5,6},{6,7},{11,8},{8,9},{9,10... | collective-permute-start | bytes 1572872 | tf_op jit(solution)/shard_map/ppermute | solution.py:55
  109.8 22.6 %collective-permute-start.17 = (bf16[8,256,128]{2,1,0:T(8,128)(2,1)S(1)}, bf16[8,256,128]{2,1,0:T(8,128)(2,1)S(1)}, u32[]{:S(2)}, u32[]{:S(2)}) collective-permute-start(bf16[8,256,128]{2,1,0:T(8,128)(2,1)S(1)} %get-tuple-element.168), channel_id=1, source_target_pairs={{1,0},{2,1},{3,2},{0,3},{5,4},{6,5},{7,6},{4,7},{9,8},{10,9},{11,1... | collective-permute-start | bytes 1572872 | tf_op jit(solution)/shard_map/ppermute | solution.py:55
  113.3 41.6 %collective-permute-start.18 = (bf16[8,256,128]{2,1,0:T(8,128)(2,1)S(1)}, bf16[8,256,128]{2,1,0:T(8,128)(2,1)S(1)}, u32[]{:S(2)}, u32[]{:S(2)}) collective-permute-start(bf16[8,256,128]{2,1,0:T(8,128)(2,1)S(1)} %get-tuple-element.169), channel_id=1, source_target_pairs={{2,0},{3,1},{0,2},{1,3},{6,4},{7,5},{4,6},{5,7},{10,8},{11,9},{8,1... | collective-permute-start | bytes 1572872 | tf_op jit(solution)/shard_map/ppermute | solution.py:55
  158.0 24.9 %collective-permute-start.22 = (bf16[184,768]{1,0:T(8,128)(2,1)S(1)}, bf16[184,768]{1,0:T(8,128)(2,1)S(1)}, u32[]{:S(2)}, u32[]{:S(2)}) collective-permute-start(bf16[184,768]{1,0:T(8,128)(2,1)S(1)} %slice.576), channel_id=1, source_target_pairs={{1,0},{2,1},{3,2},{0,3},{5,4},{6,5},{7,6},{4,7},{9,8},{10,9},{11,1... | collective-permute-start | bytes 847880 | tf_op jit(solution)/shard_map/ppermute | solution.py:48
  159.2 23.7 %collective-permute-start.19 = (bf16[184,640]{1,0:T(8,128)(2,1)S(1)}, bf16[184,640]{1,0:T(8,128)(2,1)S(1)}, u32[]{:S(2)}, u32[]{:S(2)}) collective-permute-start(bf16[184,640]{1,0:T(8,128)(2,1)S(1)} %copy-done.19), channel_id=1, source_target_pairs={{0,1},{1,2},{2,3},{3,0},{4,5},{5,6},{6,7},{7,4},{8,9},{9,10},{10,1... | collective-permute-start | bytes 706568 | tf_op jit(solution)/shard_map/ppermute | solution.py:45
  160.1 22.8 %collective-permute-start.20 = (bf16[184,640]{1,0:T(8,128)(2,1)S(1)}, bf16[184,640]{1,0:T(8,128)(2,1)S(1)}, u32[]{:S(2)}, u32[]{:S(2)}) collective-permute-start(bf16[184,640]{1,0:T(8,128)(2,1)S(1)} %slice.574), channel_id=1, source_target_pairs={{1,0},{2,1},{3,2},{0,3},{5,4},{6,5},{7,6},{4,7},{9,8},{10,9},{11,1... | collective-permute-start | bytes 706568 | tf_op jit(solution)/shard_map/ppermute | solution.py:48
  163.1 19.9 %collective-permute-start.21 = (bf16[184,640]{1,0:T(8,128)(2,1)S(1)}, bf16[184,640]{1,0:T(8,128)(2,1)S(1)}, u32[]{:S(2)}, u32[]{:S(2)}) collective-permute-start(bf16[184,640]{1,0:T(8,128)(2,1)S(1)} %slice.575), channel_id=1, source_target_pairs={{0,1},{1,2},{2,3},{3,0},{4,5},{5,6},{6,7},{7,4},{8,9},{9,10},{10,1... | collective-permute-start | bytes 706568 | tf_op jit(solution)/shard_map/ppermute | solution.py:45
  184.0 197.3 %reduce-scatter.6.cloned.1.call-start = ((), (), s32[]{:S(2)}) async-start(), calls=%async_computation.6 | async-start | bytes 11870208 | tf_op jit(solution)/shard_map/reduce_scatter | solution.py:1181
  184.0 8.3 %collective-permute-start.23 = (bf16[2,256,128]{2,1,0:T(8,128)(2,1)S(1)}, bf16[2,256,128]{2,1,0:T(8,128)(2,1)S(1)}, u32[]{:S(2)}, u32[]{:S(2)}) collective-permute-start(bf16[2,256,128]{2,1,0:T(8,128)(2,1)S(1)} %get-tuple-element.180), channel_id=1, source_target_pairs={{3,0},{0,1},{1,2},{2,3},{7,4},{4,5},{5,6},{6,7},{11,8},{8,9},{9,10... | collective-permute-start | bytes 393224 | tf_op jit(solution)/shard_map/ppermute | solution.py:55
  184.1 8.2 %collective-permute-start.24 = (bf16[2,256,128]{2,1,0:T(8,128)(2,1)S(1)}, bf16[2,256,128]{2,1,0:T(8,128)(2,1)S(1)}, u32[]{:S(2)}, u32[]{:S(2)}) collective-permute-start(bf16[2,256,128]{2,1,0:T(8,128)(2,1)S(1)} %get-tuple-element.181), channel_id=1, source_target_pairs={{1,0},{2,1},{3,2},{0,3},{5,4},{6,5},{7,6},{4,7},{9,8},{10,9},{11,1... | collective-permute-start | bytes 393224 | tf_op jit(solution)/shard_map/ppermute | solution.py:55
  189.8 8.4 %collective-permute-start.25 = (bf16[2,256,128]{2,1,0:T(8,128)(2,1)S(1)}, bf16[2,256,128]{2,1,0:T(8,128)(2,1)S(1)}, u32[]{:S(2)}, u32[]{:S(2)}) collective-permute-start(bf16[2,256,128]{2,1,0:T(8,128)(2,1)S(1)} %get-tuple-element.182), channel_id=1, source_target_pairs={{2,0},{3,1},{0,2},{1,3},{6,4},{7,5},{4,6},{5,7},{10,8},{11,9},{8,1... | collective-permute-start | bytes 393224 | tf_op jit(solution)/shard_map/ppermute | solution.py:55
  280.3 223.5 %reduce-scatter.10.cloned.1.call-start = ((), (), s32[]{:S(2)}) async-start(), calls=%async_computation.8 | async-start | bytes 23740416
  366.9 191.2 %reduce-scatter.8.cloned.1.call-start = ((), (), s32[]{:S(2)}) async-start(), calls=%async_computation.7 | async-start | bytes 5087232 | tf_op jit(solution)/shard_map/reduce_scatter | solution.py:1181
  366.9 8.3 %collective-permute-start.26 = (bf16[2,256,128]{2,1,0:T(8,128)(2,1)S(1)}, bf16[2,256,128]{2,1,0:T(8,128)(2,1)S(1)}, u32[]{:S(2)}, u32[]{:S(2)}) collective-permute-start(bf16[2,256,128]{2,1,0:T(8,128)(2,1)S(1)} %get-tuple-element.229), channel_id=1, source_target_pairs={{3,0},{0,1},{1,2},{2,3},{7,4},{4,5},{5,6},{6,7},{11,8},{8,9},{9,10... | collective-permute-start | bytes 393224 | tf_op jit(solution)/shard_map/ppermute | solution.py:55
  367.0 8.2 %collective-permute-start.27 = (bf16[2,256,128]{2,1,0:T(8,128)(2,1)S(1)}, bf16[2,256,128]{2,1,0:T(8,128)(2,1)S(1)}, u32[]{:S(2)}, u32[]{:S(2)}) collective-permute-start(bf16[2,256,128]{2,1,0:T(8,128)(2,1)S(1)} %get-tuple-element.230), channel_id=1, source_target_pairs={{1,0},{2,1},{3,2},{0,3},{5,4},{6,5},{7,6},{4,7},{9,8},{10,9},{11,1... | collective-permute-start | bytes 393224 | tf_op jit(solution)/shard_map/ppermute | solution.py:55
  370.8 9.5 %collective-permute-start.28 = (bf16[2,256,128]{2,1,0:T(8,128)(2,1)S(1)}, bf16[2,256,128]{2,1,0:T(8,128)(2,1)S(1)}, u32[]{:S(2)}, u32[]{:S(2)}) collective-permute-start(bf16[2,256,128]{2,1,0:T(8,128)(2,1)S(1)} %get-tuple-element.231), channel_id=1, source_target_pairs={{2,0},{3,1},{0,2},{1,3},{6,4},{7,5},{4,6},{5,7},{10,8},{11,9},{8,1... | collective-permute-start | bytes 393224 | tf_op jit(solution)/shard_map/ppermute | solution.py:55
  382.9 39.4 %collective-permute-start.29 = (bf16[184,896]{1,0:T(8,128)(2,1)S(1)}, bf16[184,896]{1,0:T(8,128)(2,1)S(1)}, u32[]{:S(2)}, u32[]{:S(2)}) collective-permute-start(bf16[184,896]{1,0:T(8,128)(2,1)S(1)} %get-tuple-element.240), channel_id=1, source_target_pairs={{1,0},{2,1},{3,2},{0,3},{5,4},{6,5},{7,6},{4,7},{9,8},{10,9},{11,1... | collective-permute-start | bytes 989192 | tf_op jit(solution)/shard_map/ppermute | solution.py:55
  384.3 38.0 %collective-permute-start.30 = (bf16[184,896]{1,0:T(8,128)(2,1)S(1)}, bf16[184,896]{1,0:T(8,128)(2,1)S(1)}, u32[]{:S(2)}, u32[]{:S(2)}) collective-permute-start(bf16[184,896]{1,0:T(8,128)(2,1)S(1)} %get-tuple-element.241), channel_id=1, source_target_pairs={{3,0},{0,1},{1,2},{2,3},{7,4},{4,5},{5,6},{6,7},{11,8},{8,9},{9,10... | collective-permute-start | bytes 989192 | tf_op jit(solution)/shard_map/ppermute | solution.py:55
  385.0 37.3 %collective-permute-start.31 = (bf16[184,896]{1,0:T(8,128)(2,1)S(1)}, bf16[184,896]{1,0:T(8,128)(2,1)S(1)}, u32[]{:S(2)}, u32[]{:S(2)}) collective-permute-start(bf16[184,896]{1,0:T(8,128)(2,1)S(1)} %get-tuple-element.242), channel_id=1, source_target_pairs={{2,0},{3,1},{0,2},{1,3},{6,4},{7,5},{4,6},{5,7},{10,8},{11,9},{8,1... | collective-permute-start | bytes 989192 | tf_op jit(solution)/shard_map/ppermute | solution.py:55
  422.3 17.0 %collective-permute-start.32 = (bf16[8,256,128]{2,1,0:T(8,128)(2,1)}, bf16[8,256,128]{2,1,0:T(8,128)(2,1)S(1)}, u32[]{:S(2)}, u32[]{:S(2)}) collective-permute-start(bf16[8,256,128]{2,1,0:T(8,128)(2,1)} %pad_maximum_fusion.11), channel_id=1, source_target_pairs={{3,0},{0,1},{1,2},{2,3},{7,4},{4,5},{5,6},{6,7},{11,8},{8,9},{9,10... | collective-permute-start | bytes 1572872 | tf_op jit(solution)/shard_map/ppermute | solution.py:55
  426.0 24.0 %collective-permute-start.33 = (bf16[8,256,128]{2,1,0:T(8,128)(2,1)}, bf16[8,256,128]{2,1,0:T(8,128)(2,1)S(1)}, u32[]{:S(2)}, u32[]{:S(2)}) collective-permute-start(bf16[8,256,128]{2,1,0:T(8,128)(2,1)} %pad_maximum_fusion.10), channel_id=1, source_target_pairs={{1,0},{2,1},{3,2},{0,3},{5,4},{6,5},{7,6},{4,7},{9,8},{10,9},{11,1... | collective-permute-start | bytes 1572872 | tf_op jit(solution)/shard_map/ppermute | solution.py:55
  426.4 44.5 %collective-permute-start.34 = (bf16[8,256,128]{2,1,0:T(8,128)(2,1)}, bf16[8,256,128]{2,1,0:T(8,128)(2,1)S(1)}, u32[]{:S(2)}, u32[]{:S(2)}) collective-permute-start(bf16[8,256,128]{2,1,0:T(8,128)(2,1)} %pad_maximum_fusion.12), channel_id=1, source_target_pairs={{2,0},{3,1},{0,2},{1,3},{6,4},{7,5},{4,6},{5,7},{10,8},{11,9},{8,1... | collective-permute-start | bytes 1572872 | tf_op jit(solution)/shard_map/ppermute | solution.py:55
  505.4 12.5 %collective-permute-start.36 = (bf16[184,896]{1,0:T(8,128)(2,1)S(1)}, bf16[184,896]{1,0:T(8,128)(2,1)S(1)}, u32[]{:S(2)}, u32[]{:S(2)}) collective-permute-start(bf16[184,896]{1,0:T(8,128)(2,1)S(1)} %get-tuple-element.254), channel_id=1, source_target_pairs={{0,1},{1,2},{2,3},{3,0},{4,5},{5,6},{6,7},{7,4},{8,9},{9,10},{10,1... | collective-permute-start | bytes 989192 | tf_op jit(solution)/shard_map/ppermute | solution.py:45
  505.5 16.7 %collective-permute-start.37 = (bf16[184,896]{1,0:T(8,128)(2,1)S(1)}, bf16[184,896]{1,0:T(8,128)(2,1)S(1)}, u32[]{:S(2)}, u32[]{:S(2)}) collective-permute-start(bf16[184,896]{1,0:T(8,128)(2,1)S(1)} %get-tuple-element.255), channel_id=1, source_target_pairs={{1,0},{2,1},{3,2},{0,3},{5,4},{6,5},{7,6},{4,7},{9,8},{10,9},{11,1... | collective-permute-start | bytes 989192 | tf_op jit(solution)/shard_map/ppermute | solution.py:48
  525.7 38.8 %collective-permute-start.42 = (bf16[184,1792]{1,0:T(8,128)(2,1)}, bf16[184,1792]{1,0:T(8,128)(2,1)}, u32[]{:S(2)}, u32[]{:S(2)}) collective-permute-start(bf16[184,1792]{1,0:T(8,128)(2,1)} %pad_maximum_fusion.7), channel_id=1, source_target_pairs={{0,1},{1,2},{2,3},{3,0},{4,5},{5,6},{6,7},{7,4},{8,9},{9,10},{10,1... | collective-permute-start | bytes 1978376 | tf_op jit(solution)/shard_map/ppermute | solution.py:45
  526.9 37.6 %collective-permute-start.43 = (bf16[184,1792]{1,0:T(8,128)(2,1)}, bf16[184,1792]{1,0:T(8,128)(2,1)}, u32[]{:S(2)}, u32[]{:S(2)}) collective-permute-start(bf16[184,1792]{1,0:T(8,128)(2,1)} %pad_maximum_fusion.8), channel_id=1, source_target_pairs={{1,0},{2,1},{3,2},{0,3},{5,4},{6,5},{7,6},{4,7},{9,8},{10,9},{11,1... | collective-permute-start | bytes 1978376 | tf_op jit(solution)/shard_map/ppermute | solution.py:48
  529.5 7.9 %collective-permute-start.39 = (f32[48,128]{1,0:T(8,128)S(1)}, f32[48,128]{1,0:T(8,128)S(1)}, u32[]{:S(2)}, u32[]{:S(2)}) collective-permute-start(f32[48,128]{1,0:T(8,128)S(1)} %fusion.73), channel_id=1, source_target_pairs={{0,16},{4,20},{8,24},{12,28},{16,0},{20,4},{24,8},{28,12},{1,17},{... | collective-permute-start | bytes 73736 | tf_op jit(solution)/shard_map/ppermute | solution.py:79
  537.4 20.7 %collective-permute-start.40 = (f32[48,128]{1,0:T(8,128)S(1)}, f32[48,128]{1,0:T(8,128)S(1)}, u32[]{:S(2)}, u32[]{:S(2)}) collective-permute-start(f32[48,128]{1,0:T(8,128)S(1)} %add.532), channel_id=1, source_target_pairs={{0,1},{1,0},{2,3},{3,2},{4,5},{5,4},{6,7},{7,6},{8,9},{9,8},{10,11... | collective-permute-start | bytes 73736 | tf_op jit(solution)/shard_map/ppermute | solution.py:79
  564.5 7.8 %collective-permute-start.44 = (bf16[184,384]{1,0:T(8,128)(2,1)S(1)}, bf16[184,384]{1,0:T(8,128)(2,1)S(1)}, u32[]{:S(2)}, u32[]{:S(2)}) collective-permute-start(bf16[184,384]{1,0:T(8,128)(2,1)S(1)} %get-tuple-element.260), channel_id=1, source_target_pairs={{1,0},{2,1},{3,2},{0,3},{5,4},{6,5},{7,6},{4,7},{9,8},{10,9},{11,1... | collective-permute-start | bytes 423944 | tf_op jit(solution)/shard_map/ppermute | solution.py:55
  568.1 7.9 %collective-permute-start.45 = (bf16[184,384]{1,0:T(8,128)(2,1)S(1)}, bf16[184,384]{1,0:T(8,128)(2,1)S(1)}, u32[]{:S(2)}, u32[]{:S(2)}) collective-permute-start(bf16[184,384]{1,0:T(8,128)(2,1)S(1)} %get-tuple-element.261), channel_id=1, source_target_pairs={{3,0},{0,1},{1,2},{2,3},{7,4},{4,5},{5,6},{6,7},{11,8},{8,9},{9,10... | collective-permute-start | bytes 423944 | tf_op jit(solution)/shard_map/ppermute | solution.py:55
  568.1 11.5 %collective-permute-start.46 = (bf16[184,384]{1,0:T(8,128)(2,1)S(1)}, bf16[184,384]{1,0:T(8,128)(2,1)S(1)}, u32[]{:S(2)}, u32[]{:S(2)}) collective-permute-start(bf16[184,384]{1,0:T(8,128)(2,1)S(1)} %get-tuple-element.262), channel_id=1, source_target_pairs={{2,0},{3,1},{0,2},{1,3},{6,4},{7,5},{4,6},{5,7},{10,8},{11,9},{8,1... | collective-permute-start | bytes 423944 | tf_op jit(solution)/shard_map/ppermute | solution.py:55
  (45 other events, 262.6 us)
Sparse Core Ops, SparseCore 0:
  11.0 68.1 all-gather.3
  85.7 84.6 all-gather.5
  184.1 52.8 all-gather.7
  280.4 79.3 reduce-scatter.5
  367.0 134.5 reduce-scatter.9
  504.9 53.1 reduce-scatter.7
